TPU v7x, 32 devices: a whole 2x2x4 slice. The times are simulated.
32 devices in a mesh: gz: 4 (over y, x), gy: 8 (over z, core).
Axes of the slice: x: 2, y: 2, z: 4, core: 2. Of those that a mesh axis runs over, the one named last changes fastest.
Arguments:
- fixed: float32 [128, 512, 256], P('gz', 'gy'), may hold values from -6 to 6
- moving: float32 [128, 512, 256], P('gz', 'gy'), may hold values from -6 to 6
Outputs:
- update: float32 [3, 16, 64, 32], P(None, 'gz', 'gy')
- residual: float32 [3, 16, 64, 32], P(None, 'gz', 'gy')
All inputs are finite; a program needn't handle non-finite values.
Results may differ from a plain program's by a relative error of at most 0.0031.
Values sent between devices are 32-bit elements; how exact they have to be, the bound alone decides.
No kernel may reach another device: no remote copies, remote signals or barrier semaphores. Data moves between devices by JAX's collectives and lax.ppermute only.
A program may use at most 64 MiB of HBM per device.

v0:
```python
import jax
import jax.numpy as jnp
from jax import lax
from jax.sharding import PartitionSpec as P

SPACING = 8
ITERS = 2


damping_weight = 8.0


def from_behind(value, axis, steps):
    count = lax.axis_size(axis)
    initial, last = (max(0, -steps), min(count, count - steps))
    return lax.ppermute(value, axis, [(source, source + steps) for source in range(initial, last)])


def padded_2(cells, sides, width):
    for axis, dim in sides:
        count = lax.axis_size(axis)
        ends = count - 1
        head = lax.slice_in_dim(cells, 0, width, axis=dim)
        tail = lax.slice_in_dim(cells, cells.shape[dim] - width, cells.shape[dim], axis=dim)
        cells = jnp.concatenate(
            [
                lax.ppermute(tail, axis, [(i, (i + 1) % count) for i in range(ends)]),
                cells,
                lax.ppermute(head, axis, [((i + 1) % count, i) for i in range(ends)]),
            ],
            axis=dim,
        )
    return cells


def basis_matrix(count, columns, offset):
    voxel = jnp.arange(count, dtype=jnp.int32)
    cell = voxel // SPACING
    frac = ((voxel % SPACING).astype(jnp.float32) + 0.5) / SPACING
    other = 1.0 - frac
    weights = (
        other**3 / 6.0,
        (3.0 * frac**3 - 6.0 * frac**2 + 4.0) / 6.0,
        (-3.0 * frac**3 + 3.0 * frac**2 + 3.0 * frac + 1.0) / 6.0,
        frac**3 / 6.0,
    )
    index = jnp.arange(columns, dtype=jnp.int32)
    matrix = jnp.zeros((count, columns), jnp.float32)
    for tap in range(4):
        match = index[None, :] == (cell - 1 + tap + offset)[:, None]
        matrix = matrix + jnp.where(match, weights[tap][:, None], jnp.float32(0.0))
    return matrix


def decode(control, along_z, along_y, along_x):
    hp = lax.Precision.HIGHEST
    inner = jnp.einsum("cabe,xe->cabx", control, along_x, precision=hp)
    inner = jnp.einsum("yb,cabx->cayx", along_y, inner, precision=hp)
    return jnp.einsum("za,cayx->czyx", along_z, inner, precision=hp)


def encode(volume, along_z, along_y, along_x):
    hp = lax.Precision.HIGHEST
    inner = jnp.einsum("za,czyx->cayx", along_z, volume, precision=hp)
    inner = jnp.einsum("yb,cayx->cabx", along_y, inner, precision=hp)
    return jnp.einsum("xe,cabx->cabe", along_x, inner, precision=hp)


def derivative(padded, axis):
    length = padded.shape[axis] - 6

    def part(shift_by):
        return lax.slice_in_dim(padded, 3 + shift_by, 3 + shift_by + length, axis=axis)

    return (45.0 * (part(1) - part(-1)) - 9.0 * (part(2) - part(-2)) + (part(3) - part(-3))) / 60.0


def fold_rims(extended):
    depth = extended.shape[1] - 4
    from_above = from_behind(extended[:, 0:2], "gz", -1)
    from_below = from_behind(extended[:, depth + 2 : depth + 4], "gz", 1)
    core = extended[:, 2 : depth + 2]
    core = core.at[:, depth - 2 :].add(from_above).at[:, :2].add(from_below)
    width = core.shape[2] - 4
    from_right = from_behind(core[:, :, 0:2], "gy", -1)
    from_left = from_behind(core[:, :, width + 2 : width + 4], "gy", 1)
    inner = core[:, :, 2 : width + 2]
    return inner.at[:, :, width - 2 :].add(from_right).at[:, :, :2].add(from_left)


def two_products(residual, image):
    return lax.psum((jnp.sum(residual * residual), jnp.sum(residual * image)), ("gz", "gy"))


def shards(fixed, moving):
    slab_z, slab_y, extent = fixed.shape
    pair = jnp.stack([fixed, moving])
    framed = padded_2(pair, (("gz", 1), ("gy", 2)), 3)
    framed = 0.5 * (framed[0] + framed[1])
    framed = jnp.pad(framed, ((0, 0), (0, 0), (3, 3)))
    gradient = jnp.stack(
        [
            derivative(framed[:, 3:-3, 3:-3], 0),
            derivative(framed[3:-3, :, 3:-3], 1),
            derivative(framed[3:-3, 3:-3, :], 2),
        ]
    ).astype(jnp.bfloat16)
    mismatch = moving - fixed
    ctrl_z = slab_z // SPACING
    ctrl_y = slab_y // SPACING
    ctrl_x = extent // SPACING
    along_z = basis_matrix(slab_z, ctrl_z + 4, 2)
    along_y = basis_matrix(slab_y, ctrl_y + 4, 2)
    along_x = basis_matrix(extent, ctrl_x, 0)
    slopes = gradient.astype(jnp.float32)

    def operate(control):
        extended = padded_2(control, (("gz", 1), ("gy", 2)), 2)
        field = decode(extended, along_z, along_y, along_x)
        volume = slopes * jnp.sum(slopes * field, axis=0)[None]
        return fold_rims(encode(volume, along_z, along_y, along_x)) + damping_weight * control

    rhs = -fold_rims(encode(slopes * mismatch[None], along_z, along_y, along_x))
    update = jnp.zeros_like(rhs)
    residual = rhs
    image = operate(residual)
    norm_now, product = two_products(residual, image)
    alpha = norm_now / product
    direction, along = (residual, image)
    for step_index in range(ITERS):
        update = update + alpha * direction
        residual = residual - alpha * along
        if step_index + 1 < ITERS:
            image = operate(residual)
            norm_next, product = two_products(residual, image)
            ratio = norm_next / norm_now
            alpha = norm_next / (product - ratio * norm_next / alpha)
            direction = residual + ratio * direction
            along = image + ratio * along
            norm_now = norm_next
    return (update, residual)


def solution(mesh):
    return jax.shard_map(
        shards,
        mesh=mesh,
        in_specs=(P("gz", "gy", None), P("gz", "gy", None)),
        out_specs=(P(None, "gz", "gy", None), P(None, "gz", "gy", None)),
        check_vma=False,
    )
```

profile of v0, /device:TPU:1, one launch (start us, length us, event | category | flops | bytes accessed | tf_op | source)
XLA Modules:
  0.0 263.7 jit_solution(10514513862206553743)
XLA Ops:
  0.6 4.7 %copy_bitcast_fusion = (f32[1,32,64,256]{3,1,2,0:T(8,128)S(1)}, f32[1,32,64,256]{3,1,2,0:T(8,128)S(1)}) fusion(f32[32,64,256]{2,1,0:T(8,128)} %param.27, f32[32,64,256]{2,1,0:T(8,128)} %param.26), kind=kLoop, calls=%fused_computation.51 | loop fusion | bytes 8388608 | tf_op jit(solution)/shard_map/stack | solution.py:97
  5.5 4.0 %collective-permute-start = (f32[2,3,64,256]{3,1,2,0:T(4,128)S(1)}, f32[2,3,64,256]{3,1,2,0:T(4,128)S(1)}, u32[]{:S(2)}, u32[]{:S(2)}) collective-permute-start(f32[2,3,64,256]{3,1,2,0:T(4,128)S(1)} %get-tuple-element.156), channel_id=1, source_target_pairs={{0,8},{8,16},{16,24},{1,9},{9,17},{17,25},{2,10},{10,18},{18,26},{... | collective-permute-start | bytes 1179656 | tf_op jit(solution)/shard_map/ppermute | solution.py:27
  10.9 9.1 %collective-permute-done = f32[2,3,64,256]{3,1,2,0:T(4,128)S(1)} collective-permute-done((f32[2,3,64,256]{3,1,2,0:T(4,128)S(1)}, f32[2,3,64,256]{3,1,2,0:T(4,128)S(1)}, u32[]{:S(2)}, u32[]{:S(2)}) %collective-permute-start) | collective-permute-done | bytes 393248 | tf_op jit(solution)/shard_map/ppermute | solution.py:27
  20.0 13.2 %collective-permute-done.1 = f32[2,3,64,256]{3,1,2,0:T(4,128)S(1)} collective-permute-done((f32[2,3,64,256]{3,1,2,0:T(4,128)S(1)}, f32[2,3,64,256]{3,1,2,0:T(4,128)S(1)}, u32[]{:S(2)}, u32[]{:S(2)}) %collective-permute-start.1) | collective-permute-done | bytes 393248 | tf_op jit(solution)/shard_map/ppermute | solution.py:29
  33.3 4.6 %collective-permute-start.2 = (f32[2,38,3,256]{3,1,2,0:T(8,128)S(1)}, f32[2,38,3,256]{3,1,2,0:T(8,128)S(1)}, u32[]{:S(2)}, u32[]{:S(2)}) collective-permute-start(f32[2,38,3,256]{3,1,2,0:T(8,128)S(1)} %get-tuple-element.154), channel_id=1, source_target_pairs={{0,1},{1,2},{2,3},{3,4},{4,5},{5,6},{6,7},{8,9},{9,10},{10,11},{11... | collective-permute-start | bytes 700424 | tf_op jit(solution)/shard_map/ppermute | solution.py:27
  46.8 8.0 %fusion.51 = (bf16[1,32,64,256]{3,1,2,0:T(8,128)(2,1)}, bf16[1,32,64,256]{3,1,2,0:T(8,128)(2,1)}, bf16[1,32,64,256]{3,1,2,0:T(8,128)(2,1)}) fusion(f32[38,70,256]{2,0,1:T(8,128)S(1)} %fusion.9), kind=kLoop, calls=%fused_computation.69 | loop fusion | flops 14155776 | bytes 31178752 | tf_op jit(solution)/shard_map/stack | solution.py:101
  54.8 6.4 %fusion.41 = f32[3,8,64,256]{3,1,2,0:T(8,128)S(1)} fusion(f32[32,64,256]{2,0,1:T(8,128)} %copy.6, f32[32]{0:T(128)S(1)} %get-tuple-element.198, s32[32]{0:T(128)S(1)} %get-tuple-element.203, f32[32]{0:T(128)S(1)} %get-tuple-element.190, s32[32]{0:T(128)S(1)} %get-tuple-element.205, f32[32]{0:T(128)S(1)} %get-tuple-element.197, ...), kind=kOutput, calls=%fused_computation.63 | convolution fusion | flops 157289216 | bytes 6816768 | tf_op jit(solution)/shard_map/za,czyx->cayx/dot_general | solution.py:64
  64.5 4.0 %collective-permute-start.5 = (f32[3,2,12,32]{3,2,1,0:T(8,128)S(1)}, f32[3,2,12,32]{3,2,1,0:T(8,128)S(1)}, u32[]{:S(2)}, u32[]{:S(2)}) collective-permute-start(f32[3,2,12,32]{3,2,1,0:T(8,128)S(1)} %get-tuple-element.165), channel_id=1, source_target_pairs={{0,8},{8,16},{16,24},{1,9},{9,17},{17,25},{2,10},{10,18},{18,26},{... | collective-permute-start | bytes 27656 | tf_op jit(solution)/shard_map/ppermute | solution.py:16
  71.6 3.9 %collective-permute-start.7 = (f32[3,4,2,32]{3,2,1,0:T(2,128)S(1)}, f32[3,4,2,32]{3,2,1,0:T(2,128)S(1)}, u32[]{:S(2)}, u32[]{:S(2)}) collective-permute-start(f32[3,4,2,32]{3,2,1,0:T(2,128)S(1)} %get-tuple-element.177), channel_id=1, source_target_pairs={{0,1},{1,2},{2,3},{3,4},{4,5},{5,6},{6,7},{8,9},{9,10},{10,11},{11... | collective-permute-start | bytes 9224 | tf_op jit(solution)/shard_map/ppermute | solution.py:16
  76.1 4.0 %collective-permute-start.8 = (f32[3,2,8,32]{3,2,1,0:T(8,128)S(1)}, f32[3,2,8,32]{3,2,1,0:T(8,128)S(1)}, u32[]{:S(2)}, u32[]{:S(2)}) collective-permute-start(f32[3,2,8,32]{3,2,1,0:T(8,128)S(1)} %get-tuple-element.181), channel_id=1, source_target_pairs={{0,8},{8,16},{16,24},{1,9},{9,17},{17,25},{2,10},{10,18},{18,26},{... | collective-permute-start | bytes 18440 | tf_op jit(solution)/shard_map/ppermute | solution.py:27
  81.5 4.5 %collective-permute-done.9 = f32[3,2,8,32]{3,2,1,0:T(8,128)S(1)} collective-permute-done((f32[3,2,8,32]{3,2,1,0:T(8,128)S(1)}, f32[3,2,8,32]{3,2,1,0:T(8,128)S(1)}, u32[]{:S(2)}, u32[]{:S(2)}) %collective-permute-start.9) | collective-permute-done | bytes 6176 | tf_op jit(solution)/shard_map/ppermute | solution.py:29
  86.0 5.3 %collective-permute-start.10 = (f32[3,8,2,32]{3,2,1,0:T(2,128)S(1)}, f32[3,8,2,32]{3,2,1,0:T(2,128)S(1)}, u32[]{:S(2)}, u32[]{:S(2)}) collective-permute-start(f32[3,8,2,32]{3,2,1,0:T(2,128)S(1)} %get-tuple-element.175), channel_id=1, source_target_pairs={{0,1},{1,2},{2,3},{3,4},{4,5},{5,6},{6,7},{8,9},{9,10},{10,11},{11... | collective-permute-start | bytes 18440 | tf_op jit(solution)/shard_map/ppermute | solution.py:27
  98.4 6.1 %fusion.1 = f32[32,64,256]{2,0,1:T(8,128)S(1)} fusion(f32[3,8,64,256]{3,2,1,0:T(8,128)S(1)} %convolution_bitcast_fusion.1, f32[32]{0:T(128)S(1)} %get-tuple-element.198, s32[32]{0:T(128)S(1)} %get-tuple-element.203, f32[32]{0:T(128)S(1)} %get-tuple-element.190, s32[32]{0:T(128)S(1)} %get-tuple-element.205, f32[32]{0:T(128)S(1)} %get-tuple-element.197, ...), kind=kOutput, calls=%fused_computation.12 | convolution fusion | flops 158337792 | bytes 6816768 | tf_op jit(solution)/shard_map/za,cayx->czyx/dot_general | solution.py:59
  104.5 4.1 %fusion.40 = f32[3,8,64,256]{3,1,2,0:T(8,128)S(1)} fusion(f32[32,64,256]{2,0,1:T(8,128)S(1)} %fusion.1, f32[32]{0:T(128)S(1)} %get-tuple-element.198, s32[32]{0:T(128)S(1)} %get-tuple-element.203, f32[32]{0:T(128)S(1)} %get-tuple-element.190, s32[32]{0:T(128)S(1)} %get-tuple-element.205, f32[32]{0:T(128)S(1)} %get-tuple-element.197, ...), kind=kOutput, calls=%fused_computation.62 | convolution fusion | flops 157289216 | bytes 6816768 | tf_op jit(solution)/shard_map/za,czyx->cayx/dot_general | solution.py:64
  111.8 5.2 %collective-permute-start.13 = (f32[3,2,12,32]{3,2,1,0:T(8,128)S(1)}, f32[3,2,12,32]{3,2,1,0:T(8,128)S(1)}, u32[]{:S(2)}, u32[]{:S(2)}) collective-permute-start(f32[3,2,12,32]{3,2,1,0:T(8,128)S(1)} %get-tuple-element.163), channel_id=1, source_target_pairs={{0,8},{8,16},{16,24},{1,9},{9,17},{17,25},{2,10},{10,18},{18,26},{... | collective-permute-start | bytes 27656 | tf_op jit(solution)/shard_map/ppermute | solution.py:16
  120.1 3.6 %collective-permute-start.15 = (f32[3,4,2,32]{3,2,1,0:T(2,128)S(1)}, f32[3,4,2,32]{3,2,1,0:T(2,128)S(1)}, u32[]{:S(2)}, u32[]{:S(2)}) collective-permute-start(f32[3,4,2,32]{3,2,1,0:T(2,128)S(1)} %get-tuple-element.173), channel_id=1, source_target_pairs={{0,1},{1,2},{2,3},{3,4},{4,5},{5,6},{6,7},{8,9},{9,10},{10,11},{11... | collective-permute-start | bytes 9224 | tf_op jit(solution)/shard_map/ppermute | solution.py:16
  125.2 41.9 %all-reduce.2 = (f32[]{:T(128)}, f32[]{:T(128)}) all-reduce(f32[]{:T(128)} %get-tuple-element.149, f32[]{:T(128)} %get-tuple-element.148), channel_id=1, replica_groups=mesh['gz'=4,'gy'=8] {'gz','gy'}, use_global_device_ids=true, to_apply=%region_1.2 | all-reduce | flops 2 | bytes 16 | tf_op jit(solution)/shard_map/psum | solution.py:92
  168.4 4.3 %collective-permute-start.16 = (f32[3,2,8,32]{3,2,1,0:T(8,128)S(1)}, f32[3,2,8,32]{3,2,1,0:T(8,128)S(1)}, u32[]{:S(2)}, u32[]{:S(2)}) collective-permute-start(f32[3,2,8,32]{3,2,1,0:T(8,128)S(1)} %get-tuple-element.179), channel_id=1, source_target_pairs={{0,8},{8,16},{16,24},{1,9},{9,17},{17,25},{2,10},{10,18},{18,26},{... | collective-permute-start | bytes 18440 | tf_op jit(solution)/shard_map/ppermute | solution.py:27
  177.4 5.5 %collective-permute-start.18 = (f32[3,8,2,32]{3,2,1,0:T(2,128)S(1)}, f32[3,8,2,32]{3,2,1,0:T(2,128)S(1)}, u32[]{:S(2)}, u32[]{:S(2)}) collective-permute-start(f32[3,8,2,32]{3,2,1,0:T(2,128)S(1)} %get-tuple-element.171), channel_id=1, source_target_pairs={{0,1},{1,2},{2,3},{3,4},{4,5},{5,6},{6,7},{8,9},{9,10},{10,11},{11... | collective-permute-start | bytes 18440 | tf_op jit(solution)/shard_map/ppermute | solution.py:27
  189.9 6.1 %fusion.3 = f32[32,64,256]{2,0,1:T(8,128)S(1)} fusion(f32[3,8,64,256]{3,2,1,0:T(8,128)S(1)} %convolution_bitcast_fusion, f32[32]{0:T(128)S(1)} %get-tuple-element.198, s32[32]{0:T(128)S(1)} %get-tuple-element.203, f32[32]{0:T(128)S(1)} %get-tuple-element.190, s32[32]{0:T(128)S(1)} %get-tuple-element.205, f32[32]{0:T(128)S(1)} %get-tuple-element.197, ...), kind=kOutput, calls=%fused_computation.14 | convolution fusion | flops 158337792 | bytes 6816768 | tf_op jit(solution)/shard_map/za,cayx->czyx/dot_general | solution.py:59
  196.0 4.1 %fusion.39 = f32[3,8,64,256]{3,1,2,0:T(8,128)S(1)} fusion(f32[32,64,256]{2,0,1:T(8,128)S(1)} %fusion.3, f32[32]{0:T(128)S(1)} %get-tuple-element.198, s32[32]{0:T(128)S(1)} %get-tuple-element.203, f32[32]{0:T(128)S(1)} %get-tuple-element.190, s32[32]{0:T(128)S(1)} %get-tuple-element.205, f32[32]{0:T(128)S(1)} %get-tuple-element.197, ...), kind=kOutput, calls=%fused_computation.61 | convolution fusion | flops 157289216 | bytes 6816768 | tf_op jit(solution)/shard_map/za,czyx->cayx/dot_general | solution.py:64
  203.2 4.8 %collective-permute-start.21 = (f32[3,2,12,32]{3,2,1,0:T(8,128)S(1)}, f32[3,2,12,32]{3,2,1,0:T(8,128)S(1)}, u32[]{:S(2)}, u32[]{:S(2)}) collective-permute-start(f32[3,2,12,32]{3,2,1,0:T(8,128)S(1)} %get-tuple-element.161), channel_id=1, source_target_pairs={{0,8},{8,16},{16,24},{1,9},{9,17},{17,25},{2,10},{10,18},{18,26},{... | collective-permute-start | bytes 27656 | tf_op jit(solution)/shard_map/ppermute | solution.py:16
  211.2 3.6 %collective-permute-start.23 = (f32[3,4,2,32]{3,2,1,0:T(2,128)S(1)}, f32[3,4,2,32]{3,2,1,0:T(2,128)S(1)}, u32[]{:S(2)}, u32[]{:S(2)}) collective-permute-start(f32[3,4,2,32]{3,2,1,0:T(2,128)S(1)} %get-tuple-element.169), channel_id=1, source_target_pairs={{0,1},{1,2},{2,3},{3,4},{4,5},{5,6},{6,7},{8,9},{9,10},{10,11},{11... | collective-permute-start | bytes 9224 | tf_op jit(solution)/shard_map/ppermute | solution.py:16
  216.3 41.9 %all-reduce.1 = (f32[]{:T(128)}, f32[]{:T(128)}) all-reduce(f32[]{:T(128)} %get-tuple-element.147, f32[]{:T(128)} %get-tuple-element.146), channel_id=1, replica_groups=mesh['gz'=4,'gy'=8] {'gz','gy'}, use_global_device_ids=true, to_apply=%region_6.7 | all-reduce | flops 2 | bytes 16 | tf_op jit(solution)/shard_map/psum | solution.py:92
  (104 shorter events, 53.4 us)
Async XLA Ops:
  5.5 14.5 %collective-permute-start = (f32[2,3,64,256]{3,1,2,0:T(4,128)S(1)}, f32[2,3,64,256]{3,1,2,0:T(4,128)S(1)}, u32[]{:S(2)}, u32[]{:S(2)}) collective-permute-start(f32[2,3,64,256]{3,1,2,0:T(4,128)S(1)} %get-tuple-element.156), channel_id=1, source_target_pairs={{0,8},{8,16},{16,24},{1,9},{9,17},{17,25},{2,10},{10,18},{18,26},{... | collective-permute-start | bytes 1179656 | tf_op jit(solution)/shard_map/ppermute | solution.py:27
  9.4 23.7 %collective-permute-start.1 = (f32[2,3,64,256]{3,1,2,0:T(4,128)S(1)}, f32[2,3,64,256]{3,1,2,0:T(4,128)S(1)}, u32[]{:S(2)}, u32[]{:S(2)}) collective-permute-start(f32[2,3,64,256]{3,1,2,0:T(4,128)S(1)} %get-tuple-element.157), channel_id=1, source_target_pairs={{8,0},{16,8},{24,16},{9,1},{17,9},{25,17},{10,2},{18,10},{26,18},{... | collective-permute-start | bytes 1179656 | tf_op jit(solution)/shard_map/ppermute | solution.py:29
  33.3 9.7 %collective-permute-start.2 = (f32[2,38,3,256]{3,1,2,0:T(8,128)S(1)}, f32[2,38,3,256]{3,1,2,0:T(8,128)S(1)}, u32[]{:S(2)}, u32[]{:S(2)}) collective-permute-start(f32[2,38,3,256]{3,1,2,0:T(8,128)S(1)} %get-tuple-element.154), channel_id=1, source_target_pairs={{0,1},{1,2},{2,3},{3,4},{4,5},{5,6},{6,7},{8,9},{9,10},{10,11},{11... | collective-permute-start | bytes 700424 | tf_op jit(solution)/shard_map/ppermute | solution.py:27
  37.9 7.5 %collective-permute-start.3 = (f32[2,38,3,256]{3,1,2,0:T(8,128)S(1)}, f32[2,38,3,256]{3,1,2,0:T(8,128)S(1)}, u32[]{:S(2)}, u32[]{:S(2)}) collective-permute-start(f32[2,38,3,256]{3,1,2,0:T(8,128)S(1)} %get-tuple-element.155), channel_id=1, source_target_pairs={{1,0},{2,1},{3,2},{4,3},{5,4},{6,5},{7,6},{9,8},{10,9},{11,10},{12... | collective-permute-start | bytes 700424 | tf_op jit(solution)/shard_map/ppermute | solution.py:29
  63.1 5.4 %collective-permute-start.4 = (f32[3,2,12,32]{3,2,1,0:T(8,128)S(1)}, f32[3,2,12,32]{3,2,1,0:T(8,128)S(1)}, u32[]{:S(2)}, u32[]{:S(2)}) collective-permute-start(f32[3,2,12,32]{3,2,1,0:T(8,128)S(1)} %get-tuple-element.166), channel_id=1, source_target_pairs={{8,0},{16,8},{24,16},{9,1},{17,9},{25,17},{10,2},{18,10},{26,18},{... | collective-permute-start | bytes 27656 | tf_op jit(solution)/shard_map/ppermute | solution.py:16
  64.5 5.2 %collective-permute-start.5 = (f32[3,2,12,32]{3,2,1,0:T(8,128)S(1)}, f32[3,2,12,32]{3,2,1,0:T(8,128)S(1)}, u32[]{:S(2)}, u32[]{:S(2)}) collective-permute-start(f32[3,2,12,32]{3,2,1,0:T(8,128)S(1)} %get-tuple-element.165), channel_id=1, source_target_pairs={{0,8},{8,16},{16,24},{1,9},{9,17},{17,25},{2,10},{10,18},{18,26},{... | collective-permute-start | bytes 27656 | tf_op jit(solution)/shard_map/ppermute | solution.py:16
  69.7 5.8 %collective-permute-start.6 = (f32[3,4,2,32]{3,2,1,0:T(2,128)S(1)}, f32[3,4,2,32]{3,2,1,0:T(2,128)S(1)}, u32[]{:S(2)}, u32[]{:S(2)}) collective-permute-start(f32[3,4,2,32]{3,2,1,0:T(2,128)S(1)} %get-tuple-element.178), channel_id=1, source_target_pairs={{1,0},{2,1},{3,2},{4,3},{5,4},{6,5},{7,6},{9,8},{10,9},{11,10},{12... | collective-permute-start | bytes 9224 | tf_op jit(solution)/shard_map/ppermute | solution.py:16
  71.6 4.5 %collective-permute-start.7 = (f32[3,4,2,32]{3,2,1,0:T(2,128)S(1)}, f32[3,4,2,32]{3,2,1,0:T(2,128)S(1)}, u32[]{:S(2)}, u32[]{:S(2)}) collective-permute-start(f32[3,4,2,32]{3,2,1,0:T(2,128)S(1)} %get-tuple-element.177), channel_id=1, source_target_pairs={{0,1},{1,2},{2,3},{3,4},{4,5},{5,6},{6,7},{8,9},{9,10},{10,11},{11... | collective-permute-start | bytes 9224 | tf_op jit(solution)/shard_map/ppermute | solution.py:16
  76.1 5.3 %collective-permute-start.8 = (f32[3,2,8,32]{3,2,1,0:T(8,128)S(1)}, f32[3,2,8,32]{3,2,1,0:T(8,128)S(1)}, u32[]{:S(2)}, u32[]{:S(2)}) collective-permute-start(f32[3,2,8,32]{3,2,1,0:T(8,128)S(1)} %get-tuple-element.181), channel_id=1, source_target_pairs={{0,8},{8,16},{16,24},{1,9},{9,17},{17,25},{2,10},{10,18},{18,26},{... | collective-permute-start | bytes 18440 | tf_op jit(solution)/shard_map/ppermute | solution.py:27
  80.2 5.8 %collective-permute-start.9 = (f32[3,2,8,32]{3,2,1,0:T(8,128)S(1)}, f32[3,2,8,32]{3,2,1,0:T(8,128)S(1)}, u32[]{:S(2)}, u32[]{:S(2)}) collective-permute-start(f32[3,2,8,32]{3,2,1,0:T(8,128)S(1)} %get-tuple-element.182), channel_id=1, source_target_pairs={{8,0},{16,8},{24,16},{9,1},{17,9},{25,17},{10,2},{18,10},{26,18},{... | collective-permute-start | bytes 18440 | tf_op jit(solution)/shard_map/ppermute | solution.py:29
  86.0 7.3 %collective-permute-start.10 = (f32[3,8,2,32]{3,2,1,0:T(2,128)S(1)}, f32[3,8,2,32]{3,2,1,0:T(2,128)S(1)}, u32[]{:S(2)}, u32[]{:S(2)}) collective-permute-start(f32[3,8,2,32]{3,2,1,0:T(2,128)S(1)} %get-tuple-element.175), channel_id=1, source_target_pairs={{0,1},{1,2},{2,3},{3,4},{4,5},{5,6},{6,7},{8,9},{9,10},{10,11},{11... | collective-permute-start | bytes 18440 | tf_op jit(solution)/shard_map/ppermute | solution.py:27
  91.3 5.1 %collective-permute-start.11 = (f32[3,8,2,32]{3,2,1,0:T(2,128)S(1)}, f32[3,8,2,32]{3,2,1,0:T(2,128)S(1)}, u32[]{:S(2)}, u32[]{:S(2)}) collective-permute-start(f32[3,8,2,32]{3,2,1,0:T(2,128)S(1)} %get-tuple-element.176), channel_id=1, source_target_pairs={{1,0},{2,1},{3,2},{4,3},{5,4},{6,5},{7,6},{9,8},{10,9},{11,10},{12... | collective-permute-start | bytes 18440 | tf_op jit(solution)/shard_map/ppermute | solution.py:29
  110.4 6.5 %collective-permute-start.12 = (f32[3,2,12,32]{3,2,1,0:T(8,128)S(1)}, f32[3,2,12,32]{3,2,1,0:T(8,128)S(1)}, u32[]{:S(2)}, u32[]{:S(2)}) collective-permute-start(f32[3,2,12,32]{3,2,1,0:T(8,128)S(1)} %get-tuple-element.164), channel_id=1, source_target_pairs={{8,0},{16,8},{24,16},{9,1},{17,9},{25,17},{10,2},{18,10},{26,18},{... | collective-permute-start | bytes 27656 | tf_op jit(solution)/shard_map/ppermute | solution.py:16
  111.8 6.3 %collective-permute-start.13 = (f32[3,2,12,32]{3,2,1,0:T(8,128)S(1)}, f32[3,2,12,32]{3,2,1,0:T(8,128)S(1)}, u32[]{:S(2)}, u32[]{:S(2)}) collective-permute-start(f32[3,2,12,32]{3,2,1,0:T(8,128)S(1)} %get-tuple-element.163), channel_id=1, source_target_pairs={{0,8},{8,16},{16,24},{1,9},{9,17},{17,25},{2,10},{10,18},{18,26},{... | collective-permute-start | bytes 27656 | tf_op jit(solution)/shard_map/ppermute | solution.py:16
  118.1 5.6 %collective-permute-start.14 = (f32[3,4,2,32]{3,2,1,0:T(2,128)S(1)}, f32[3,4,2,32]{3,2,1,0:T(2,128)S(1)}, u32[]{:S(2)}, u32[]{:S(2)}) collective-permute-start(f32[3,4,2,32]{3,2,1,0:T(2,128)S(1)} %get-tuple-element.174), channel_id=1, source_target_pairs={{1,0},{2,1},{3,2},{4,3},{5,4},{6,5},{7,6},{9,8},{10,9},{11,10},{12... | collective-permute-start | bytes 9224 | tf_op jit(solution)/shard_map/ppermute | solution.py:16
  120.1 4.5 %collective-permute-start.15 = (f32[3,4,2,32]{3,2,1,0:T(2,128)S(1)}, f32[3,4,2,32]{3,2,1,0:T(2,128)S(1)}, u32[]{:S(2)}, u32[]{:S(2)}) collective-permute-start(f32[3,4,2,32]{3,2,1,0:T(2,128)S(1)} %get-tuple-element.173), channel_id=1, source_target_pairs={{0,1},{1,2},{2,3},{3,4},{4,5},{5,6},{6,7},{8,9},{9,10},{10,11},{11... | collective-permute-start | bytes 9224 | tf_op jit(solution)/shard_map/ppermute | solution.py:16
  168.4 5.7 %collective-permute-start.16 = (f32[3,2,8,32]{3,2,1,0:T(8,128)S(1)}, f32[3,2,8,32]{3,2,1,0:T(8,128)S(1)}, u32[]{:S(2)}, u32[]{:S(2)}) collective-permute-start(f32[3,2,8,32]{3,2,1,0:T(8,128)S(1)} %get-tuple-element.179), channel_id=1, source_target_pairs={{0,8},{8,16},{16,24},{1,9},{9,17},{17,25},{2,10},{10,18},{18,26},{... | collective-permute-start | bytes 18440 | tf_op jit(solution)/shard_map/ppermute | solution.py:27
  172.8 4.6 %collective-permute-start.17 = (f32[3,2,8,32]{3,2,1,0:T(8,128)S(1)}, f32[3,2,8,32]{3,2,1,0:T(8,128)S(1)}, u32[]{:S(2)}, u32[]{:S(2)}) collective-permute-start(f32[3,2,8,32]{3,2,1,0:T(8,128)S(1)} %get-tuple-element.180), channel_id=1, source_target_pairs={{8,0},{16,8},{24,16},{9,1},{17,9},{25,17},{10,2},{18,10},{26,18},{... | collective-permute-start | bytes 18440 | tf_op jit(solution)/shard_map/ppermute | solution.py:29
  177.4 7.4 %collective-permute-start.18 = (f32[3,8,2,32]{3,2,1,0:T(2,128)S(1)}, f32[3,8,2,32]{3,2,1,0:T(2,128)S(1)}, u32[]{:S(2)}, u32[]{:S(2)}) collective-permute-start(f32[3,8,2,32]{3,2,1,0:T(2,128)S(1)} %get-tuple-element.171), channel_id=1, source_target_pairs={{0,1},{1,2},{2,3},{3,4},{4,5},{5,6},{6,7},{8,9},{9,10},{10,11},{11... | collective-permute-start | bytes 18440 | tf_op jit(solution)/shard_map/ppermute | solution.py:27
  182.8 5.1 %collective-permute-start.19 = (f32[3,8,2,32]{3,2,1,0:T(2,128)S(1)}, f32[3,8,2,32]{3,2,1,0:T(2,128)S(1)}, u32[]{:S(2)}, u32[]{:S(2)}) collective-permute-start(f32[3,8,2,32]{3,2,1,0:T(2,128)S(1)} %get-tuple-element.172), channel_id=1, source_target_pairs={{1,0},{2,1},{3,2},{4,3},{5,4},{6,5},{7,6},{9,8},{10,9},{11,10},{12... | collective-permute-start | bytes 18440 | tf_op jit(solution)/shard_map/ppermute | solution.py:29
  201.9 6.1 %collective-permute-start.20 = (f32[3,2,12,32]{3,2,1,0:T(8,128)S(1)}, f32[3,2,12,32]{3,2,1,0:T(8,128)S(1)}, u32[]{:S(2)}, u32[]{:S(2)}) collective-permute-start(f32[3,2,12,32]{3,2,1,0:T(8,128)S(1)} %get-tuple-element.162), channel_id=1, source_target_pairs={{8,0},{16,8},{24,16},{9,1},{17,9},{25,17},{10,2},{18,10},{26,18},{... | collective-permute-start | bytes 27656 | tf_op jit(solution)/shard_map/ppermute | solution.py:16
  203.2 6.0 %collective-permute-start.21 = (f32[3,2,12,32]{3,2,1,0:T(8,128)S(1)}, f32[3,2,12,32]{3,2,1,0:T(8,128)S(1)}, u32[]{:S(2)}, u32[]{:S(2)}) collective-permute-start(f32[3,2,12,32]{3,2,1,0:T(8,128)S(1)} %get-tuple-element.161), channel_id=1, source_target_pairs={{0,8},{8,16},{16,24},{1,9},{9,17},{17,25},{2,10},{10,18},{18,26},{... | collective-permute-start | bytes 27656 | tf_op jit(solution)/shard_map/ppermute | solution.py:16
  209.2 5.6 %collective-permute-start.22 = (f32[3,4,2,32]{3,2,1,0:T(2,128)S(1)}, f32[3,4,2,32]{3,2,1,0:T(2,128)S(1)}, u32[]{:S(2)}, u32[]{:S(2)}) collective-permute-start(f32[3,4,2,32]{3,2,1,0:T(2,128)S(1)} %get-tuple-element.170), channel_id=1, source_target_pairs={{1,0},{2,1},{3,2},{4,3},{5,4},{6,5},{7,6},{9,8},{10,9},{11,10},{12... | collective-permute-start | bytes 9224 | tf_op jit(solution)/shard_map/ppermute | solution.py:16
  211.2 4.5 %collective-permute-start.23 = (f32[3,4,2,32]{3,2,1,0:T(2,128)S(1)}, f32[3,4,2,32]{3,2,1,0:T(2,128)S(1)}, u32[]{:S(2)}, u32[]{:S(2)}) collective-permute-start(f32[3,4,2,32]{3,2,1,0:T(2,128)S(1)} %get-tuple-element.169), channel_id=1, source_target_pairs={{0,1},{1,2},{2,3},{3,4},{4,5},{5,6},{6,7},{8,9},{9,10},{10,11},{11... | collective-permute-start | bytes 9224 | tf_op jit(solution)/shard_map/ppermute | solution.py:16
  (5 other events, 165.8 us)
where the time goes:
time: 269 us; the launch traced here: 264 us
  blocking collectives  83.7 us (31%)
  starting transfers between devices  72.4 us (27%)
  waiting for transfers between devices  44.4 us (17%)
  matrix products  35.9 us (13%)
  other arithmetic  12.3 us (5%)
  between operations  7.48 us (3%)
  local copies, waits for them, and re-layouts  7.36 us (3%)
    psum x2, blocking collectives, two_products(): lax.psum((jnp.sum(residual * residual), jnp.sum(residual * image)), ('gz'...  83.7 us
    ppermute x12, starting transfers between devices, from_behind(): lax.ppermute(value, axis, [(source, source + steps) for source in range(i...  34.9 us
    ppermute x6, waiting for transfers between devices, padded_2(): lax.ppermute(head, axis, [((i + 1) % count, i) for i in range(ends)])  29.8 us
    ppermute x6, starting transfers between devices, padded_2(): lax.ppermute(tail, axis, [(i, (i + 1) % count) for i in range(ends)])  27.8 us
    dot_general x3, matrix products, encode(): inner = jnp.einsum('za,czyx->cayx', along_z, volume, precision=hp)  14.5 us
    dot_general x2, matrix products, decode(): return jnp.einsum('za,cayx->czyx', along_z, inner, precision=hp)  12.2 us
    ppermute x6, starting transfers between devices, padded_2(): lax.ppermute(head, axis, [((i + 1) % count, i) for i in range(ends)])  9.81 us
    ppermute x6, waiting for transfers between devices, padded_2(): lax.ppermute(tail, axis, [(i, (i + 1) % count) for i in range(ends)])  9.12 us
  transfers between devices with their start and end apart: 24, of which 13 were waited for; matrix products, arithmetic and copies ran while one was open for 1% of the time, Pallas kernels for 0%

commit v1 on v0

v1 whole, which is shorter than its diff:
```python
import functools

import jax
import jax.numpy as jnp
import numpy as np
from jax import lax
from jax.experimental import pallas as pl
from jax.experimental.pallas import tpu as pltpu
from jax.sharding import PartitionSpec as P

SPACING = 8
DAMPING = 8.0
LANES = 128
F32 = jnp.float32
BF16 = jnp.bfloat16
VMEM = pl.BlockSpec(memory_space=pltpu.VMEM)
PARAMS = pltpu.CompilerParams(vmem_limit_bytes=20 * 1024 * 1024)


def round_up(value, step):
    return -(-value // step) * step


class Sizes:
    def __init__(self, shape):
        self.sz, self.sy, self.nx = shape
        self.cz, self.cy, self.cx = (n // SPACING for n in shape)
        self.na, self.nb = self.cz + 3, self.cy + 3
        self.ap = round_up(self.na, 8)
        self.rows = self.nb * self.ap
        self.rp = round_up(self.rows, LANES)
        self.used = 3 * self.cx
        self.lp = round_up(self.used + 1, LANES)
        self.zface = round_up(3 * self.nb, 8)
        self.yface = 3 * self.ap
        self.own = self.cz * self.cy
        self.block = round_up(max(2 * self.cy, 2 * self.cz, 8), 8)


def taps():
    t = (np.arange(SPACING) + 0.5) / SPACING
    return np.stack(
        [
            (1 - t) ** 3 / 6,
            (3 * t**3 - 6 * t**2 + 4) / 6,
            (-3 * t**3 + 3 * t**2 + 3 * t + 1) / 6,
            t**3 / 6,
        ]
    )


def basis(count, columns, offset):
    w = taps()
    out = np.zeros((count, columns))
    for v in range(count):
        for k in range(4):
            col = v // SPACING - 1 + k + offset
            if 0 <= col < columns:
                out[v, col] += w[k, v % SPACING]
    return out


def halves(matrix):
    high = np.asarray(matrix, np.float32).astype(jnp.bfloat16)
    low = (matrix - high.astype(np.float64)).astype(np.float32).astype(jnp.bfloat16)
    return high, low


def decode_consts(s):
    by = basis(s.sy, s.nb, 1)
    kd = np.zeros((s.na * s.sy, s.rp))
    for a in range(s.na):
        for b in range(s.nb):
            kd[a * s.sy : (a + 1) * s.sy, b * s.ap + a] = by[:, b]
    kh, kl = halves(kd)
    xh, xl = halves(x_matrix(s))
    return (
        np.concatenate([kh, kh], 1),
        kl,
        np.concatenate([xh, xh], 0),
        xl,
    )


def x_matrix(s):
    bx = basis(s.nx, s.cx, 0)
    out = np.zeros((s.lp, 3 * s.nx))
    for c in range(3):
        out[c * s.cx : (c + 1) * s.cx, c * s.nx : (c + 1) * s.nx] = bx.T
    return out


def encode_x_consts(s):
    xh, xl = halves(x_matrix(s).T)
    return np.concatenate([xh, xl], 1), xh


def y_rows(s, order):
    by = basis(s.sy, s.nb, 1)
    out = np.zeros((len(order), s.na * s.sy))
    for row, item in enumerate(order):
        if item is not None:
            a, b = item
            out[row, a * s.sy : (a + 1) * s.sy] = by[:, b]
    return halves(out)


def padded(order, count):
    return order + [None] * (count - len(order))


def grid_order(s):
    return [(a, b) if a < s.na else None for b in range(s.nb) for a in range(s.ap)]


def exchange_order(s):
    down = [(k, b) for b in range(s.nb) for k in range(3)]
    up = [(s.cz + k, b) for b in range(s.nb) for k in range(3)]
    return grid_order(s) + padded(down, s.zface) + padded(up, s.zface)


def spans(count):
    return {
        -1: ([0], [count - 1]),
        0: (list(range(1, count + 1)), list(range(count))),
        1: ([count + 1, count + 2], [0, 1]),
    }


NEIGHBOURS = [(dz, dy) for dz in (-1, 0, 1) for dy in (-1, 0, 1) if dz or dy]


def message(s, dz, dy):
    za, ta = spans(s.cz)[dz]
    yb, tb = spans(s.cy)[dy]
    if dy == 0:
        return [(a, b) for a in za for b in yb], [(a, b) for a in ta for b in tb]
    return [(a, b) for b in yb for a in za], [(a, b) for b in tb for a in ta]


def final_order(s):
    order = [(a + 1, b + 1) for a in range(s.cz) for b in range(s.cy)]
    starts = []
    for dz, dy in NEIGHBOURS:
        starts.append(len(order))
        mine = message(s, dz, dy)[0]
        order = order + padded(mine, round_up(len(mine), 8))
    return order, starts


def gradient_consts(s):
    coef = {-3: -1.0, -2: 9.0, -1: -45.0, 1: 45.0, 2: -9.0, 3: 1.0}
    dx = np.zeros((s.nx, s.nx))
    for x in range(s.nx):
        for d, value in coef.items():
            if 0 <= x + d < s.nx:
                dx[x + d, x] = value
    dy = np.zeros((s.sy, s.sy + 16))
    for y in range(s.sy):
        for d, value in coef.items():
            at = y + d
            if at < 0:
                dy[y, s.sy + 3 + at] = value
            elif at >= s.sy:
                dy[y, s.sy + 3 + at - s.sy] = value
            else:
                dy[y, at] = value
    return dx.astype(jnp.bfloat16), dy.astype(jnp.bfloat16)


def split(value):
    high = value.astype(BF16)
    return high, (value - high.astype(F32)).astype(BF16)


def dot(a, b):
    return jnp.dot(a, b, preferred_element_type=F32)


def place(axis):
    index = lax.axis_index(axis)
    count = lax.axis_size(axis)
    return index, index > 0, index < count - 1, lax.rem(index, 2) == 0


def z_weights():
    w = taps()
    even = 0.5 * (w[0] + w[3])
    odd0 = 0.5 * (w[0] - w[3])
    odd1 = 0.5 * (w[1] - w[2])
    return [(float(even[k]), float(odd0[k]), float(odd1[k])) for k in range(SPACING // 2)]


def encode_cell(volume):
    sums = None
    for k, (ev, o0, o1) in enumerate(z_weights()):
        near, far = volume(k)
        new = []
        for c in range(3):
            e = near[c] + far[c]
            o = near[c] - far[c]
            new.append((e, ev * e, o0 * o, o1 * o))
        if sums is None:
            sums = new
        else:
            sums = [tuple(x + y for x, y in zip(old, add)) for old, add in zip(sums, new)]
    out = []
    for total, outer, o0, o1 in sums:
        inner = 0.5 * total - outer
        out.append((outer + o0, inner + o1, inner - o1, outer - o0))
    return out


def decode_cell(p):
    parts = []
    for p0, p1, p2, p3 in p:
        s12 = p1 + p2
        parts.append((0.5 * s12, (p0 + p3) - s12, p0 - p3, p1 - p2))
    weights = z_weights()

    def at(k):
        ev, o0, o1 = weights[k]
        near, far = [], []
        for half, outer, d03, d12 in parts:
            even = half + ev * outer
            odd = o0 * d03 + o1 * d12
            near.append(even + odd)
            far.append(even - odd)
        return near, far

    return at


def decode_xy(control, consts, f_ref):
    yh_ref, yl_ref, xh_ref, xl_ref = consts
    ph, plow = split(control)
    inner = dot(yh_ref[...], jnp.concatenate([ph, plow], 0)) + dot(yl_ref[...], ph)
    ih, il = split(inner)
    f_ref[...] = dot(jnp.concatenate([ih, il], 1), xh_ref[...]) + dot(ih, xl_ref[...])


def encode_xy(e_ref, x_consts, y_consts):
    xw_ref, xh_ref = x_consts
    yh_ref, yl_ref = y_consts
    eh, el = split(e_ref[...])
    wide = dot(eh, xw_ref[...])
    lp = wide.shape[1] // 2
    inner = wide[:, :lp] + wide[:, lp:] + dot(el, xh_ref[...])
    ih, il = split(inner)
    wide = dot(yh_ref[...], jnp.concatenate([ih, il], 1))
    return wide[:, :lp] + wide[:, lp:] + dot(yl_ref[...], ih)


def store_rows(e_ref, s, a, y0, lane, values):
    for c in range(3):
        e_ref[pl.ds(a * s.sy + y0, 8), pl.ds(c * s.nx + lane, LANES)] = values[c]


def load_rows(f_ref, s, a, y0, lane):
    return [
        f_ref[pl.ds(a * s.sy + y0, 8), pl.ds(c * s.nx + lane, LANES)] for c in range(3)
    ]


def gradient_planes(s, planes, near, s_plane, halo_ref, dx_ref, dy_ref, put):
    dx = dx_ref[...]
    dy = dy_ref[...]
    scale = F32(1.0 / 120.0)

    def step(i, carry):
        centre = near(i, 0)
        sh, sl = split(centre)
        hh, hl = split(halo_ref[s_plane(i)])
        gx = dot(sh, dx) + dot(sl, dx)
        gy = dot(dy, jnp.concatenate([sh, hh], 0)) + dot(dy, jnp.concatenate([sl, hl], 0))
        gz = (
            45.0 * (near(i, 1) - near(i, -1))
            - 9.0 * (near(i, 2) - near(i, -2))
            + (near(i, 3) - near(i, -3))
        )
        for c, value in enumerate((gz, gy, gx)):
            put(i, c, (value * scale).astype(BF16).astype(F32))
        return carry

    lax.fori_loop(0, planes, step, 0)


def mid_kernel(s, f_ref, m_ref, sum_ref, ra_ref, rb_ref, dx_ref, dy_ref, g_ref, e_ref, h_ref):
    _, below, above, even = place("gy")
    h_ref[...] = jnp.zeros_like(h_ref)
    for k in range(3):
        a, b = ra_ref[k], rb_ref[k]
        up = jnp.where(even, a, b)
        down = jnp.where(even, b, a)
        h_ref[:, k, :] = jnp.where(below, down, 0.0)
        h_ref[:, 3 + k, :] = jnp.where(above, up, 0.0)
    first = SPACING

    def put(i, c, value):
        g_ref[c, i] = value

    gradient_planes(
        s,
        s.sz - 2 * SPACING,
        lambda i, d: sum_ref[first + i + d],
        lambda i: first + i,
        h_ref,
        dx_ref,
        dy_ref,
        put,
    )

    def tile(t, carry):
        y0 = pl.multiple_of(t * 8, 8)
        for lane in range(0, s.nx, LANES):
            rows, cols = pl.ds(y0, 8), pl.ds(lane, LANES)
            pend = None
            for zc in range(1, s.cz - 1):

                def volume(k):
                    out = []
                    for v in (k, SPACING - 1 - k):
                        z = zc * SPACING + v
                        mm = f_ref[z, rows, cols] - m_ref[z, rows, cols]
                        out.append([mm * g_ref[c, z - first, rows, cols] for c in range(3)])
                    return out

                new = encode_cell(volume)
                if pend is not None:
                    new = [
                        (p[0] + n[0], p[1] + n[1], p[2] + n[2], n[3]) for p, n in zip(pend, new)
                    ]
                store_rows(e_ref, s, zc - 1, y0, lane, [n[0] for n in new])
                pend = [n[1:] for n in new]
            for k in range(3):
                store_rows(e_ref, s, s.cz - 2 + k, y0, lane, [p[k] for p in pend])
        return carry

    lax.fori_loop(0, s.sy // 8, tile, 0)


def edge_kernel(
    s, f_ref, m_ref, sum_ref, ra_ref, rb_ref, h_ref, em_ref, dx_ref, dy_ref,
    xw_ref, xh_ref, yh_ref, yl_ref, g_ref, p_ref, za_ref, zb_ref, t_ref, e_ref,
):
    _, below, above, even = place("gz")
    span = SPACING + 6
    for k in range(3):
        a, b = ra_ref[k], rb_ref[k]
        t_ref[k] = jnp.where(below, jnp.where(even, b, a), 0.0)
        t_ref[2 * span - 3 + k] = jnp.where(above, jnp.where(even, a, b), 0.0)
    t_ref[3:span] = sum_ref[0 : span - 3]
    t_ref[span : 2 * span - 3] = sum_ref[s.sz - span + 3 : s.sz]

    for side in range(2):
        base = side * span + 3
        shift = side * SPACING
        plane = 0 if side == 0 else s.sz - SPACING

        def put(i, c, value, shift=shift):
            g_ref[c, i + shift] = value

        gradient_planes(
            s,
            SPACING,
            lambda i, d, base=base: t_ref[base + i + d],
            lambda i, plane=plane: plane + i,
            h_ref,
            dx_ref,
            dy_ref,
            put,
        )

    def tile(t, carry):
        y0 = pl.multiple_of(t * 8, 8)
        for lane in range(0, s.nx, LANES):
            rows, cols = pl.ds(y0, 8), pl.ds(lane, LANES)
            layers = [None] * s.na
            for a in range(1, s.cz + 2):
                layers[a] = load_rows(em_ref, s, a - 1, y0, lane)
            for side, zc in ((0, 0), (1, s.cz - 1)):

                def volume(k):
                    out = []
                    for v in (k, SPACING - 1 - k):
                        z = zc * SPACING + v
                        mm = f_ref[z, rows, cols] - m_ref[z, rows, cols]
                        out.append(
                            [mm * g_ref[c, side * SPACING + v, rows, cols] for c in range(3)]
                        )
                    return out

                new = encode_cell(volume)
                for k in range(4):
                    a = zc + k
                    add = [n[k] for n in new]
                    old = layers[a]
                    layers[a] = add if old is None else [x + y for x, y in zip(old, add)]
            for a in range(s.na):
                store_rows(e_ref, s, a, y0, lane, layers[a])
        return carry

    lax.fori_loop(0, s.sy // 8, tile, 0)
    send_faces(s, encode_xy(e_ref, (xw_ref, xh_ref), (yh_ref, yl_ref)), p_ref, za_ref, zb_ref)


def send_faces(s, rows, p_ref, za_ref, zb_ref):
    even = place("gz")[3]
    p_ref[...] = rows[: s.rows]
    down = rows[s.rows : s.rows + s.zface]
    up = rows[s.rows + s.zface :]
    za_ref[...] = jnp.where(even, up, down)
    zb_ref[...] = jnp.where(even, down, up)


def fold_z_kernel(s, p_ref, ra_ref, rb_ref, o_ref, ya_ref, yb_ref, t_ref):
    _, below, above, even = place("gz")
    layer = lax.broadcasted_iota(jnp.int32, (s.rows, s.lp), 0) % s.ap
    first = jnp.where(below, 0, 1)
    last = jnp.where(above, s.cz + 2, s.cz)
    inside = (layer >= first) & (layer <= last)
    t_ref[...] = jnp.where(inside, p_ref[...], 0.0)
    a, b = ra_ref[...], rb_ref[...]
    up = jnp.where(above, jnp.where(even, a, b), 0.0)
    down = jnp.where(below, jnp.where(even, b, a), 0.0)
    for k in range(s.nb):
        low = k * s.ap
        t_ref[low : low + 3, :] += down[3 * k : 3 * k + 3, :]
        t_ref[low + s.cz : low + s.cz + 3, :] += up[3 * k : 3 * k + 3, :]
    total = t_ref[...]
    o_ref[...] = total
    even = place("gy")[3]
    down, up = total[: s.yface], total[s.cy * s.ap : s.cy * s.ap + s.yface]
    ya_ref[...] = jnp.where(even, up, down)
    yb_ref[...] = jnp.where(even, down, up)


def fold_y(s, p_ref, ra_ref, rb_ref, v_ref):
    _, below, above, even = place("gy")
    v_ref[...] = jnp.zeros_like(v_ref)
    v_ref[: s.rows, :] = p_ref[...]
    a, b = ra_ref[...], rb_ref[...]
    up, down = jnp.where(even, a, b), jnp.where(even, b, a)
    v_ref[: s.yface, :] += down
    high = s.cy * s.ap
    v_ref[high : high + s.yface, :] += up

    @pl.when(jnp.logical_not(below))
    def _():
        v_ref[: s.yface, :] = p_ref[: s.yface, :]
        v_ref[: s.ap, :] = jnp.zeros((s.ap, s.lp), F32)

    @pl.when(jnp.logical_not(above))
    def _():
        v_ref[high : high + s.yface, :] = p_ref[high : high + s.yface, :]
        v_ref[high + s.ap : high + s.yface, :] = jnp.zeros((s.yface - s.ap, s.lp), F32)


def own_part(s, v_ref, out_ref):
    for a in range(s.cz):
        out_ref[a * s.cy : (a + 1) * s.cy, :] = v_ref[pl.ds(s.ap + a + 1, s.cy, stride=s.ap), :]


def operate(s, v_ref, decode, g_mid, g_edge, f_ref, e_ref):
    decode_xy(v_ref[...], decode, f_ref)

    def tile(t, square):
        y0 = pl.multiple_of(t * 8, 8)
        for lane in range(0, s.nx, LANES):
            rows, cols = pl.ds(y0, 8), pl.ds(lane, LANES)
            pend = None
            layers = [load_rows(f_ref, s, a, y0, lane) for a in range(3)]
            for zc in range(s.cz):
                layers = layers[-3:] + [load_rows(f_ref, s, zc + 3, y0, lane)]
                field = decode_cell([[layers[i][c] for i in range(4)] for c in range(3)])
                if zc == 0:
                    g_ref, base = g_edge, 0
                elif zc == s.cz - 1:
                    g_ref, base = g_edge, SPACING
                else:
                    g_ref, base = g_mid, (zc - 1) * SPACING
                squares = []

                def volume(k):
                    out = []
                    for v, value in zip((k, SPACING - 1 - k), field(k)):
                        g = [g_ref[c, base + v, rows, cols] for c in range(3)]
                        dotted = g[0] * value[0] + g[1] * value[1] + g[2] * value[2]
                        squares.append(dotted * dotted)
                        out.append([g[c] * dotted for c in range(3)])
                    return out

                new = encode_cell(volume)
                for value in squares:
                    square = square + value
                if pend is not None:
                    new = [
                        (p[0] + n[0], p[1] + n[1], p[2] + n[2], n[3]) for p, n in zip(pend, new)
                    ]
                store_rows(e_ref, s, zc, y0, lane, [n[0] for n in new])
                pend = [n[1:] for n in new]
            for k in range(3):
                store_rows(e_ref, s, s.cz + k, y0, lane, [p[k] for p in pend])
        return square

    return lax.fori_loop(0, s.sy // 8, tile, jnp.zeros((8, LANES), F32))


def total_of(value):
    return jnp.sum(value, keepdims=True)


def apply_kernel(
    s, p_ref, ra_ref, rb_ref, gm_ref, ge_ref, d0, d1, d2, d3,
    xw_ref, xh_ref, yh_ref, yl_ref,
    o_ref, za_ref, zb_ref, own_ref, sum_ref, v_ref, f_ref, e_ref,
):
    fold_y(s, p_ref, ra_ref, rb_ref, v_ref)
    own_part(s, v_ref, own_ref)
    square = operate(s, v_ref, (d0, d1, d2, d3), gm_ref, ge_ref, f_ref, e_ref)
    send_faces(s, encode_xy(e_ref, (xw_ref, xh_ref), (yh_ref, yl_ref)), o_ref, za_ref, zb_ref)
    own = own_ref[...]
    sums = [total_of(own * own), total_of(square)]
    sum_ref[...] = moments(sums, 0)


def moments(sums, start):
    row = lax.broadcasted_iota(jnp.int32, (8, LANES), 0)
    out = jnp.zeros((8, LANES), F32)
    for k, value in enumerate(sums):
        out = jnp.where(row == start + k, value, out)
    return out


def last_kernel(
    s, starts, p_ref, ra_ref, rb_ref, gm_ref, ge_ref, m_ref, d0, d1, d2, d3,
    xw_ref, xh_ref, yh_ref, yl_ref,
    own_ref, part_ref, send_ref, v_ref, f_ref, e_ref,
):
    fold_y(s, p_ref, ra_ref, rb_ref, v_ref)
    own_part(s, v_ref, own_ref)
    square = operate(s, v_ref, (d0, d1, d2, d3), gm_ref, ge_ref, f_ref, e_ref)
    rows = encode_xy(e_ref, (xw_ref, xh_ref), (yh_ref, yl_ref))
    part_ref[...] = rows[: s.own]
    own = own_ref[...]
    sums = m_ref[...] + moments([total_of(own * own), total_of(square)], 2)
    free = lax.broadcasted_iota(jnp.int32, (8, s.lp), 1) >= s.used
    for d in range(send_ref.shape[0]):
        send_ref[d, 0:8, :] = sums
    iz, iy = lax.axis_index("gz"), lax.axis_index("gy")
    nz, ny = lax.axis_size("gz"), lax.axis_size("gy")
    for (dz, dy), start in zip(NEIGHBOURS, starts):
        count = round_up(len(message(s, dz, dy)[0]), 8)
        tz, ty = iz + dz, iy + dy
        ok = (tz >= 0) & (tz < nz) & (ty >= 0) & (ty < ny)

        @pl.when(ok)
        def _(start=start, count=count, target=tz * ny + ty):
            send_ref[target, 0:8, :] = jnp.where(free, sums, rows[start : start + 8])
            if count > 8:
                send_ref[target, 8:count, :] = rows[start + 8 : start + count]


def finish_kernel(s, v0_ref, v1_ref, part_ref, got_ref, u_ref, r_ref, t_ref):
    iz, iy = lax.axis_index("gz"), lax.axis_index("gy")
    nz, ny = lax.axis_size("gz"), lax.axis_size("gy")
    t_ref[...] = part_ref[...]
    for dz, dy in NEIGHBOURS:
        target = message(s, -dz, -dy)[1]
        tz, ty = iz + dz, iy + dy
        ok = (tz >= 0) & (tz < nz) & (ty >= 0) & (ty < ny)

        @pl.when(ok)
        def _(target=target, source=tz * ny + ty):
            row = 0
            while row < len(target):
                a, b = target[row]
                run = 1
                while row + run < len(target) and target[row + run] == (a, b + run):
                    run += 1
                at = a * s.cy + b
                t_ref[at : at + run, :] += got_ref[source, row : row + run, :]
                row += run

    tot = got_ref[0, 0:8, :]
    for d in range(1, got_ref.shape[0]):
        tot = tot + got_ref[d, 0:8, :]
    m0, m1, m2, m3 = (tot[k : k + 1, s.used : s.used + 1] for k in range(4))
    v0, v1, v2 = v0_ref[...], v1_ref[...], t_ref[...]
    rho = m1 / m0
    a0 = 1.0 / (rho + DAMPING)
    rr1 = a0 * a0 * (m2 - rho * m1)
    beta = rr1 / m0
    quad = a0 * a0 * (m3 - 2.0 * rho * m2 + rho * rho * m1) + DAMPING * rr1
    a1 = rr1 / (quad - beta * rr1 / a0)
    r1 = a0 * (rho * v0 - v1)
    image = a0 * (rho * v1 - v2) + DAMPING * r1 + beta * (v1 + DAMPING * v0)
    update = a0 * v0 + a1 * (r1 + beta * v0)
    residual = r1 - a1 * image
    for c in range(3):
        lanes = slice(c * s.cx, (c + 1) * s.cx)
        for a in range(s.cz):
            at = slice(a * s.cy, (a + 1) * s.cy)
            u_ref[c, a] = update[at, lanes]
            r_ref[c, a] = residual[at, lanes]


def swap(value_a, value_b, axis):
    count = lax.axis_size(axis)
    even = [(i, i ^ 1) for i in range(count)]
    odd = [(i, (i + (1 if i % 2 else -1)) % count) for i in range(count)]
    return lax.ppermute(value_a, axis, even), lax.ppermute(value_b, axis, odd)


def faces(fixed, moving, axis, dim):
    even = lax.rem(lax.axis_index(axis), 2) == 0
    high = fixed.shape[dim] - 3
    out = []
    for start in (jnp.where(even, high, 0), jnp.where(even, 0, high)):
        pair = [lax.dynamic_slice_in_dim(v, start, 3, dim) for v in (fixed, moving)]
        out.append(jnp.moveaxis(pair[0] + pair[1], dim, 0))
    return out


def call(kernel, name, outs, scratch, *args):
    shapes = [jax.ShapeDtypeStruct(o, F32) for o in outs]
    return pl.pallas_call(
        kernel,
        out_shape=shapes,
        in_specs=[VMEM] * len(args),
        out_specs=[VMEM] * len(outs),
        scratch_shapes=[pltpu.VMEM(n, F32) for n in scratch],
        compiler_params=PARAMS,
        name=name,
    )(*args)


def shards(fixed, moving):
    s = Sizes(fixed.shape)
    devices = lax.axis_size("gz") * lax.axis_size("gy")
    dx, dy = (jnp.asarray(v) for v in gradient_consts(s))
    decode = tuple(jnp.asarray(v) for v in decode_consts(s))
    encode_x = tuple(jnp.asarray(v) for v in encode_x_consts(s))
    encode_y = tuple(jnp.asarray(v) for v in y_rows(s, exchange_order(s)))
    order, starts = final_order(s)
    encode_last = tuple(jnp.asarray(v) for v in y_rows(s, order))

    ya, yb = swap(*faces(fixed, moving, "gy", 1), "gy")
    za, zb = swap(*faces(fixed, moving, "gz", 0), "gz")
    total = fixed + moving
    mid = s.sz - 2 * SPACING
    wide = (s.na * s.sy, 3 * s.nx)
    g_mid, e_mid, halo = call(
        functools.partial(mid_kernel, s),
        "mid",
        [(3, mid, s.sy, s.nx), ((s.cz + 1) * s.sy, 3 * s.nx), (s.sz, 16, s.nx)],
        [],
        fixed, moving, total, ya, yb, dx, dy,
    )
    grid = (s.rows, s.lp)
    zshape, yshape = (s.zface, s.lp), (s.yface, s.lp)
    g_edge, part, za, zb = call(
        functools.partial(edge_kernel, s),
        "edge",
        [(3, 2 * SPACING, s.sy, s.nx), grid, zshape, zshape],
        [(2 * (SPACING + 6), s.sy, s.nx), wide],
        fixed, moving, total, za, zb, halo, e_mid, dx, dy, *encode_x, *encode_y,
    )

    def fold_z(part, za, zb):
        za, zb = swap(za, zb, "gz")
        return call(
            functools.partial(fold_z_kernel, s), "fold_z", [grid, yshape, yshape], [grid], part, za, zb
        )

    part, ya, yb = fold_z(part, za, zb)
    ya, yb = swap(ya, yb, "gy")
    own = (s.own, s.lp)
    part, za, zb, v0, sums = call(
        functools.partial(apply_kernel, s),
        "apply",
        [grid, zshape, zshape, own, (8, LANES)],
        [(s.rp, s.lp), wide, wide],
        part, ya, yb, g_mid, g_edge, *decode, *encode_x, *encode_y,
    )
    part, ya, yb = fold_z(part, za, zb)
    ya, yb = swap(ya, yb, "gy")
    v1, part, send = call(
        functools.partial(last_kernel, s, starts),
        "last",
        [own, own, (devices, s.block, s.lp)],
        [(s.rp, s.lp), wide, wide],
        part, ya, yb, g_mid, g_edge, sums, *decode, *encode_x, *encode_last,
    )
    got = lax.all_to_all(send, ("gz", "gy"), 0, 0)
    out = (3, s.cz, s.cy, s.cx)
    return tuple(
        call(functools.partial(finish_kernel, s), "finish", [out, out], [own], v0, v1, part, got)
    )


def solution(mesh):
    return jax.shard_map(
        shards,
        mesh=mesh,
        in_specs=(P("gz", "gy", None), P("gz", "gy", None)),
        out_specs=(P(None, "gz", "gy", None), P(None, "gz", "gy", None)),
        check_vma=False,
    )
```

time: 269 us -> 67.8 us (0.25); the launches traced: 264 us -> 67.6 us
  blocking collectives: 83.7 us -> 13.8 us
  starting transfers between devices: 72.4 us -> 15.5 us
  matrix products: 35.9 us -> 0 us
  waiting for transfers between devices: 44.4 us -> 13.3 us
  Pallas kernels: 0 us -> 19.3 us
  other arithmetic: 12.3 us -> 3.35 us
  between operations: 7.48 us -> 0.88 us
  local copies, waits for them, and re-layouts: 7.36 us -> 1.38 us
    psum x2 -> x0, blocking collectives: 83.7 us -> none  [two_products(): lax.psum((jnp.sum(residual * residual), jnp.sum(residual * image)), ('gz'...]
    ppermute x24 -> x12, starting transfers between devices: 72.4 us -> 15.5 us  [swap(): return (lax.ppermute(value_a, axis, even), lax.ppermute(value_b, axis, odd))]
    dot_general x15 -> x0, matrix products: 35.9 us -> none  [the longest x3 14.5 us: encode(): inner = jnp.einsum('za,czyx->cayx', along_z, volume, precision=hp)]
    ppermute x24 -> x12, waiting for transfers between devices: 44.4 us -> 13.3 us  [swap(): return (lax.ppermute(value_a, axis, even), lax.ppermute(value_b, axis, odd))]
    pallas_call x0 -> x7, Pallas kernels: none -> 19.3 us  [call(): pl.pallas_call(kernel, out_shape=shapes, in_specs=[VMEM] * len(args), out...]
    all_to_all x0 -> x1, blocking collectives: none -> 13.8 us  [shards(): got = lax.all_to_all(send, ('gz', 'gy'), 0, 0)]
    another operation x1 -> x0, other arithmetic: 8.02 us -> none  [shards(): jnp.stack([derivative(framed[:, 3:-3, 3:-3], 0), derivative(framed[3:-3,...]
    another operation x1 -> x0, local copies, waits for them, and re-layouts: 4.65 us -> none  [shards(): pair = jnp.stack([fixed, moving])]
  transfers between devices with their start and end apart: 24 -> 12, of which waited for: 13 -> 9; matrix products, arithmetic and copies ran while one was open for 1% -> 5% of each run, Pallas kernels for 0% -> 7%
where the time goes in v1:
time: 67.8 us; the launch traced here: 67.6 us
  Pallas kernels  19.3 us (28%)
  starting transfers between devices  15.5 us (23%)
  blocking collectives  13.8 us (20%)
  waiting for transfers between devices  13.3 us (20%)
  other arithmetic  3.35 us (5%)
  local copies, waits for them, and re-layouts  1.38 us (2%)
  between operations  0.88 us (1%)
    pallas_call x7, Pallas kernels, call(): pl.pallas_call(kernel, out_shape=shapes, in_specs=[VMEM] * len(args), out...  19.3 us
    ppermute x12, starting transfers between devices, swap(): return (lax.ppermute(value_a, axis, even), lax.ppermute(value_b, axis, odd))  15.5 us
    all_to_all x1, blocking collectives, shards(): got = lax.all_to_all(send, ('gz', 'gy'), 0, 0)  13.8 us
    ppermute x12, waiting for transfers between devices, swap(): return (lax.ppermute(value_a, axis, even), lax.ppermute(value_b, axis, odd))  13.3 us
    add x1, other arithmetic, shards(): total = fixed + moving  1.87 us
    add x1, other arithmetic, faces(): out.append(jnp.moveaxis(pair[0] + pair[1], dim, 0))  1.41 us
  transfers between devices with their start and end apart: 12, of which 9 were waited for; matrix products, arithmetic and copies ran while one was open for 5% of the time, Pallas kernels for 7%

profile of v1, /device:TPU:1, one launch (start us, length us, event | category | flops | bytes accessed | tf_op | source)
XLA Modules:
  0.0 67.6 jit_solution(5994007282240939480)
XLA Ops:
  0.7 1.4 %dynamic-slice_add_fusion = (f32[3,64,256]{2,1,0:T(8,128)S(1)}, f32[3,64,256]{2,1,0:T(8,128)S(1)}) fusion(f32[32,64,256]{2,1,0:T(8,128)} %m_ref.3, s32[]{:T(128)S(6)} %select_n.22, f32[32,64,256]{2,1,0:T(8,128)} %f_ref.3, s32[]{:T(128)S(6)} %select_n.21), kind=kLoop, calls=%fused_computation | loop fusion | flops 98304 | bytes 1179656 | tf_op jit(solution)/shard_map/add | solution.py:621
  2.1 3.0 %collective-permute-start.1 = (f32[3,64,256]{2,1,0:T(8,128)S(1)}, f32[3,64,256]{2,1,0:T(8,128)S(1)}, u32[]{:S(2)}, u32[]{:S(2)}) collective-permute-start(f32[3,64,256]{2,1,0:T(8,128)S(1)} %get-tuple-element.44), channel_id=1, source_target_pairs={{0,24},{8,16},{16,8},{24,0},{1,25},{9,17},{17,9},{25,1},{2,26},{10... | collective-permute-start | bytes 589832 | tf_op jit(solution)/shard_map/ppermute | solution.py:612
  5.4 1.3 %constant_dynamic-slice_fusion.2 = (f32[32,3,256]{2,1,0:T(4,128)S(1)}, f32[32,3,256]{2,1,0:T(4,128)S(1)}, f32[32,3,256]{2,1,0:T(4,128)S(1)}, f32[32,3,256]{2,1,0:T(4,128)S(1)}) fusion(f32[32,64,256]{2,1,0:T(8,128)} %m_ref.3, s32[]{:T(128)S(6)} %select_n.24, s32[]{:T(128)S(6)} %select_n.23, f32[32,64,256]{2,1,0:T(8,128)} %f_ref.3), kind=kLoop, calls=%fused_computation.8 | loop fusion | bytes 786440 | tf_op jit(solution)/shard_map/dynamic_slice | solution.py:620
  6.7 1.3 %collective-permute-start.2 = (f32[3,32,256]{2,1,0:T(8,128)S(1)}, f32[3,32,256]{2,1,0:T(8,128)S(1)}, u32[]{:S(2)}, u32[]{:S(2)}) collective-permute-start(f32[3,32,256]{2,1,0:T(8,128)S(1)} %fusion.1), channel_id=1, source_target_pairs={{0,1},{1,0},{2,3},{3,2},{4,5},{5,4},{6,7},{7,6},{8,9},{9,8},{10,11... | collective-permute-start | bytes 294920 | tf_op jit(solution)/shard_map/ppermute | solution.py:612
  8.1 1.3 %collective-permute-start.3 = (f32[3,32,256]{2,1,0:T(8,128)S(1)}, f32[3,32,256]{2,1,0:T(8,128)S(1)}, u32[]{:S(2)}, u32[]{:S(2)}) collective-permute-start(f32[3,32,256]{2,1,0:T(8,128)S(1)} %fusion), channel_id=1, source_target_pairs={{0,7},{1,2},{2,1},{3,4},{4,3},{5,6},{6,5},{7,0},{8,15},{9,10},{10,... | collective-permute-start | bytes 294920 | tf_op jit(solution)/shard_map/ppermute | solution.py:612
  9.4 1.9 %add.10.sum_ref = f32[32,64,256]{2,1,0:T(8,128)S(1)} add(f32[32,64,256]{2,1,0:T(8,128)S(1)} %copy-done, f32[32,64,256]{2,1,0:T(8,128)} %m_ref.3) | non-fusion elementwise | flops 524288 | bytes 6291456 | tf_op jit(solution)/shard_map/add | solution.py:650
  11.3 1.2 %collective-permute-done.3.rb_ref = f32[3,32,256]{2,1,0:T(8,128)S(1)} collective-permute-done((f32[3,32,256]{2,1,0:T(8,128)S(1)}, f32[3,32,256]{2,1,0:T(8,128)S(1)}, u32[]{:S(2)}, u32[]{:S(2)}) %collective-permute-start.3) | collective-permute-done | bytes 98336 | tf_op jit(solution)/shard_map/ppermute | solution.py:612
  12.5 4.4 %mid.1 = (f32[3,16,64,256]{3,2,1,0:T(8,128)S(1)}, f32[320,768]{1,0:T(8,128)S(1)}, f32[32,16,256]{2,1,0:T(8,128)S(1)}) custom-call(f32[32,64,256]{2,1,0:T(8,128)S(1)} %copy-done, f32[32,64,256]{2,1,0:T(8,128)S(1)} %copy-done.1, f32[32,64,256]{2,1,0:T(8,128)S(1)} %add.10.sum_ref, f32[3,32,256]{2,1,0:T(8,128)S(1)} %collective-permute-done.2.ra_ref, ...), custom_call_target="tpu_custom_call" | custom-call | tf_op jit(solution)/shard_map/mid/pallas_call | solution.py:627
  17.0 5.2 %edge.1 = (f32[3,16,64,256]{3,2,1,0:T(8,128)S(1)}, f32[88,128]{1,0:T(8,128)S(1)}, f32[40,128]{1,0:T(8,128)S(1)}, f32[40,128]{1,0:T(8,128)S(1)}) custom-call(f32[32,64,256]{2,1,0:T(8,128)S(1)} %copy-done, f32[32,64,256]{2,1,0:T(8,128)S(1)} %copy-done.1, f32[32,64,256]{2,1,0:T(8,128)S(1)} %add.10.sum_ref, f32[3,64,256]{2,1,0:T(8,128)S(1)} %collective-permute-done.ra_ref, ...), custom_call_target="tpu_custom_call" | custom-call | tf_op jit(solution)/shard_map/edge/pallas_call | solution.py:627
  22.2 1.3 %collective-permute-start.4 = (f32[40,128]{1,0:T(8,128)S(1)}, f32[40,128]{1,0:T(8,128)S(1)}, u32[]{:S(2)}, u32[]{:S(2)}) collective-permute-start(f32[40,128]{1,0:T(8,128)S(1)} %get-tuple-element.26), channel_id=1, source_target_pairs={{0,8},{8,0},{16,24},{24,16},{1,9},{9,1},{17,25},{25,17},{2,10},{10... | collective-permute-start | bytes 61448 | tf_op jit(solution)/shard_map/ppermute | solution.py:612
  23.5 1.4 %collective-permute-done.4.ra_ref = f32[40,128]{1,0:T(8,128)S(1)} collective-permute-done((f32[40,128]{1,0:T(8,128)S(1)}, f32[40,128]{1,0:T(8,128)S(1)}, u32[]{:S(2)}, u32[]{:S(2)}) %collective-permute-start.4) | collective-permute-done | bytes 20512 | tf_op jit(solution)/shard_map/ppermute | solution.py:612
  24.9 2.1 %collective-permute-done.5.rb_ref = f32[40,128]{1,0:T(8,128)S(1)} collective-permute-done((f32[40,128]{1,0:T(8,128)S(1)}, f32[40,128]{1,0:T(8,128)S(1)}, u32[]{:S(2)}, u32[]{:S(2)}) %collective-permute-start.5) | collective-permute-done | bytes 20512 | tf_op jit(solution)/shard_map/ppermute | solution.py:612
  27.0 3.5 %collective-permute-start.6 = (f32[24,128]{1,0:T(8,128)S(1)}, f32[24,128]{1,0:T(8,128)S(1)}, u32[]{:S(2)}, u32[]{:S(2)}) collective-permute-start(f32[24,128]{1,0:T(8,128)S(1)} %get-tuple-element.29), channel_id=1, source_target_pairs={{0,1},{1,0},{2,3},{3,2},{4,5},{5,4},{6,7},{7,6},{8,9},{9,8},{10,11... | collective-permute-start | bytes 36872 | tf_op jit(solution)/shard_map/ppermute | solution.py:612
  30.5 0.8 %collective-permute-done.6.ra_ref = f32[24,128]{1,0:T(8,128)S(1)} collective-permute-done((f32[24,128]{1,0:T(8,128)S(1)}, f32[24,128]{1,0:T(8,128)S(1)}, u32[]{:S(2)}, u32[]{:S(2)}) %collective-permute-start.6) | collective-permute-done | bytes 12320 | tf_op jit(solution)/shard_map/ppermute | solution.py:612
  31.4 2.3 %collective-permute-done.7.rb_ref = f32[24,128]{1,0:T(8,128)S(1)} collective-permute-done((f32[24,128]{1,0:T(8,128)S(1)}, f32[24,128]{1,0:T(8,128)S(1)}, u32[]{:S(2)}, u32[]{:S(2)}) %collective-permute-start.7) | collective-permute-done | bytes 12320 | tf_op jit(solution)/shard_map/ppermute | solution.py:612
  33.7 4.4 %apply.1 = (f32[88,128]{1,0:T(8,128)S(1)}, f32[40,128]{1,0:T(8,128)S(1)}, f32[40,128]{1,0:T(8,128)S(1)}, f32[32,128]{1,0:T(8,128)S(1)}, f32[8,128]{1,0:T(8,128)S(1)}) custom-call(f32[88,128]{1,0:T(8,128)S(1)} %get-tuple-element.28.p_ref, f32[24,128]{1,0:T(8,128)S(1)} %collective-permute-done.6.ra_ref, f32[24,128]{1,0:T(8,128)S(1)} %collective-permute-done.7.rb_ref, ...), custom_call_target="tpu_custom_call" | custom-call | tf_op jit(solution)/shard_map/apply/pallas_call | solution.py:627
  38.4 1.2 %collective-permute-start.9 = (f32[40,128]{1,0:T(8,128)S(1)}, f32[40,128]{1,0:T(8,128)S(1)}, u32[]{:S(2)}, u32[]{:S(2)}) collective-permute-start(f32[40,128]{1,0:T(8,128)S(1)} %get-tuple-element.36), channel_id=1, source_target_pairs={{0,24},{8,16},{16,8},{24,0},{1,25},{9,17},{17,9},{25,1},{2,26},{10... | collective-permute-start | bytes 61448 | tf_op jit(solution)/shard_map/ppermute | solution.py:612
  39.6 1.2 %collective-permute-done.8.ra_ref = f32[40,128]{1,0:T(8,128)S(1)} collective-permute-done((f32[40,128]{1,0:T(8,128)S(1)}, f32[40,128]{1,0:T(8,128)S(1)}, u32[]{:S(2)}, u32[]{:S(2)}) %collective-permute-start.8) | collective-permute-done | bytes 20512 | tf_op jit(solution)/shard_map/ppermute | solution.py:612
  40.8 1.2 %collective-permute-done.9.rb_ref = f32[40,128]{1,0:T(8,128)S(1)} collective-permute-done((f32[40,128]{1,0:T(8,128)S(1)}, f32[40,128]{1,0:T(8,128)S(1)}, u32[]{:S(2)}, u32[]{:S(2)}) %collective-permute-start.9) | collective-permute-done | bytes 20512 | tf_op jit(solution)/shard_map/ppermute | solution.py:612
  42.0 3.4 %collective-permute-start.10 = (f32[24,128]{1,0:T(8,128)S(1)}, f32[24,128]{1,0:T(8,128)S(1)}, u32[]{:S(2)}, u32[]{:S(2)}) collective-permute-start(f32[24,128]{1,0:T(8,128)S(1)} %get-tuple-element.38), channel_id=1, source_target_pairs={{0,1},{1,0},{2,3},{3,2},{4,5},{5,4},{6,7},{7,6},{8,9},{9,8},{10,11... | collective-permute-start | bytes 36872 | tf_op jit(solution)/shard_map/ppermute | solution.py:612
  46.2 2.3 %collective-permute-done.11.rb_ref = f32[24,128]{1,0:T(8,128)S(1)} collective-permute-done((f32[24,128]{1,0:T(8,128)S(1)}, f32[24,128]{1,0:T(8,128)S(1)}, u32[]{:S(2)}, u32[]{:S(2)}) %collective-permute-start.11) | collective-permute-done | bytes 12320 | tf_op jit(solution)/shard_map/ppermute | solution.py:612
  48.5 4.4 %last.1 = (f32[32,128]{1,0:T(8,128)S(1)}, f32[32,128]{1,0:T(8,128)S(1)}, f32[32,16,128]{2,1,0:T(8,128)S(1)}) custom-call(f32[88,128]{1,0:T(8,128)S(1)} %get-tuple-element.37.p_ref, f32[24,128]{1,0:T(8,128)S(1)} %collective-permute-done.10.ra_ref, f32[24,128]{1,0:T(8,128)S(1)} %collective-permute-done.11.rb_ref, ...), custom_call_target="tpu_custom_call" | custom-call | tf_op jit(solution)/shard_map/last/pallas_call | solution.py:627
  52.9 13.8 %all_to_all.5.got_ref = f32[32,16,128]{2,1,0:T(8,128)S(1)} all-to-all(f32[32,16,128]{2,1,0:T(8,128)S(1)} %get-tuple-element.43), channel_id=1, replica_groups=mesh['gz'=4,'gy'=8] {'gz','gy'}, dimensions={0} | all-to-all | bytes 524288 | tf_op jit(solution)/shard_map/all_to_all | solution.py:695
  66.7 0.9 %finish.1 = (f32[3,4,8,32]{3,2,1,0:T(8,128)}, f32[3,4,8,32]{3,2,1,0:T(8,128)}) custom-call(f32[32,128]{1,0:T(8,128)S(1)} %get-tuple-element.33.v0_ref, f32[32,128]{1,0:T(8,128)S(1)} %get-tuple-element.41.v1_ref, f32[32,128]{1,0:T(8,128)S(1)} %get-tuple-element.42.part_ref, f32[32,16,128]{2,1,0:T(8,128)S(1)} %all_to_all.5.got_ref), custom_call_target="tpu_custom_call" | custom-call | tf_op jit(solution)/shard_map/finish/pallas_call | solution.py:627
  (41 shorter events, 1.7 us)
Async XLA Ops:
  0.6 8.7 %copy-start = (f32[32,64,256]{2,1,0:T(8,128)S(1)}, f32[32,64,256]{2,1,0:T(8,128)}, u32[]{:S(2)}) copy-start(f32[32,64,256]{2,1,0:T(8,128)} %f_ref.3) | copy-start | bytes 6291460
  2.1 14.8 %collective-permute-start.1 = (f32[3,64,256]{2,1,0:T(8,128)S(1)}, f32[3,64,256]{2,1,0:T(8,128)S(1)}, u32[]{:S(2)}, u32[]{:S(2)}) collective-permute-start(f32[3,64,256]{2,1,0:T(8,128)S(1)} %get-tuple-element.44), channel_id=1, source_target_pairs={{0,24},{8,16},{16,8},{24,0},{1,25},{9,17},{17,9},{25,1},{2,26},{10... | collective-permute-start | bytes 589832 | tf_op jit(solution)/shard_map/ppermute | solution.py:612
  5.1 11.8 %collective-permute-start = (f32[3,64,256]{2,1,0:T(8,128)S(1)}, f32[3,64,256]{2,1,0:T(8,128)S(1)}, u32[]{:S(2)}, u32[]{:S(2)}) collective-permute-start(f32[3,64,256]{2,1,0:T(8,128)S(1)} %get-tuple-element.45), channel_id=1, source_target_pairs={{0,8},{8,0},{16,24},{24,16},{1,9},{9,1},{17,25},{25,17},{2,10},{10... | collective-permute-start | bytes 589832 | tf_op jit(solution)/shard_map/ppermute | solution.py:612
  6.7 4.6 %collective-permute-start.2 = (f32[3,32,256]{2,1,0:T(8,128)S(1)}, f32[3,32,256]{2,1,0:T(8,128)S(1)}, u32[]{:S(2)}, u32[]{:S(2)}) collective-permute-start(f32[3,32,256]{2,1,0:T(8,128)S(1)} %fusion.1), channel_id=1, source_target_pairs={{0,1},{1,0},{2,3},{3,2},{4,5},{5,4},{6,7},{7,6},{8,9},{9,8},{10,11... | collective-permute-start | bytes 294920 | tf_op jit(solution)/shard_map/ppermute | solution.py:612
  8.0 4.4 %copy-start.1 = (f32[32,64,256]{2,1,0:T(8,128)S(1)}, f32[32,64,256]{2,1,0:T(8,128)}, u32[]{:S(2)}) copy-start(f32[32,64,256]{2,1,0:T(8,128)} %m_ref.3) | copy-start | bytes 6291460
  8.1 4.4 %collective-permute-start.3 = (f32[3,32,256]{2,1,0:T(8,128)S(1)}, f32[3,32,256]{2,1,0:T(8,128)S(1)}, u32[]{:S(2)}, u32[]{:S(2)}) collective-permute-start(f32[3,32,256]{2,1,0:T(8,128)S(1)} %fusion), channel_id=1, source_target_pairs={{0,7},{1,2},{2,1},{3,4},{4,3},{5,6},{6,5},{7,0},{8,15},{9,10},{10,... | collective-permute-start | bytes 294920 | tf_op jit(solution)/shard_map/ppermute | solution.py:612
  11.2 5.7 %copy-start.2 = (bf16[768,256]{1,0:T(8,128)(2,1)S(1)}, bf16[768,256]{1,0:T(8,128)(2,1)}, u32[]{:S(2)}) copy-start(bf16[768,256]{1,0:T(8,128)(2,1)} %constant.56.clone.xw_ref) | copy-start | bytes 1179652
  11.2 5.7 %copy-start.3 = (bf16[768,128]{1,0:T(8,128)(2,1)S(1)}, bf16[768,128]{1,0:T(8,128)(2,1)}, u32[]{:S(2)}) copy-start(bf16[768,128]{1,0:T(8,128)(2,1)} %constant.57.clone.xh_ref) | copy-start | bytes 589828
  11.2 5.7 %copy-start.7 = (bf16[168,448]{1,0:T(8,128)(2,1)S(1)}, bf16[168,448]{1,0:T(8,128)(2,1)}, u32[]{:S(2)}) copy-start(bf16[168,448]{1,0:T(8,128)(2,1)} %constant.59.clone.yl_ref) | copy-start | bytes 451588
  11.3 5.7 %copy-start.8 = (bf16[168,448]{1,0:T(8,128)(2,1)S(1)}, bf16[168,448]{1,0:T(8,128)(2,1)}, u32[]{:S(2)}) copy-start(bf16[168,448]{1,0:T(8,128)(2,1)} %constant.58.clone.yh_ref) | copy-start | bytes 451588
  17.0 16.7 %copy-start.4 = (bf16[256,768]{1,0:T(8,128)(2,1)S(1)}, bf16[256,768]{1,0:T(8,128)(2,1)}, u32[]{:S(2)}) copy-start(bf16[256,768]{1,0:T(8,128)(2,1)} %constant.54.clone.d2) | copy-start | bytes 1179652
  17.0 16.7 %copy-start.5 = (bf16[448,256]{1,0:T(8,128)(2,1)S(1)}, bf16[448,256]{1,0:T(8,128)(2,1)}, u32[]{:S(2)}) copy-start(bf16[448,256]{1,0:T(8,128)(2,1)} %constant.52.clone.d0) | copy-start | bytes 688132
  17.0 16.7 %copy-start.6 = (bf16[128,768]{1,0:T(8,128)(2,1)S(1)}, bf16[128,768]{1,0:T(8,128)(2,1)}, u32[]{:S(2)}) copy-start(bf16[128,768]{1,0:T(8,128)(2,1)} %constant.55.clone.d3) | copy-start | bytes 589828
  17.0 16.7 %copy-start.10 = (bf16[448,128]{1,0:T(8,128)(2,1)S(1)}, bf16[448,128]{1,0:T(8,128)(2,1)}, u32[]{:S(2)}) copy-start(bf16[448,128]{1,0:T(8,128)(2,1)} %constant.53.clone.d1) | copy-start | bytes 344068
  22.2 2.7 %collective-permute-start.4 = (f32[40,128]{1,0:T(8,128)S(1)}, f32[40,128]{1,0:T(8,128)S(1)}, u32[]{:S(2)}, u32[]{:S(2)}) collective-permute-start(f32[40,128]{1,0:T(8,128)S(1)} %get-tuple-element.26), channel_id=1, source_target_pairs={{0,8},{8,0},{16,24},{24,16},{1,9},{9,1},{17,25},{25,17},{2,10},{10... | collective-permute-start | bytes 61448 | tf_op jit(solution)/shard_map/ppermute | solution.py:612
  23.5 3.5 %collective-permute-start.5 = (f32[40,128]{1,0:T(8,128)S(1)}, f32[40,128]{1,0:T(8,128)S(1)}, u32[]{:S(2)}, u32[]{:S(2)}) collective-permute-start(f32[40,128]{1,0:T(8,128)S(1)} %get-tuple-element.27), channel_id=1, source_target_pairs={{0,24},{8,16},{16,8},{24,0},{1,25},{9,17},{17,9},{25,1},{2,26},{10... | collective-permute-start | bytes 61448 | tf_op jit(solution)/shard_map/ppermute | solution.py:612
  27.0 4.3 %collective-permute-start.6 = (f32[24,128]{1,0:T(8,128)S(1)}, f32[24,128]{1,0:T(8,128)S(1)}, u32[]{:S(2)}, u32[]{:S(2)}) collective-permute-start(f32[24,128]{1,0:T(8,128)S(1)} %get-tuple-element.29), channel_id=1, source_target_pairs={{0,1},{1,0},{2,3},{3,2},{4,5},{5,4},{6,7},{7,6},{8,9},{9,8},{10,11... | collective-permute-start | bytes 36872 | tf_op jit(solution)/shard_map/ppermute | solution.py:612
  30.5 3.1 %collective-permute-start.7 = (f32[24,128]{1,0:T(8,128)S(1)}, f32[24,128]{1,0:T(8,128)S(1)}, u32[]{:S(2)}, u32[]{:S(2)}) collective-permute-start(f32[24,128]{1,0:T(8,128)S(1)} %get-tuple-element.30), channel_id=1, source_target_pairs={{0,7},{1,2},{2,1},{3,4},{4,3},{5,6},{6,5},{7,0},{8,15},{9,10},{10,... | collective-permute-start | bytes 36872 | tf_op jit(solution)/shard_map/ppermute | solution.py:612
  33.7 14.8 %copy-start.11 = (bf16[104,448]{1,0:T(8,128)(2,1)S(1)}, bf16[104,448]{1,0:T(8,128)(2,1)}, u32[]{:S(2)}) copy-start(bf16[104,448]{1,0:T(8,128)(2,1)} %constant.61.clone.yl_ref) | copy-start | bytes 279556
  33.7 14.8 %copy-start.12 = (bf16[104,448]{1,0:T(8,128)(2,1)S(1)}, bf16[104,448]{1,0:T(8,128)(2,1)}, u32[]{:S(2)}) copy-start(bf16[104,448]{1,0:T(8,128)(2,1)} %constant.60.clone.yh_ref) | copy-start | bytes 279556
  38.1 2.7 %collective-permute-start.8 = (f32[40,128]{1,0:T(8,128)S(1)}, f32[40,128]{1,0:T(8,128)S(1)}, u32[]{:S(2)}, u32[]{:S(2)}) collective-permute-start(f32[40,128]{1,0:T(8,128)S(1)} %get-tuple-element.35), channel_id=1, source_target_pairs={{0,8},{8,0},{16,24},{24,16},{1,9},{9,1},{17,25},{25,17},{2,10},{10... | collective-permute-start | bytes 61448 | tf_op jit(solution)/shard_map/ppermute | solution.py:612
  38.4 3.5 %collective-permute-start.9 = (f32[40,128]{1,0:T(8,128)S(1)}, f32[40,128]{1,0:T(8,128)S(1)}, u32[]{:S(2)}, u32[]{:S(2)}) collective-permute-start(f32[40,128]{1,0:T(8,128)S(1)} %get-tuple-element.36), channel_id=1, source_target_pairs={{0,24},{8,16},{16,8},{24,0},{1,25},{9,17},{17,9},{25,1},{2,26},{10... | collective-permute-start | bytes 61448 | tf_op jit(solution)/shard_map/ppermute | solution.py:612
  42.0 4.2 %collective-permute-start.10 = (f32[24,128]{1,0:T(8,128)S(1)}, f32[24,128]{1,0:T(8,128)S(1)}, u32[]{:S(2)}, u32[]{:S(2)}) collective-permute-start(f32[24,128]{1,0:T(8,128)S(1)} %get-tuple-element.38), channel_id=1, source_target_pairs={{0,1},{1,0},{2,3},{3,2},{4,5},{5,4},{6,7},{7,6},{8,9},{9,8},{10,11... | collective-permute-start | bytes 36872 | tf_op jit(solution)/shard_map/ppermute | solution.py:612
  45.3 3.1 %collective-permute-start.11 = (f32[24,128]{1,0:T(8,128)S(1)}, f32[24,128]{1,0:T(8,128)S(1)}, u32[]{:S(2)}, u32[]{:S(2)}) collective-permute-start(f32[24,128]{1,0:T(8,128)S(1)} %get-tuple-element.39), channel_id=1, source_target_pairs={{0,7},{1,2},{2,1},{3,4},{4,3},{5,6},{6,5},{7,0},{8,15},{9,10},{10,... | collective-permute-start | bytes 36872 | tf_op jit(solution)/shard_map/ppermute | solution.py:612
  (2 other events, 8.9 us)

commit v2 on v0

v2 whole, which is shorter than its diff:
```python
import functools

import jax
import jax.numpy as jnp
import numpy as np
from jax import lax
from jax.experimental import pallas as pl
from jax.experimental.pallas import tpu as pltpu
from jax.sharding import PartitionSpec as P

SPACING = 8
DAMPING = 8.0
LANES = 128
REACH = 3
F32 = jnp.float32
BF16 = jnp.bfloat16
VMEM = pl.BlockSpec(memory_space=pltpu.VMEM)
HBM = pl.BlockSpec(memory_space=pltpu.MemorySpace.HBM)
PARAMS = pltpu.CompilerParams(vmem_limit_bytes=20 * 1024 * 1024)


def round_up(value, step):
    return -(-value // step) * step


class Sizes:
    def __init__(self, shape):
        self.sz, self.sy, self.nx = shape
        self.cz, self.cy, self.cx = (n // SPACING for n in shape)
        self.na, self.nb = self.cz + 3, self.cy + 3
        self.bp = round_up(self.nb, 16)
        self.per = round_up(self.na * self.cx, LANES)
        self.wide = 3 * self.per
        self.tap = 4 * self.cx
        self.face = round_up(REACH * self.cx, LANES)
        self.used = REACH * self.cx
        self.own = self.cz * self.cx
        self.cells = 3 * self.cz * self.sy
        self.pair = 2 * self.cx
        self.block = round_up(3 * self.pair + 1, LANES)
        assert self.tap % LANES == 0 and self.own % LANES == 0
        assert self.cy % 8 == 0 and self.bp == self.cy + 8 and self.cz > 1


def taps():
    t = (np.arange(SPACING) + 0.5) / SPACING
    return np.stack(
        [
            (1 - t) ** 3 / 6,
            (3 * t**3 - 6 * t**2 + 4) / 6,
            (-3 * t**3 + 3 * t**2 + 3 * t + 1) / 6,
            t**3 / 6,
        ]
    )


def basis(count, columns, offset):
    w = taps()
    out = np.zeros((count, columns))
    for v in range(count):
        for k in range(4):
            col = v // SPACING - 1 + k + offset
            if 0 <= col < columns:
                out[v, col] += w[k, v % SPACING]
    return out


def halves(matrix):
    high = np.asarray(matrix, np.float32).astype(jnp.bfloat16)
    low = (matrix - high.astype(np.float64)).astype(np.float32).astype(jnp.bfloat16)
    return high, low


def consts(s):
    by = basis(s.sy, s.bp, 1)
    yh, yl = halves(by)
    y_decode = np.concatenate([yh, yh, yl], 1)
    y_encode = np.concatenate([yh.T, yh.T, yl.T], 1)
    bx = basis(s.nx, s.cx, 0)
    w = taps()
    decode, encode = [], []
    for k in range(SPACING):
        high, low = halves(np.concatenate([w[t, k] * bx.T for t in range(4)], 0))
        encode.append(np.concatenate([high.T, low.T], 1))
    for sign in (1.0, -1.0):
        for k in range(SPACING // 2):
            parts = [0.5 * (w[t, k] + sign * w[3 - t, k]) * bx.T for t in range(2)]
            (h0, l0), (h1, l1) = (halves(v) for v in parts)
            flip = np.asarray(sign, jnp.bfloat16)
            zero = np.zeros((2 * s.cx, s.nx), jnp.bfloat16)
            decode.append(np.concatenate([h0, h1, flip * l1, flip * l0, h0, h1, zero], 0))
    return tuple(jnp.asarray(v) for v in (y_decode, np.stack(decode), y_encode, np.stack(encode)))


def gradient_consts(s):
    coef = {-3: -1.0, -2: 9.0, -1: -45.0, 1: 45.0, 2: -9.0, 3: 1.0}
    dx = np.zeros((s.nx, s.nx))
    for x in range(s.nx):
        for d, value in coef.items():
            if 0 <= x + d < s.nx:
                dx[x + d, x] = value
    dy = np.zeros((s.sy, s.sy + 16))
    for y in range(s.sy):
        for d, value in coef.items():
            at = y + d
            if at < 0:
                dy[y, s.sy + REACH + at] = value
            elif at >= s.sy:
                dy[y, s.sy + REACH + at - s.sy] = value
            else:
                dy[y, at] = value
    dx, dy = (v.astype(jnp.bfloat16) for v in (dx, dy))
    return jnp.asarray(np.concatenate([dx, dx], 0)), jnp.asarray(np.concatenate([dy, dy], 1))


def split(value):
    high = value.astype(BF16)
    return high, (value - high.astype(F32)).astype(BF16)


def dot(a, b):
    return jnp.dot(a, b, preferred_element_type=F32)


def rounded(value):
    return (value * F32(1.0 / 120.0)).astype(BF16).astype(F32)


def place(axis):
    index = lax.axis_index(axis)
    count = lax.axis_size(axis)
    return index > 0, index < count - 1, lax.rem(index, 2) == 0


def from_sides(even, a, b):
    return jnp.where(even, a, b), jnp.where(even, b, a)


def difference(near):
    return (
        45.0 * (near(1) - near(-1)) - 9.0 * (near(2) - near(-2)) + (near(3) - near(-3))
    )


def iota(shape, dim):
    return lax.broadcasted_iota(jnp.int32, shape, dim)


def roll(value, shift):
    shift = shift % value.shape[1]
    return pltpu.roll(value, shift, 1) if shift else value


def start_all(copies):
    for copy in copies:
        copy.start()
    return copies


def faces_z_kernel(s, f_ref, m_ref, za_ref, zb_ref, t_ref, sems):
    copies = []
    for i, ref in enumerate((f_ref, m_ref)):
        for j in range(2):
            z = pl.ds(j * (s.sz - REACH), REACH)
            copies.append(pltpu.make_async_copy(ref.at[z], t_ref.at[i, j], sems.at[i, j]))
    for copy in start_all(copies):
        copy.wait()
    even = place("gz")[2]
    down, up = (t_ref[0, j] + t_ref[1, j] for j in range(2))
    za_ref[...] = jnp.where(even, up, down)
    zb_ref[...] = jnp.where(even, down, up)


def faces_y_kernel(s, f_ref, m_ref, ya_ref, yb_ref):
    even = place("gy")[2]
    for k in range(REACH):
        high = s.sy - REACH + k
        down = f_ref[:, k, :] + m_ref[:, k, :]
        up = f_ref[:, high, :] + m_ref[:, high, :]
        ya_ref[k] = jnp.where(even, up, down)
        yb_ref[k] = jnp.where(even, down, up)


GROUP = 4


def start_kernel(s, f_ref, m_ref, dx_ref, sum_ref, diff_ref, gx_ref, gz_ref):
    dx = dx_ref[...]
    for i in range(s.sz // GROUP):
        planes = slice(i * GROUP, (i + 1) * GROUP)
        f, m = f_ref[planes], m_ref[planes]
        total = f + m
        sum_ref[planes] = total
        diff_ref[planes] = f - m
        sh, sl = split(total.reshape(GROUP * s.sy, s.nx))
        gx = rounded(dot(jnp.concatenate([sh, sl], 1), dx))
        gx_ref[planes] = gx.reshape(GROUP, s.sy, s.nx)

    def step(i, carry):
        for y in range(0, s.sy, 16):
            rows = slice(y, y + 16)
            gz_ref[i, rows] = rounded(difference(lambda d: sum_ref[i + REACH + d, rows]))
        return carry

    lax.fori_loop(0, s.sz - 2 * REACH, step, 0)


def edge_planes(s):
    return [z < REACH or z >= s.sz - REACH for z in range(s.sz)]


def put_volume(s, row, z, rows, diff_ref, grads, high_ref, low_ref):
    mm = diff_ref[z, rows]
    for c in range(3):
        high, low = split(mm * grads[c])
        at = slice(row + c * s.sy + rows.start, row + c * s.sy + rows.stop)
        high_ref[at, :] = high
        low_ref[at, :] = low


def inner_kernel(
    s, sum_ref, diff_ref, gx_ref, gz_ref, ra_ref, rb_ref, dy_ref, re_ref,
    gy_ref, acc_ref, h_ref, vh0, vh1, vl0, vl1,
):
    below, above, even = place("gy")
    h_ref[...] = jnp.zeros_like(h_ref)
    for k in range(REACH):
        up, down = from_sides(even, ra_ref[k], rb_ref[k])
        h_ref[:, k, :] = jnp.where(below, down, 0.0)
        h_ref[:, REACH + k, :] = jnp.where(above, up, 0.0)
    dy = dy_ref[...]

    def step(i, carry):
        for j in range(GROUP):
            z = i * GROUP + j
            sh, sl = split(sum_ref[z])
            hh, hl = split(h_ref[z])
            gy_ref[z] = rounded(dot(dy, jnp.concatenate([sh, hh, sl, hl], 0)))
        return carry

    lax.fori_loop(0, s.sz // GROUP, step, 0)
    waits = edge_planes(s)
    part = 3 * s.sy
    acc_ref[...] = jnp.zeros_like(acc_ref)
    for k in range(SPACING):
        vh, vl = ((vh0, vl0), (vh1, vl1))[k % 2]
        ready = [zc for zc in range(s.cz) if not waits[zc * SPACING + k]]
        for zc in ready:
            z = zc * SPACING + k
            for y in range(0, s.sy, 16):
                rows = slice(y, y + 16)
                grads = [r[i, rows] for r, i in ((gz_ref, z - REACH), (gy_ref, z), (gx_ref, z))]
                put_volume(s, zc * part, z, rows, diff_ref, grads, vh, vl)
        at = slice(ready[0] * part, (ready[-1] + 1) * part)
        weights = re_ref[k]
        acc_ref[at, :] += dot(
            jnp.concatenate([vh[at, :], vl[at, :]], 1), jnp.concatenate([weights, weights], 0)
        )


def edge_kernel(
    s, sum_ref, diff_ref, gx_ref, gy_ref, ra_ref, rb_ref, acc_in, ye_ref, re_ref,
    gz_ref, p_ref, za_ref, zb_ref, h_ref, vh_ref, vl_ref, acc_ref,
):
    below, above, even = place("gz")
    for k in range(REACH):
        up, down = from_sides(even, ra_ref[k], rb_ref[k])
        h_ref[k] = jnp.where(below, down, 0.0)
        h_ref[REACH + k] = jnp.where(above, up, 0.0)
    part = 3 * s.sy
    acc_ref[...] = acc_in[...]
    for side, zc in ((0, 0), (1, s.cz - 1)):
        first = 0 if side == 0 else s.sz - REACH
        for j in range(REACH):
            z = first + j
            for y in range(0, s.sy, 16):
                rows = slice(y, y + 16)

                def near(d):
                    if z + d < 0:
                        return h_ref[z + d + REACH, rows]
                    if z + d >= s.sz:
                        return h_ref[REACH + z + d - s.sz, rows]
                    return sum_ref[z + d, rows]

                gz = rounded(difference(near))
                gz_ref[side * REACH + j, rows] = gz
                row = (side * REACH + j) * part
                grads = [gz, gy_ref[z, rows], gx_ref[z, rows]]
                put_volume(s, row, z, rows, diff_ref, grads, vh_ref, vl_ref)
        lhs, rhs = [], []
        for j in range(REACH):
            row = (side * REACH + j) * part
            weights = re_ref[(first + j) % SPACING]
            for ref in (vh_ref, vl_ref):
                lhs.append(ref[row : row + part, :])
                rhs.append(weights)
        at = slice(zc * part, (zc + 1) * part)
        acc_ref[at, :] += dot(jnp.concatenate(lhs, 1), jnp.concatenate(rhs, 0))
    encode_y(s, acc_ref, ye_ref, p_ref)
    send_faces(s, p_ref, za_ref, zb_ref)


def encode_y(s, acc_ref, ye_ref, p_ref):
    columns = []
    for i in range(3 * s.cz):
        both = acc_ref[i * s.sy : (i + 1) * s.sy, :]
        columns.append(both[:, : s.tap] + both[:, s.tap :])
    high, low = split(jnp.concatenate(columns, 1))
    out = dot(ye_ref[...], jnp.concatenate([high, low, high], 0))
    for c in range(3):
        total = jnp.zeros((s.bp, s.per), F32)
        for zc in range(s.cz):
            at = (zc * 3 + c) * s.tap
            cell = out[:, at : at + s.tap]
            if s.per > s.tap:
                cell = jnp.concatenate([cell, jnp.zeros((s.bp, s.per - s.tap), F32)], 1)
            total = total + roll(cell, zc * s.cx)
        p_ref[:, c * s.per : (c + 1) * s.per] = total


def send_faces(s, p_ref, za_ref, zb_ref):
    even = place("gz")[2]
    for c in range(3):
        low = c * s.per
        down = p_ref[:, low : low + s.face]
        up = p_ref[:, low + s.own : low + s.own + s.face]
        at = slice(c * s.face, (c + 1) * s.face)
        za_ref[:, at] = jnp.where(even, up, down)
        zb_ref[:, at] = jnp.where(even, down, up)


def fold_z_kernel(s, p_ref, ra_ref, rb_ref, o_ref, ya_ref, yb_ref):
    below, above, even = place("gz")
    layer = iota((s.bp, s.per), 1) // s.cx
    first = jnp.where(below, 0, 1)
    last = jnp.where(above, s.cz + 2, s.cz)
    inside = (layer >= first) & (layer <= last)
    shared = iota((s.bp, s.face), 1) < s.used
    for c in range(3):
        low = c * s.per
        at = slice(c * s.face, (c + 1) * s.face)
        up, down = from_sides(even, ra_ref[:, at], rb_ref[:, at])
        o_ref[:, low : low + s.per] = jnp.where(inside, p_ref[:, low : low + s.per], 0.0)
        o_ref[:, low : low + s.face] += jnp.where(shared & below, down, 0.0)
        high = low + s.own
        o_ref[:, high : high + s.face] += jnp.where(shared & above, up, 0.0)
    even = place("gy")[2]
    down, up = o_ref[:8, :], o_ref[s.cy : s.cy + 8, :]
    ya_ref[...] = jnp.where(even, up, down)
    yb_ref[...] = jnp.where(even, down, up)


def fold_y(s, p_ref, ra_ref, rb_ref, v_ref):
    below, above, even = place("gy")
    up, down = from_sides(even, ra_ref[...], rb_ref[...])
    row = iota((s.bp, s.wide), 0)
    inside = (row >= jnp.where(below, 0, 1)) & (row <= jnp.where(above, s.cy + 2, s.cy))
    v_ref[...] = jnp.where(inside, p_ref[...], 0.0)
    shared = iota((8, s.wide), 0) < REACH
    v_ref[:8, :] += jnp.where(shared & below, down, 0.0)
    v_ref[s.cy : s.cy + 8, :] += jnp.where(shared & above, up, 0.0)


def own_part(s, v_ref, out_ref):
    for c in range(3):
        rows = v_ref[1 : s.cy + 1, c * s.per : (c + 1) * s.per]
        out_ref[:, c * s.own : (c + 1) * s.own] = roll(rows, -s.cx)[:, : s.own]


def operate(s, v_ref, yd_ref, rd_ref, re_ref, grads, scratch):
    even_ref, odd_ref, *pairs, acc_ref = scratch
    cells = []
    for zc in range(s.cz):
        for c in range(3):
            lanes = v_ref[:, c * s.per : (c + 1) * s.per]
            cell = roll(lanes, -zc * s.cx)[:, : s.tap]
            group = iota(cell.shape, 1) // s.cx % 2
            back = jnp.where(group == 0, roll(cell, s.cx), roll(cell, 3 * s.cx))
            cells += [cell + back, cell - back]
    ph, plow = split(jnp.concatenate(cells, 1))
    inner = dot(yd_ref[...], jnp.concatenate([ph, plow, ph], 0))
    for i in range(3 * s.cz):
        at = slice(i * s.sy, (i + 1) * s.sy)
        for j, ref in enumerate((even_ref, odd_ref)):
            low = (2 * i + j) * s.tap
            ref[at, :] = jnp.concatenate(split(inner[:, low : low + s.tap]), 1)
    gz_inner, gz_edge, gy_ref, gx_ref = grads
    square = jnp.zeros((16, s.nx), F32)
    half = SPACING // 2
    for k in range(half):
        fe_ref, fo_ref, w0, w1 = pairs[4 * (k % 2) : 4 * (k % 2) + 4]
        fe_ref[...] = dot(even_ref[...], rd_ref[k])
        fo_ref[...] = dot(odd_ref[...], rd_ref[half + k])
        for zc in range(s.cz):
            for y in range(0, s.sy, 16):
                rows = slice(y, y + 16)
                at = [
                    slice((zc * 3 + c) * s.sy + y, (zc * 3 + c) * s.sy + y + 16) for c in range(3)
                ]
                even = [fe_ref[i, :] for i in at]
                odd = [fo_ref[i, :] for i in at]
                for sign, v, w_ref in ((1, k, w0), (-1, SPACING - 1 - k, w1)):
                    z = zc * SPACING + v
                    if z < REACH:
                        gz_ref, iz = gz_edge, z
                    elif z >= s.sz - REACH:
                        gz_ref, iz = gz_edge, REACH + z - (s.sz - REACH)
                    else:
                        gz_ref, iz = gz_inner, z - REACH
                    g = [r[i, rows] for r, i in ((gz_ref, iz), (gy_ref, z), (gx_ref, z))]
                    f = [e + o if sign > 0 else e - o for e, o in zip(even, odd)]
                    dotted = g[0] * f[0] + g[1] * f[1] + g[2] * f[2]
                    square = square + dotted * dotted
                    for c in range(3):
                        w_ref[at[c], :] = (g[c] * dotted).astype(BF16)
        add = dot(
            jnp.concatenate([w0[...], w1[...]], 1),
            jnp.concatenate([re_ref[k], re_ref[SPACING - 1 - k]], 0),
        )
        acc_ref[...] = add if k == 0 else acc_ref[...] + add
    return square


def total_of(value):
    return jnp.sum(value, keepdims=True)


def moments(sums, start):
    row = iota((8, LANES), 0)
    out = jnp.zeros((8, LANES), F32)
    for k, value in enumerate(sums):
        out = jnp.where(row == start + k, value, out)
    return out


def apply_kernel(
    s, p_ref, ra_ref, rb_ref, gi_ref, ge_ref, gy_ref, gx_ref, yd_ref, rd_ref, ye_ref, re_ref,
    o_ref, za_ref, zb_ref, own_ref, sum_ref, v_ref, *scratch,
):
    fold_y(s, p_ref, ra_ref, rb_ref, v_ref)
    own_part(s, v_ref, own_ref)
    square = operate(
        s, v_ref, yd_ref, rd_ref, re_ref, (gi_ref, ge_ref, gy_ref, gx_ref), scratch
    )
    encode_y(s, scratch[-1], ye_ref, o_ref)
    send_faces(s, o_ref, za_ref, zb_ref)
    own = own_ref[...]
    sum_ref[...] = moments([total_of(own * own), total_of(square)], 0)


NEIGHBOURS = [(dz, dy) for dz in (-1, 0, 1) for dy in (-1, 0, 1) if dz or dy]


def neighbour(dz, dy):
    nz, ny = lax.axis_size("gz"), lax.axis_size("gy")
    tz, ty = lax.axis_index("gz") + dz, lax.axis_index("gy") + dy
    ok = (tz >= 0) & (tz < nz) & (ty >= 0) & (ty < ny)
    return ok, tz * ny + ty


def last_kernel(
    s, p_ref, ra_ref, rb_ref, gi_ref, ge_ref, gy_ref, gx_ref, m_ref,
    yd_ref, rd_ref, ye_ref, re_ref,
    own_ref, part_ref, send_ref, v_ref, o_ref, t_ref, y_ref, *scratch,
):
    fold_y(s, p_ref, ra_ref, rb_ref, v_ref)
    own_part(s, v_ref, own_ref)
    square = operate(
        s, v_ref, yd_ref, rd_ref, re_ref, (gi_ref, ge_ref, gy_ref, gx_ref), scratch
    )
    own = own_ref[...]
    sums = m_ref[...] + moments([total_of(own * own), total_of(square)], 2)
    encode_y(s, scratch[-1], ye_ref, o_ref)
    own_part(s, o_ref, part_ref)
    edge = s.block - LANES
    free = iota((8, LANES), 1) >= 3 * s.pair - edge
    base = jnp.where(free, sums, 0.0)
    for d in range(send_ref.shape[0]):
        send_ref[d, 0:8, edge:] = base
    lane = iota((s.bp, s.block), 1)
    t_ref[...] = jnp.zeros_like(t_ref)
    for i, dz in enumerate((-1, 1)):
        layer = 0 if dz < 0 else s.cz + 1
        width = s.cx if dz < 0 else s.pair
        total = jnp.zeros((s.bp, s.block), F32)
        for c in range(3):
            low = c * s.pair
            lanes = roll(o_ref[:, c * s.per : (c + 1) * s.per], low - layer * s.cx)
            total = jnp.where((lane >= low) & (lane < low + width), lanes[:, : s.block], total)
        t_ref[i, 8 : 8 + s.bp, :] = total
    for c in range(3):
        lanes = roll(o_ref[:, c * s.per : (c + 1) * s.per], -s.cx)
        y_ref[:, c * s.own : (c + 1) * s.own] = lanes[:, : s.own]
    for dz, dy in NEIGHBOURS:
        ok, target = neighbour(dz, dy)

        @pl.when(ok)
        def _(dz=dz, dy=dy, target=target):
            if dz:
                start = {-1: 9 - s.cy, 0: 9, 1: 9 + s.cy}[dy]
                rows = t_ref[(dz + 1) // 2, start : start + 8, :]
                send_ref[target, 0:8, :edge] = rows[:, :edge]
                send_ref[target, 0:8, edge:] = jnp.where(free, sums, rows[:, edge:])
            else:
                for c in range(3):
                    lanes = slice(c * s.own, (c + 1) * s.own)
                    if dy > 0:
                        send_ref[target, 2 * c : 2 * c + 2, : s.own] = y_ref[
                            s.cy + 1 : s.cy + 3, lanes
                        ]
                    else:
                        send_ref[target, c : c + 1, : s.own] = y_ref[0:1, lanes]


def finish_kernel(s, v0_ref, v1_ref, part_ref, got_ref, u_ref, r_ref, v_ref, t_ref):
    v_ref[...] = part_ref[...]
    for i, dz in enumerate((-1, 1)):
        t_ref[i] = jnp.zeros((8, s.block), F32)
        for dy in (-1, 0, 1):
            ok, source = neighbour(dz, dy)

            @pl.when(ok)
            def _(i=i, source=source):
                t_ref[i] += got_ref[source]

    lane = iota((8, s.own), 1)
    for c in range(3):
        low = c * s.pair
        lanes = slice(c * s.own, (c + 1) * s.own)
        first = roll(t_ref[0], -low)[:, : s.own]
        last = roll(t_ref[1], (s.cz - 1) * s.cx - low)[:, : s.own]
        v_ref[:, lanes] += jnp.where(lane < s.pair, first, 0.0)
        v_ref[:, lanes] += jnp.where(lane >= s.own - s.cx, last, 0.0)
    for dy in (-1, 1):
        ok, source = neighbour(0, dy)

        @pl.when(ok)
        def _(dy=dy, source=source):
            for c in range(3):
                lanes = slice(c * s.own, (c + 1) * s.own)
                if dy < 0:
                    v_ref[0:2, lanes] += got_ref[source, 2 * c : 2 * c + 2, : s.own]
                else:
                    v_ref[s.cy - 1 : s.cy, lanes] += got_ref[source, c : c + 1, : s.own]

    edge = s.block - LANES
    tot = got_ref[0, :, edge:]
    for d in range(1, got_ref.shape[0]):
        tot = tot + got_ref[d, :, edge:]
    m0, m1, m2, m3 = (tot[k : k + 1, LANES - 1 : LANES] for k in range(4))
    v0, v1, v2 = v0_ref[...], v1_ref[...], v_ref[...]
    rho = m1 / m0
    a0 = 1.0 / (rho + DAMPING)
    rr1 = a0 * a0 * (m2 - rho * m1)
    beta = rr1 / m0
    quad = a0 * a0 * (m3 - 2.0 * rho * m2 + rho * rho * m1) + DAMPING * rr1
    a1 = rr1 / (quad - beta * rr1 / a0)
    r1 = a0 * (rho * v0 - v1)
    image = a0 * (rho * v1 - v2) + DAMPING * r1 + beta * (v1 + DAMPING * v0)
    update = a0 * v0 + a1 * (r1 + beta * v0)
    residual = r1 - a1 * image
    for out_ref, value in ((u_ref, update), (r_ref, residual)):
        for c in range(3):
            for a in range(s.cz):
                at = c * s.own + a * s.cx
                out_ref[c, a] = value[:, at : at + s.cx]


def swap(value_a, value_b, axis):
    count = lax.axis_size(axis)
    even = [(i, i ^ 1) for i in range(count)]
    odd = [(i, (i + (1 if i % 2 else -1)) % count) for i in range(count)]
    return lax.ppermute(value_a, axis, even), lax.ppermute(value_b, axis, odd)


def scratch_of(item):
    if not isinstance(item, tuple):
        return item
    return pltpu.VMEM(*(item if isinstance(item[0], tuple) else (item, F32)))


def call(kernel, name, outs, scratch, *args, far=0):
    shapes = [jax.ShapeDtypeStruct(o, F32) for o in outs]
    return pl.pallas_call(
        kernel,
        out_shape=shapes,
        in_specs=[HBM] * far + [VMEM] * (len(args) - far),
        out_specs=[VMEM] * len(outs),
        scratch_shapes=[scratch_of(n) for n in scratch],
        compiler_params=PARAMS,
        name=name,
    )(*[pltpu.with_memory_space_constraint(v, pltpu.HBM) for v in args[:far]], *args[far:])


def shards(fixed, moving):
    s = Sizes(fixed.shape)
    devices = lax.axis_size("gz") * lax.axis_size("gy")
    dx, dy = gradient_consts(s)
    yd, rd, ye, re = consts(s)
    part = functools.partial

    zhalo, yhalo = (REACH, s.sy, s.nx), (REACH, s.sz, s.nx)
    za, zb = call(
        part(faces_z_kernel, s),
        "faces_z",
        [zhalo, zhalo],
        [(2, 2, *zhalo), pltpu.SemaphoreType.DMA((2, 2))],
        fixed, moving, far=2,
    )
    za, zb = swap(za, zb, "gz")
    ya, yb = call(part(faces_y_kernel, s), "faces_y", [yhalo, yhalo], [], fixed, moving)
    ya, yb = swap(ya, yb, "gy")
    volume = fixed.shape
    total, diff, gx, gz_inner = call(
        part(start_kernel, s),
        "start",
        [volume, volume, volume, (s.sz - 2 * REACH, s.sy, s.nx)],
        [],
        fixed, moving, dx,
    )
    acc = (s.cells, 2 * s.tap)
    half = ((s.cells, s.nx), BF16)
    gy, inner = call(
        part(inner_kernel, s),
        "inner",
        [volume, acc],
        [(s.sz, 16, s.nx), half, half, half, half],
        total, diff, gx, gz_inner, ya, yb, dy, re,
    )
    grid, zface, yface = (s.bp, s.wide), (s.bp, 3 * s.face), (8, s.wide)
    few = ((2 * REACH * 3 * s.sy, s.nx), BF16)
    gz_edge, grid0, za, zb = call(
        part(edge_kernel, s),
        "edge",
        [(2 * REACH, s.sy, s.nx), grid, zface, zface],
        [(2 * REACH, s.sy, s.nx), few, few, acc],
        total, diff, gx, gy, za, zb, inner, ye, re,
    )

    def fold_z(value, za, zb):
        za, zb = swap(za, zb, "gz")
        value, ya, yb = call(
            part(fold_z_kernel, s), "fold_z", [grid, yface, yface], [], value, za, zb
        )
        return (value, *swap(ya, yb, "gy"))

    own = (s.cy, 3 * s.own)
    field = (s.cells, s.nx)
    left = ((s.cells, 2 * s.tap), BF16)
    work = [left, left, *[field, field, half, half] * 2, acc]
    grads = (gz_inner, gz_edge, gy, gx)
    grid1, za, zb, v0, sums = call(
        part(apply_kernel, s),
        "apply",
        [grid, zface, zface, own, (8, LANES)],
        [grid, *work],
        *fold_z(grid0, za, zb), *grads, yd, rd, ye, re,
    )
    v1, mine, send = call(
        part(last_kernel, s),
        "last",
        [own, own, (devices, s.cy, s.block)],
        [grid, grid, (2, 16 + s.bp, s.block), (s.bp, 3 * s.own), *work],
        *fold_z(grid1, za, zb), *grads, sums, yd, rd, ye, re,
    )
    got = lax.all_to_all(send, ("gz", "gy"), 0, 0)
    out = (3, s.cz, s.cy, s.cx)
    return tuple(
        call(
            part(finish_kernel, s), "finish", [out, out], [own, (2, s.cy, s.block)], v0, v1, mine, got
        )
    )


def solution(mesh):
    return jax.shard_map(
        shards,
        mesh=mesh,
        in_specs=(P("gz", "gy", None), P("gz", "gy", None)),
        out_specs=(P(None, "gz", "gy", None), P(None, "gz", "gy", None)),
        check_vma=False,
    )
```

time: 269 us -> 59.1 us (0.22); the launches traced: 264 us -> 59 us
  blocking collectives: 83.7 us -> 14.3 us
  starting transfers between devices: 72.4 us -> 16.4 us
  matrix products: 35.9 us -> 0 us
  waiting for transfers between devices: 44.4 us -> 13.1 us
  Pallas kernels: 0 us -> 14.3 us
  other arithmetic: 12.3 us -> 0 us
  local copies, waits for them, and re-layouts: 7.36 us -> 0.04 us
  between operations: 7.48 us -> 0.76 us
    psum x2 -> x0, blocking collectives: 83.7 us -> none  [two_products(): lax.psum((jnp.sum(residual * residual), jnp.sum(residual * image)), ('gz'...]
    ppermute x24 -> x12, starting transfers between devices: 72.4 us -> 16.4 us  [swap(): return (lax.ppermute(value_a, axis, even), lax.ppermute(value_b, axis, odd))]
    dot_general x15 -> x0, matrix products: 35.9 us -> none  [the longest x3 14.5 us: encode(): inner = jnp.einsum('za,czyx->cayx', along_z, volume, precision=hp)]
    ppermute x24 -> x12, waiting for transfers between devices: 44.4 us -> 13.1 us  [swap(): return (lax.ppermute(value_a, axis, even), lax.ppermute(value_b, axis, odd))]
    all_to_all x0 -> x1, blocking collectives: none -> 14.3 us  [shards(): got = lax.all_to_all(send, ('gz', 'gy'), 0, 0)]
    pallas_call x0 -> x10, Pallas kernels: none -> 14.3 us  [call(): pl.pallas_call(kernel, out_shape=shapes, in_specs=[HBM] * far + [VMEM] *...]
    another operation x1 -> x0, other arithmetic: 8.02 us -> none  [shards(): jnp.stack([derivative(framed[:, 3:-3, 3:-3], 0), derivative(framed[3:-3,...]
    another operation x1 -> x0, local copies, waits for them, and re-layouts: 4.65 us -> none  [shards(): pair = jnp.stack([fixed, moving])]
  transfers between devices with their start and end apart: 24 -> 12, of which waited for: 13 -> 9; matrix products, arithmetic and copies ran while one was open for 1% -> 0% of each run, Pallas kernels for 0% -> 8%
where the time goes in v2:
time: 59.1 us; the launch traced here: 59 us
  starting transfers between devices  16.4 us (28%)
  Pallas kernels  14.3 us (24%)
  blocking collectives  14.3 us (24%)
  waiting for transfers between devices  13.1 us (22%)
  between operations  0.76 us (1%)
    ppermute x12, starting transfers between devices, swap(): return (lax.ppermute(value_a, axis, even), lax.ppermute(value_b, axis, odd))  16.4 us
    all_to_all x1, blocking collectives, shards(): got = lax.all_to_all(send, ('gz', 'gy'), 0, 0)  14.3 us
    pallas_call x10, Pallas kernels, call(): pl.pallas_call(kernel, out_shape=shapes, in_specs=[HBM] * far + [VMEM] *...  14.3 us
    ppermute x12, waiting for transfers between devices, swap(): return (lax.ppermute(value_a, axis, even), lax.ppermute(value_b, axis, odd))  13.1 us
  transfers between devices with their start and end apart: 12, of which 9 were waited for; matrix products, arithmetic and copies ran while one was open for 0% of the time, Pallas kernels for 8%

profile of v2, /device:TPU:1, one launch (start us, length us, event | category | flops | bytes accessed | tf_op | source)
XLA Modules:
  0.0 59.0 jit_solution(7183809594626919516)
XLA Ops:
  0.6 1.4 %faces_z.1 = (f32[3,64,256]{2,1,0:T(8,128)S(1)}, f32[3,64,256]{2,1,0:T(8,128)S(1)}) custom-call(f32[32,64,256]{2,1,0:T(8,128)} %f_ref.5, f32[32,64,256]{2,1,0:T(8,128)} %m_ref.5), custom_call_target="tpu_custom_call" | custom-call | tf_op jit(solution)/shard_map/faces_z/pallas_call | solution.py:585
  2.1 2.1 %collective-permute-start.2 = (f32[3,64,256]{2,1,0:T(8,128)S(1)}, f32[3,64,256]{2,1,0:T(8,128)S(1)}, u32[]{:S(2)}, u32[]{:S(2)}) collective-permute-start(f32[3,64,256]{2,1,0:T(8,128)S(1)} %get-tuple-element.37), channel_id=1, source_target_pairs={{0,8},{8,0},{16,24},{24,16},{1,9},{9,1},{17,25},{25,17},{2,10},{10... | collective-permute-start | bytes 589832 | tf_op jit(solution)/shard_map/ppermute | solution.py:574
  4.2 1.2 %collective-permute-start.3 = (f32[3,64,256]{2,1,0:T(8,128)S(1)}, f32[3,64,256]{2,1,0:T(8,128)S(1)}, u32[]{:S(2)}, u32[]{:S(2)}) collective-permute-start(f32[3,64,256]{2,1,0:T(8,128)S(1)} %get-tuple-element.38), channel_id=1, source_target_pairs={{0,24},{8,16},{16,8},{24,0},{1,25},{9,17},{17,9},{25,1},{2,26},{10... | collective-permute-start | bytes 589832 | tf_op jit(solution)/shard_map/ppermute | solution.py:574
  5.6 1.3 %collective-permute-start = (f32[3,32,256]{2,1,0:T(8,128)S(1)}, f32[3,32,256]{2,1,0:T(8,128)S(1)}, u32[]{:S(2)}, u32[]{:S(2)}) collective-permute-start(f32[3,32,256]{2,1,0:T(8,128)S(1)} %get-tuple-element.34), channel_id=1, source_target_pairs={{0,1},{1,0},{2,3},{3,2},{4,5},{5,4},{6,7},{7,6},{8,9},{9,8},{10,11... | collective-permute-start | bytes 294920 | tf_op jit(solution)/shard_map/ppermute | solution.py:574
  6.9 1.3 %collective-permute-start.1 = (f32[3,32,256]{2,1,0:T(8,128)S(1)}, f32[3,32,256]{2,1,0:T(8,128)S(1)}, u32[]{:S(2)}, u32[]{:S(2)}) collective-permute-start(f32[3,32,256]{2,1,0:T(8,128)S(1)} %get-tuple-element.35), channel_id=1, source_target_pairs={{0,7},{1,2},{2,1},{3,4},{4,3},{5,6},{6,5},{7,0},{8,15},{9,10},{10,... | collective-permute-start | bytes 294920 | tf_op jit(solution)/shard_map/ppermute | solution.py:574
  8.1 1.6 %start.1 = (f32[32,64,256]{2,1,0:T(8,128)S(1)}, f32[32,64,256]{2,1,0:T(8,128)S(1)}, f32[32,64,256]{2,1,0:T(8,128)S(1)}, f32[26,64,256]{2,1,0:T(8,128)S(1)}) custom-call(f32[32,64,256]{2,1,0:T(8,128)S(1)} %copy-done, f32[32,64,256]{2,1,0:T(8,128)S(1)} %copy-done.1, bf16[512,256]{1,0:T(8,128)(2,1)S(1)} %copy-done.4), custom_call_target="tpu_custom_call" | custom-call | tf_op jit(solution)/shard_map/start/pallas_call | solution.py:585
  9.8 1.1 %collective-permute-done.1.rb_ref = f32[3,32,256]{2,1,0:T(8,128)S(1)} collective-permute-done((f32[3,32,256]{2,1,0:T(8,128)S(1)}, f32[3,32,256]{2,1,0:T(8,128)S(1)}, u32[]{:S(2)}, u32[]{:S(2)}) %collective-permute-start.1) | collective-permute-done | bytes 98336 | tf_op jit(solution)/shard_map/ppermute | solution.py:574
  10.9 3.2 %inner.1 = (f32[32,64,256]{2,1,0:T(8,128)S(1)}, f32[768,256]{1,0:T(8,128)S(1)}) custom-call(f32[32,64,256]{2,1,0:T(8,128)S(1)} %get-tuple-element.30.sum_ref, f32[32,64,256]{2,1,0:T(8,128)S(1)} %get-tuple-element.31.diff_ref, f32[32,64,256]{2,1,0:T(8,128)S(1)} %get-tuple-element.32.gx_ref, f32[26,64,256]{2,1,0:T(8,128)S(1)} %get-tuple-element.33.gz_ref.gi_ref, ...), custom_call_target="tpu_custom_call" | custom-call | tf_op jit(solution)/shard_map/inner/pallas_call | solution.py:585
  14.1 0.9 %edge.1 = (f32[6,64,256]{2,1,0:T(8,128)S(1)}, f32[16,768]{1,0:T(8,128)S(1)}, f32[16,384]{1,0:T(8,128)S(1)}, f32[16,384]{1,0:T(8,128)S(1)}) custom-call(f32[32,64,256]{2,1,0:T(8,128)S(1)} %get-tuple-element.30.sum_ref, f32[32,64,256]{2,1,0:T(8,128)S(1)} %get-tuple-element.31.diff_ref, f32[32,64,256]{2,1,0:T(8,128)S(1)} %get-tuple-element.32.gx_ref, ...), custom_call_target="tpu_custom_call" | custom-call | tf_op jit(solution)/shard_map/edge/pallas_call | solution.py:585
  15.0 1.4 %collective-permute-start.4 = (f32[16,384]{1,0:T(8,128)S(1)}, f32[16,384]{1,0:T(8,128)S(1)}, u32[]{:S(2)}, u32[]{:S(2)}) collective-permute-start(f32[16,384]{1,0:T(8,128)S(1)} %get-tuple-element.41), channel_id=1, source_target_pairs={{0,8},{8,0},{16,24},{24,16},{1,9},{9,1},{17,25},{25,17},{2,10},{10... | collective-permute-start | bytes 73736 | tf_op jit(solution)/shard_map/ppermute | solution.py:574
  16.6 1.1 %collective-permute-done.4.ra_ref = f32[16,384]{1,0:T(8,128)S(1)} collective-permute-done((f32[16,384]{1,0:T(8,128)S(1)}, f32[16,384]{1,0:T(8,128)S(1)}, u32[]{:S(2)}, u32[]{:S(2)}) %collective-permute-start.4) | collective-permute-done | bytes 24608 | tf_op jit(solution)/shard_map/ppermute | solution.py:574
  17.8 2.2 %collective-permute-done.5.rb_ref = f32[16,384]{1,0:T(8,128)S(1)} collective-permute-done((f32[16,384]{1,0:T(8,128)S(1)}, f32[16,384]{1,0:T(8,128)S(1)}, u32[]{:S(2)}, u32[]{:S(2)}) %collective-permute-start.5) | collective-permute-done | bytes 24608 | tf_op jit(solution)/shard_map/ppermute | solution.py:574
  20.0 3.7 %collective-permute-start.6 = (f32[8,768]{1,0:T(8,128)S(1)}, f32[8,768]{1,0:T(8,128)S(1)}, u32[]{:S(2)}, u32[]{:S(2)}) collective-permute-start(f32[8,768]{1,0:T(8,128)S(1)} %get-tuple-element.44), channel_id=1, source_target_pairs={{0,1},{1,0},{2,3},{3,2},{4,5},{5,4},{6,7},{7,6},{8,9},{9,8},{10,11... | collective-permute-start | bytes 73736 | tf_op jit(solution)/shard_map/ppermute | solution.py:574
  24.5 2.4 %collective-permute-done.7.rb_ref = f32[8,768]{1,0:T(8,128)S(1)} collective-permute-done((f32[8,768]{1,0:T(8,128)S(1)}, f32[8,768]{1,0:T(8,128)S(1)}, u32[]{:S(2)}, u32[]{:S(2)}) %collective-permute-start.7) | collective-permute-done | bytes 24608 | tf_op jit(solution)/shard_map/ppermute | solution.py:574
  26.9 2.9 %apply.1 = (f32[16,768]{1,0:T(8,128)S(1)}, f32[16,384]{1,0:T(8,128)S(1)}, f32[16,384]{1,0:T(8,128)S(1)}, f32[8,384]{1,0:T(8,128)S(1)}, f32[8,128]{1,0:T(8,128)S(1)}) custom-call(f32[16,768]{1,0:T(8,128)S(1)} %get-tuple-element.43.p_ref, f32[8,768]{1,0:T(8,128)S(1)} %collective-permute-done.6.ra_ref, f32[8,768]{1,0:T(8,128)S(1)} %collective-permute-done.7.rb_ref, ...), custom_call_target="tpu_custom_call" | custom-call | tf_op jit(solution)/shard_map/apply/pallas_call | solution.py:585
  30.2 1.2 %collective-permute-start.9 = (f32[16,384]{1,0:T(8,128)S(1)}, f32[16,384]{1,0:T(8,128)S(1)}, u32[]{:S(2)}, u32[]{:S(2)}) collective-permute-start(f32[16,384]{1,0:T(8,128)S(1)} %get-tuple-element.50), channel_id=1, source_target_pairs={{0,24},{8,16},{16,8},{24,0},{1,25},{9,17},{17,9},{25,1},{2,26},{10... | collective-permute-start | bytes 73736 | tf_op jit(solution)/shard_map/ppermute | solution.py:574
  31.3 1.3 %collective-permute-done.8.ra_ref = f32[16,384]{1,0:T(8,128)S(1)} collective-permute-done((f32[16,384]{1,0:T(8,128)S(1)}, f32[16,384]{1,0:T(8,128)S(1)}, u32[]{:S(2)}, u32[]{:S(2)}) %collective-permute-start.8) | collective-permute-done | bytes 24608 | tf_op jit(solution)/shard_map/ppermute | solution.py:574
  32.6 1.1 %collective-permute-done.9.rb_ref = f32[16,384]{1,0:T(8,128)S(1)} collective-permute-done((f32[16,384]{1,0:T(8,128)S(1)}, f32[16,384]{1,0:T(8,128)S(1)}, u32[]{:S(2)}, u32[]{:S(2)}) %collective-permute-start.9) | collective-permute-done | bytes 24608 | tf_op jit(solution)/shard_map/ppermute | solution.py:574
  33.8 3.5 %collective-permute-start.10 = (f32[8,768]{1,0:T(8,128)S(1)}, f32[8,768]{1,0:T(8,128)S(1)}, u32[]{:S(2)}, u32[]{:S(2)}) collective-permute-start(f32[8,768]{1,0:T(8,128)S(1)} %get-tuple-element.52), channel_id=1, source_target_pairs={{0,1},{1,0},{2,3},{3,2},{4,5},{5,4},{6,7},{7,6},{8,9},{9,8},{10,11... | collective-permute-start | bytes 73736 | tf_op jit(solution)/shard_map/ppermute | solution.py:574
  37.3 0.8 %collective-permute-done.10.ra_ref = f32[8,768]{1,0:T(8,128)S(1)} collective-permute-done((f32[8,768]{1,0:T(8,128)S(1)}, f32[8,768]{1,0:T(8,128)S(1)}, u32[]{:S(2)}, u32[]{:S(2)}) %collective-permute-start.10) | collective-permute-done | bytes 24608 | tf_op jit(solution)/shard_map/ppermute | solution.py:574
  38.2 2.4 %collective-permute-done.11.rb_ref = f32[8,768]{1,0:T(8,128)S(1)} collective-permute-done((f32[8,768]{1,0:T(8,128)S(1)}, f32[8,768]{1,0:T(8,128)S(1)}, u32[]{:S(2)}, u32[]{:S(2)}) %collective-permute-start.11) | collective-permute-done | bytes 24608 | tf_op jit(solution)/shard_map/ppermute | solution.py:574
  40.6 3.1 %last.1 = (f32[8,384]{1,0:T(8,128)S(1)}, f32[8,384]{1,0:T(8,128)S(1)}, f32[32,8,256]{2,1,0:T(8,128)S(1)}) custom-call(f32[16,768]{1,0:T(8,128)S(1)} %get-tuple-element.51.p_ref, f32[8,768]{1,0:T(8,128)S(1)} %collective-permute-done.10.ra_ref, f32[8,768]{1,0:T(8,128)S(1)} %collective-permute-done.11.rb_ref, ...), custom_call_target="tpu_custom_call" | custom-call | tf_op jit(solution)/shard_map/last/pallas_call | solution.py:585
  43.6 14.3 %all_to_all.5.got_ref = f32[32,8,256]{2,1,0:T(8,128)S(1)} all-to-all(f32[32,8,256]{2,1,0:T(8,128)S(1)} %get-tuple-element.57), channel_id=1, replica_groups=mesh['gz'=4,'gy'=8] {'gz','gy'}, dimensions={0} | all-to-all | bytes 524288 | tf_op jit(solution)/shard_map/all_to_all | solution.py:667
  58.0 1.0 %finish.1 = (f32[3,4,8,32]{3,2,1,0:T(8,128)}, f32[3,4,8,32]{3,2,1,0:T(8,128)}) custom-call(f32[8,384]{1,0:T(8,128)S(1)} %get-tuple-element.47.v0_ref, f32[8,384]{1,0:T(8,128)S(1)} %get-tuple-element.55.v1_ref, f32[8,384]{1,0:T(8,128)S(1)} %get-tuple-element.56.part_ref, f32[32,8,256]{2,1,0:T(8,128)S(1)} %all_to_all.5.got_ref), custom_call_target="tpu_custom_call" | custom-call | tf_op jit(solution)/shard_map/finish/pallas_call | solution.py:585
  (27 shorter events, 1.6 us)
Async XLA Ops:
  0.6 4.8 %copy-start.1 = (f32[32,64,256]{2,1,0:T(8,128)S(1)}, f32[32,64,256]{2,1,0:T(8,128)}, u32[]{:S(2)}) copy-start(f32[32,64,256]{2,1,0:T(8,128)} %m_ref.5) | copy-start | bytes 6291460
  0.6 4.8 %copy-start = (f32[32,64,256]{2,1,0:T(8,128)S(1)}, f32[32,64,256]{2,1,0:T(8,128)}, u32[]{:S(2)}) copy-start(f32[32,64,256]{2,1,0:T(8,128)} %f_ref.5) | copy-start | bytes 6291460
  2.1 12.0 %collective-permute-start.2 = (f32[3,64,256]{2,1,0:T(8,128)S(1)}, f32[3,64,256]{2,1,0:T(8,128)S(1)}, u32[]{:S(2)}, u32[]{:S(2)}) collective-permute-start(f32[3,64,256]{2,1,0:T(8,128)S(1)} %get-tuple-element.37), channel_id=1, source_target_pairs={{0,8},{8,0},{16,24},{24,16},{1,9},{9,1},{17,25},{25,17},{2,10},{10... | collective-permute-start | bytes 589832 | tf_op jit(solution)/shard_map/ppermute | solution.py:574
  4.2 4.0 %copy-start.4 = (bf16[512,256]{1,0:T(8,128)(2,1)S(1)}, bf16[512,256]{1,0:T(8,128)(2,1)}, u32[]{:S(2)}) copy-start(bf16[512,256]{1,0:T(8,128)(2,1)} %constant.12.clone.dx_ref) | copy-start | bytes 786436
  4.2 9.9 %collective-permute-start.3 = (f32[3,64,256]{2,1,0:T(8,128)S(1)}, f32[3,64,256]{2,1,0:T(8,128)S(1)}, u32[]{:S(2)}, u32[]{:S(2)}) collective-permute-start(f32[3,64,256]{2,1,0:T(8,128)S(1)} %get-tuple-element.38), channel_id=1, source_target_pairs={{0,24},{8,16},{16,8},{24,0},{1,25},{9,17},{17,9},{25,1},{2,26},{10... | collective-permute-start | bytes 589832 | tf_op jit(solution)/shard_map/ppermute | solution.py:574
  5.6 4.2 %collective-permute-start = (f32[3,32,256]{2,1,0:T(8,128)S(1)}, f32[3,32,256]{2,1,0:T(8,128)S(1)}, u32[]{:S(2)}, u32[]{:S(2)}) collective-permute-start(f32[3,32,256]{2,1,0:T(8,128)S(1)} %get-tuple-element.34), channel_id=1, source_target_pairs={{0,1},{1,0},{2,3},{3,2},{4,5},{5,4},{6,7},{7,6},{8,9},{9,8},{10,11... | collective-permute-start | bytes 294920 | tf_op jit(solution)/shard_map/ppermute | solution.py:574
  6.9 4.0 %copy-start.2 = (bf16[8,256,256]{2,1,0:T(8,128)(2,1)S(1)}, bf16[8,256,256]{2,1,0:T(8,128)(2,1)}, u32[]{:S(2)}) copy-start(bf16[8,256,256]{2,1,0:T(8,128)(2,1)} %constant.17.clone.re_ref) | copy-start | bytes 3145732
  6.9 4.0 %copy-start.7 = (bf16[64,160]{1,0:T(8,128)(2,1)S(1)}, bf16[64,160]{1,0:T(8,128)(2,1)}, u32[]{:S(2)}) copy-start(bf16[64,160]{1,0:T(8,128)(2,1)} %constant.13.clone.dy_ref) | copy-start | bytes 61444
  6.9 4.0 %collective-permute-start.1 = (f32[3,32,256]{2,1,0:T(8,128)S(1)}, f32[3,32,256]{2,1,0:T(8,128)S(1)}, u32[]{:S(2)}, u32[]{:S(2)}) collective-permute-start(f32[3,32,256]{2,1,0:T(8,128)S(1)} %get-tuple-element.35), channel_id=1, source_target_pairs={{0,7},{1,2},{2,1},{3,4},{4,3},{5,6},{6,5},{7,0},{8,15},{9,10},{10,... | collective-permute-start | bytes 294920 | tf_op jit(solution)/shard_map/ppermute | solution.py:574
  10.9 3.2 %copy-start.5 = (bf16[16,192]{1,0:T(8,128)(2,1)S(1)}, bf16[16,192]{1,0:T(8,128)(2,1)}, u32[]{:S(2)}) copy-start(bf16[16,192]{1,0:T(8,128)(2,1)} %constant.16.clone.ye_ref) | copy-start | bytes 18436
  14.1 12.8 %copy-start.3 = (bf16[8,256,256]{2,1,0:T(8,128)(2,1)S(1)}, bf16[8,256,256]{2,1,0:T(8,128)(2,1)}, u32[]{:S(2)}) copy-start(bf16[8,256,256]{2,1,0:T(8,128)(2,1)} %constant.15.clone.rd_ref) | copy-start | bytes 3145732
  14.1 12.8 %copy-start.6 = (bf16[64,48]{1,0:T(8,128)(2,1)S(1)}, bf16[64,48]{1,0:T(8,128)(2,1)}, u32[]{:S(2)}) copy-start(bf16[64,48]{1,0:T(8,128)(2,1)} %constant.14.clone.yd_ref) | copy-start | bytes 18436
  15.0 2.7 %collective-permute-start.4 = (f32[16,384]{1,0:T(8,128)S(1)}, f32[16,384]{1,0:T(8,128)S(1)}, u32[]{:S(2)}, u32[]{:S(2)}) collective-permute-start(f32[16,384]{1,0:T(8,128)S(1)} %get-tuple-element.41), channel_id=1, source_target_pairs={{0,8},{8,0},{16,24},{24,16},{1,9},{9,1},{17,25},{25,17},{2,10},{10... | collective-permute-start | bytes 73736 | tf_op jit(solution)/shard_map/ppermute | solution.py:574
  16.4 3.6 %collective-permute-start.5 = (f32[16,384]{1,0:T(8,128)S(1)}, f32[16,384]{1,0:T(8,128)S(1)}, u32[]{:S(2)}, u32[]{:S(2)}) collective-permute-start(f32[16,384]{1,0:T(8,128)S(1)} %get-tuple-element.42), channel_id=1, source_target_pairs={{0,24},{8,16},{16,8},{24,0},{1,25},{9,17},{17,9},{25,1},{2,26},{10... | collective-permute-start | bytes 73736 | tf_op jit(solution)/shard_map/ppermute | solution.py:574
  20.0 4.5 %collective-permute-start.6 = (f32[8,768]{1,0:T(8,128)S(1)}, f32[8,768]{1,0:T(8,128)S(1)}, u32[]{:S(2)}, u32[]{:S(2)}) collective-permute-start(f32[8,768]{1,0:T(8,128)S(1)} %get-tuple-element.44), channel_id=1, source_target_pairs={{0,1},{1,0},{2,3},{3,2},{4,5},{5,4},{6,7},{7,6},{8,9},{9,8},{10,11... | collective-permute-start | bytes 73736 | tf_op jit(solution)/shard_map/ppermute | solution.py:574
  23.7 3.3 %collective-permute-start.7 = (f32[8,768]{1,0:T(8,128)S(1)}, f32[8,768]{1,0:T(8,128)S(1)}, u32[]{:S(2)}, u32[]{:S(2)}) collective-permute-start(f32[8,768]{1,0:T(8,128)S(1)} %get-tuple-element.45), channel_id=1, source_target_pairs={{0,7},{1,2},{2,1},{3,4},{4,3},{5,6},{6,5},{7,0},{8,15},{9,10},{10,... | collective-permute-start | bytes 73736 | tf_op jit(solution)/shard_map/ppermute | solution.py:574
  29.9 2.7 %collective-permute-start.8 = (f32[16,384]{1,0:T(8,128)S(1)}, f32[16,384]{1,0:T(8,128)S(1)}, u32[]{:S(2)}, u32[]{:S(2)}) collective-permute-start(f32[16,384]{1,0:T(8,128)S(1)} %get-tuple-element.49), channel_id=1, source_target_pairs={{0,8},{8,0},{16,24},{24,16},{1,9},{9,1},{17,25},{25,17},{2,10},{10... | collective-permute-start | bytes 73736 | tf_op jit(solution)/shard_map/ppermute | solution.py:574
  30.2 3.6 %collective-permute-start.9 = (f32[16,384]{1,0:T(8,128)S(1)}, f32[16,384]{1,0:T(8,128)S(1)}, u32[]{:S(2)}, u32[]{:S(2)}) collective-permute-start(f32[16,384]{1,0:T(8,128)S(1)} %get-tuple-element.50), channel_id=1, source_target_pairs={{0,24},{8,16},{16,8},{24,0},{1,25},{9,17},{17,9},{25,1},{2,26},{10... | collective-permute-start | bytes 73736 | tf_op jit(solution)/shard_map/ppermute | solution.py:574
  33.8 4.4 %collective-permute-start.10 = (f32[8,768]{1,0:T(8,128)S(1)}, f32[8,768]{1,0:T(8,128)S(1)}, u32[]{:S(2)}, u32[]{:S(2)}) collective-permute-start(f32[8,768]{1,0:T(8,128)S(1)} %get-tuple-element.52), channel_id=1, source_target_pairs={{0,1},{1,0},{2,3},{3,2},{4,5},{5,4},{6,7},{7,6},{8,9},{9,8},{10,11... | collective-permute-start | bytes 73736 | tf_op jit(solution)/shard_map/ppermute | solution.py:574
  37.3 3.3 %collective-permute-start.11 = (f32[8,768]{1,0:T(8,128)S(1)}, f32[8,768]{1,0:T(8,128)S(1)}, u32[]{:S(2)}, u32[]{:S(2)}) collective-permute-start(f32[8,768]{1,0:T(8,128)S(1)} %get-tuple-element.53), channel_id=1, source_target_pairs={{0,7},{1,2},{2,1},{3,4},{4,3},{5,6},{6,5},{7,0},{8,15},{9,10},{10,... | collective-permute-start | bytes 73736 | tf_op jit(solution)/shard_map/ppermute | solution.py:574

commit v3 on v2

--- a/solution.py
+++ b/solution.py
@@ -37,7 +37,8 @@
         self.own = self.cz * self.cx
         self.cells = 3 * self.cz * self.sy
         self.pair = 2 * self.cx
-        self.block = round_up(3 * self.pair + 1, LANES)
+        assert 2 * 3 * self.pair == 3 * LANES and self.own == LANES
+        self.block = self.cy + self.cy // 2 + 1
         assert self.tap % LANES == 0 and self.own % LANES == 0
         assert self.cy % 8 == 0 and self.bp == self.cy + 8 and self.cz > 1
 
@@ -268,7 +269,6 @@
         h_ref[k] = jnp.where(below, down, 0.0)
         h_ref[REACH + k] = jnp.where(above, up, 0.0)
     part = 3 * s.sy
-    acc_ref[...] = acc_in[...]
     for side, zc in ((0, 0), (1, s.cz - 1)):
         first = 0 if side == 0 else s.sz - REACH
         for j in range(REACH):
@@ -296,15 +296,15 @@
                 lhs.append(ref[row : row + part, :])
                 rhs.append(weights)
         at = slice(zc * part, (zc + 1) * part)
-        acc_ref[at, :] += dot(jnp.concatenate(lhs, 1), jnp.concatenate(rhs, 0))
-    encode_y(s, acc_ref, ye_ref, p_ref)
+        acc_ref[at, :] = acc_in[at, :] + dot(jnp.concatenate(lhs, 1), jnp.concatenate(rhs, 0))
+    encode_y(s, [acc_ref] + [acc_in] * (s.cz - 2) + [acc_ref], ye_ref, p_ref)
     send_faces(s, p_ref, za_ref, zb_ref)
 
 
-def encode_y(s, acc_ref, ye_ref, p_ref):
+def encode_y(s, acc_refs, ye_ref, p_ref):
     columns = []
     for i in range(3 * s.cz):
-        both = acc_ref[i * s.sy : (i + 1) * s.sy, :]
+        both = acc_refs[i // 3][i * s.sy : (i + 1) * s.sy, :]
         columns.append(both[:, : s.tap] + both[:, s.tap :])
     high, low = split(jnp.concatenate(columns, 1))
     out = dot(ye_ref[...], jnp.concatenate([high, low, high], 0))
@@ -326,8 +326,10 @@
         down = p_ref[:, low : low + s.face]
         up = p_ref[:, low + s.own : low + s.own + s.face]
         at = slice(c * s.face, (c + 1) * s.face)
-        za_ref[:, at] = jnp.where(even, up, down)
-        zb_ref[:, at] = jnp.where(even, down, up)
+        to_a, to_b = jnp.where(even, up, down), jnp.where(even, down, up)
+        for i in range(za_ref.shape[0]):
+            za_ref[i, :, at] = to_a[4 * i : 4 * i + 4]
+            zb_ref[i, :, at] = to_b[4 * i : 4 * i + 4]
 
 
 def fold_z_kernel(s, p_ref, ra_ref, rb_ref, o_ref, ya_ref, yb_ref):
@@ -336,17 +338,19 @@
     first = jnp.where(below, 0, 1)
     last = jnp.where(above, s.cz + 2, s.cz)
     inside = (layer >= first) & (layer <= last)
-    shared = iota((s.bp, s.face), 1) < s.used
+    shared = iota((4, s.face), 1) < s.used
     for c in range(3):
         low = c * s.per
+        high = low + s.own
         at = slice(c * s.face, (c + 1) * s.face)
-        up, down = from_sides(even, ra_ref[:, at], rb_ref[:, at])
         o_ref[:, low : low + s.per] = jnp.where(inside, p_ref[:, low : low + s.per], 0.0)
-        o_ref[:, low : low + s.face] += jnp.where(shared & below, down, 0.0)
-        high = low + s.own
-        o_ref[:, high : high + s.face] += jnp.where(shared & above, up, 0.0)
+        for i in range(ra_ref.shape[0]):
+            rows = slice(4 * i, 4 * i + 4)
+            up, down = from_sides(even, ra_ref[i, :, at], rb_ref[i, :, at])
+            o_ref[rows, low : low + s.face] += jnp.where(shared & below, down, 0.0)
+            o_ref[rows, high : high + s.face] += jnp.where(shared & above, up, 0.0)
     even = place("gy")[2]
-    down, up = o_ref[:8, :], o_ref[s.cy : s.cy + 8, :]
+    down, up = o_ref[:4, :], o_ref[s.cy : s.cy + 4, :]
     ya_ref[...] = jnp.where(even, up, down)
     yb_ref[...] = jnp.where(even, down, up)
 
@@ -357,9 +361,9 @@
     row = iota((s.bp, s.wide), 0)
     inside = (row >= jnp.where(below, 0, 1)) & (row <= jnp.where(above, s.cy + 2, s.cy))
     v_ref[...] = jnp.where(inside, p_ref[...], 0.0)
-    shared = iota((8, s.wide), 0) < REACH
-    v_ref[:8, :] += jnp.where(shared & below, down, 0.0)
-    v_ref[s.cy : s.cy + 8, :] += jnp.where(shared & above, up, 0.0)
+    shared = iota((4, s.wide), 0) < REACH
+    v_ref[:4, :] += jnp.where(shared & below, down, 0.0)
+    v_ref[s.cy : s.cy + 4, :] += jnp.where(shared & above, up, 0.0)
 
 
 def own_part(s, v_ref, out_ref):
@@ -427,10 +431,10 @@
 
 
 def moments(sums, start):
-    row = iota((8, LANES), 0)
-    out = jnp.zeros((8, LANES), F32)
+    lane = iota((1, LANES), 1)
+    out = jnp.zeros((1, LANES), F32)
     for k, value in enumerate(sums):
-        out = jnp.where(row == start + k, value, out)
+        out = jnp.where(lane == start + k, value, out)
     return out
 
 
@@ -443,7 +447,7 @@
     square = operate(
         s, v_ref, yd_ref, rd_ref, re_ref, (gi_ref, ge_ref, gy_ref, gx_ref), scratch
     )
-    encode_y(s, scratch[-1], ye_ref, o_ref)
+    encode_y(s, [scratch[-1]] * s.cz, ye_ref, o_ref)
     send_faces(s, o_ref, za_ref, zb_ref)
     own = own_ref[...]
     sum_ref[...] = moments([total_of(own * own), total_of(square)], 0)
@@ -454,9 +458,10 @@
 
 def neighbour(dz, dy):
     nz, ny = lax.axis_size("gz"), lax.axis_size("gy")
-    tz, ty = lax.axis_index("gz") + dz, lax.axis_index("gy") + dy
+    iz, iy = lax.axis_index("gz"), lax.axis_index("gy")
+    tz, ty = iz + dz, iy + dy
     ok = (tz >= 0) & (tz < nz) & (ty >= 0) & (ty < ny)
-    return ok, tz * ny + ty
+    return ok, jnp.where(ok, tz * ny + ty, iz * ny + iy)
 
 
 def last_kernel(
@@ -471,84 +476,80 @@
     )
     own = own_ref[...]
     sums = m_ref[...] + moments([total_of(own * own), total_of(square)], 2)
-    encode_y(s, scratch[-1], ye_ref, o_ref)
+    encode_y(s, [scratch[-1]] * s.cz, ye_ref, o_ref)
     own_part(s, o_ref, part_ref)
-    edge = s.block - LANES
-    free = iota((8, LANES), 1) >= 3 * s.pair - edge
-    base = jnp.where(free, sums, 0.0)
     for d in range(send_ref.shape[0]):
-        send_ref[d, 0:8, edge:] = base
-    lane = iota((s.bp, s.block), 1)
+        send_ref[d, s.block - 1, :, :] = sums
+    lane = iota((s.bp, 2 * LANES), 1)
     t_ref[...] = jnp.zeros_like(t_ref)
     for i, dz in enumerate((-1, 1)):
         layer = 0 if dz < 0 else s.cz + 1
         width = s.cx if dz < 0 else s.pair
-        total = jnp.zeros((s.bp, s.block), F32)
+        total = jnp.zeros((s.bp, 2 * LANES), F32)
         for c in range(3):
             low = c * s.pair
             lanes = roll(o_ref[:, c * s.per : (c + 1) * s.per], low - layer * s.cx)
-            total = jnp.where((lane >= low) & (lane < low + width), lanes[:, : s.block], total)
+            total = jnp.where((lane >= low) & (lane < low + width), lanes[:, : 2 * LANES], total)
         t_ref[i, 8 : 8 + s.bp, :] = total
     for c in range(3):
         lanes = roll(o_ref[:, c * s.per : (c + 1) * s.per], -s.cx)
         y_ref[:, c * s.own : (c + 1) * s.own] = lanes[:, : s.own]
+    half = s.cy // 2
+    low_half = iota((half, LANES), 1) < LANES // 2
     for dz, dy in NEIGHBOURS:
-        ok, target = neighbour(dz, dy)
-
-        @pl.when(ok)
-        def _(dz=dz, dy=dy, target=target):
-            if dz:
-                start = {-1: 9 - s.cy, 0: 9, 1: 9 + s.cy}[dy]
-                rows = t_ref[(dz + 1) // 2, start : start + 8, :]
-                send_ref[target, 0:8, :edge] = rows[:, :edge]
-                send_ref[target, 0:8, edge:] = jnp.where(free, sums, rows[:, edge:])
-            else:
-                for c in range(3):
-                    lanes = slice(c * s.own, (c + 1) * s.own)
-                    if dy > 0:
-                        send_ref[target, 2 * c : 2 * c + 2, : s.own] = y_ref[
-                            s.cy + 1 : s.cy + 3, lanes
-                        ]
-                    else:
-                        send_ref[target, c : c + 1, : s.own] = y_ref[0:1, lanes]
-
-
-def finish_kernel(s, v0_ref, v1_ref, part_ref, got_ref, u_ref, r_ref, v_ref, t_ref):
+        _, target = neighbour(dz, dy)
+        if dz:
+            start = 9 + dy * s.cy
+            side = (dz + 1) // 2
+            send_ref[target, 0 : s.cy, 0, :] = t_ref[side, start : start + s.cy, :LANES]
+            near = t_ref[side, start : start + half, LANES:]
+            far = t_ref[side, start + half : start + s.cy, LANES:]
+            send_ref[target, s.cy : s.cy + half, 0, :] = jnp.where(
+                low_half, near, roll(far, LANES // 2)
+            )
+        else:
+            for c in range(3):
+                lanes = slice(c * s.own, (c + 1) * s.own)
+                if dy > 0:
+                    send_ref[target, 2 * c : 2 * c + 2, 0, :] = y_ref[s.cy + 1 : s.cy + 3, lanes]
+                else:
+                    send_ref[target, c, :, :] = y_ref[0:1, lanes]
+
+
+def finish_kernel(s, v0_ref, v1_ref, part_ref, got_ref, u_ref, r_ref, v_ref, t_ref, w_ref):
     v_ref[...] = part_ref[...]
+    half = s.cy // 2
     for i, dz in enumerate((-1, 1)):
-        t_ref[i] = jnp.zeros((8, s.block), F32)
+        first = jnp.zeros((s.cy, LANES), F32)
+        rest = jnp.zeros((half, LANES), F32)
         for dy in (-1, 0, 1):
             ok, source = neighbour(dz, dy)
-
-            @pl.when(ok)
-            def _(i=i, source=source):
-                t_ref[i] += got_ref[source]
-
-    lane = iota((8, s.own), 1)
+            first += jnp.where(ok, got_ref[source, 0 : s.cy, 0, :], 0.0)
+            rest += jnp.where(ok, got_ref[source, s.cy : s.cy + half, 0, :], 0.0)
+        t_ref[i] = first
+        w_ref[i, 0:half, :] = rest
+        w_ref[i, half:, :] = roll(rest, LANES // 2)
+
+    lane = iota((s.cy, s.own), 1)
     for c in range(3):
-        low = c * s.pair
         lanes = slice(c * s.own, (c + 1) * s.own)
-        first = roll(t_ref[0], -low)[:, : s.own]
-        last = roll(t_ref[1], (s.cz - 1) * s.cx - low)[:, : s.own]
-        v_ref[:, lanes] += jnp.where(lane < s.pair, first, 0.0)
+        first, last = (w_ref[0], w_ref[1]) if c == 2 else (t_ref[0], t_ref[1])
+        low = c % 2 * s.pair
+        v_ref[:, lanes] += jnp.where(lane < s.pair, roll(first, -low), 0.0)
+        last = roll(last, (s.cz - 1) * s.cx - low)
         v_ref[:, lanes] += jnp.where(lane >= s.own - s.cx, last, 0.0)
     for dy in (-1, 1):
         ok, source = neighbour(0, dy)
-
-        @pl.when(ok)
-        def _(dy=dy, source=source):
-            for c in range(3):
-                lanes = slice(c * s.own, (c + 1) * s.own)
-                if dy < 0:
-                    v_ref[0:2, lanes] += got_ref[source, 2 * c : 2 * c + 2, : s.own]
-                else:
-                    v_ref[s.cy - 1 : s.cy, lanes] += got_ref[source, c : c + 1, : s.own]
-
-    edge = s.block - LANES
-    tot = got_ref[0, :, edge:]
-    for d in range(1, got_ref.shape[0]):
-        tot = tot + got_ref[d, :, edge:]
-    m0, m1, m2, m3 = (tot[k : k + 1, LANES - 1 : LANES] for k in range(4))
+        for c in range(3):
+            lanes = slice(c * s.own, (c + 1) * s.own)
+            if dy < 0:
+                value = got_ref[source, 2 * c : 2 * c + 2, 0, :]
+                v_ref[0:2, lanes] += jnp.where(ok, value, 0.0)
+            else:
+                v_ref[s.cy - 1 : s.cy, lanes] += jnp.where(ok, got_ref[source, c, :, :], 0.0)
+
+    tot = jnp.sum(got_ref[:, s.block - 1, 0, :], axis=0, keepdims=True)
+    m0, m1, m2, m3 = (tot[:, k : k + 1] for k in range(4))
     v0, v1, v2 = v0_ref[...], v1_ref[...], v_ref[...]
     rho = m1 / m0
     a0 = 1.0 / (rho + DAMPING)
@@ -628,7 +629,7 @@
         [(s.sz, 16, s.nx), half, half, half, half],
         total, diff, gx, gz_inner, ya, yb, dy, re,
     )
-    grid, zface, yface = (s.bp, s.wide), (s.bp, 3 * s.face), (8, s.wide)
+    grid, zface, yface = (s.bp, s.wide), (round_up(s.nb, 4) // 4, 4, 3 * s.face), (4, s.wide)
     few = ((2 * REACH * 3 * s.sy, s.nx), BF16)
     gz_edge, grid0, za, zb = call(
         part(edge_kernel, s),
@@ -653,22 +654,22 @@
     grid1, za, zb, v0, sums = call(
         part(apply_kernel, s),
         "apply",
-        [grid, zface, zface, own, (8, LANES)],
+        [grid, zface, zface, own, (1, LANES)],
         [grid, *work],
         *fold_z(grid0, za, zb), *grads, yd, rd, ye, re,
     )
     v1, mine, send = call(
         part(last_kernel, s),
         "last",
-        [own, own, (devices, s.cy, s.block)],
-        [grid, grid, (2, 16 + s.bp, s.block), (s.bp, 3 * s.own), *work],
+        [own, own, (devices, s.block, 1, LANES)],
+        [grid, grid, (2, 16 + s.bp, 2 * LANES), (s.bp, 3 * s.own), *work],
         *fold_z(grid1, za, zb), *grads, sums, yd, rd, ye, re,
     )
     got = lax.all_to_all(send, ("gz", "gy"), 0, 0)
     out = (3, s.cz, s.cy, s.cx)
     return tuple(
         call(
-            part(finish_kernel, s), "finish", [out, out], [own, (2, s.cy, s.block)], v0, v1, mine, got
+            part(finish_kernel, s), "finish", [out, out], [own, (2, s.cy, LANES), (2, s.cy, LANES)], v0, v1, mine, got
         )
     )
 

time: 59.1 us -> 57.8 us (0.978)
  blocking collectives: 14.3 us -> 13.5 us
    all_to_all x1, blocking collectives: 14.3 us -> 13.5 us  [shards(): got = lax.all_to_all(send, ('gz', 'gy'), 0, 0)]
  transfers between devices with their start and end apart: 12 -> 12, of which waited for: 9 -> 9; matrix products, arithmetic and copies ran while one was open for 0% -> 0% of each run, Pallas kernels for 8% -> 9%
where the time goes in v3:
time: 57.8 us; the launch traced here: 57.6 us
  starting transfers between devices  16.3 us (28%)
  Pallas kernels  14.3 us (25%)
  blocking collectives  13.5 us (23%)
  waiting for transfers between devices  12.7 us (22%)
  between operations  0.75 us (1%)
    ppermute x12, starting transfers between devices, swap(): return (lax.ppermute(value_a, axis, even), lax.ppermute(value_b, axis, odd))  16.3 us
    pallas_call x10, Pallas kernels, call(): pl.pallas_call(kernel, out_shape=shapes, in_specs=[HBM] * far + [VMEM] *...  14.3 us
    all_to_all x1, blocking collectives, shards(): got = lax.all_to_all(send, ('gz', 'gy'), 0, 0)  13.5 us
    ppermute x12, waiting for transfers between devices, swap(): return (lax.ppermute(value_a, axis, even), lax.ppermute(value_b, axis, odd))  12.7 us
  transfers between devices with their start and end apart: 12, of which 9 were waited for; matrix products, arithmetic and copies ran while one was open for 0% of the time, Pallas kernels for 9%

profile of v3, /device:TPU:1, one launch (start us, length us, event | category | flops | bytes accessed | tf_op | source)
XLA Modules:
  0.0 57.6 jit_solution(1959518696361280389)
XLA Ops:
  0.6 1.4 %faces_z.1 = (f32[3,64,256]{2,1,0:T(8,128)S(1)}, f32[3,64,256]{2,1,0:T(8,128)S(1)}) custom-call(f32[32,64,256]{2,1,0:T(8,128)} %f_ref.5, f32[32,64,256]{2,1,0:T(8,128)} %m_ref.5), custom_call_target="tpu_custom_call" | custom-call | tf_op jit(solution)/shard_map/faces_z/pallas_call | solution.py:586
  2.1 2.1 %collective-permute-start.2 = (f32[3,64,256]{2,1,0:T(8,128)S(1)}, f32[3,64,256]{2,1,0:T(8,128)S(1)}, u32[]{:S(2)}, u32[]{:S(2)}) collective-permute-start(f32[3,64,256]{2,1,0:T(8,128)S(1)} %get-tuple-element.37), channel_id=1, source_target_pairs={{0,8},{8,0},{16,24},{24,16},{1,9},{9,1},{17,25},{25,17},{2,10},{10... | collective-permute-start | bytes 589832 | tf_op jit(solution)/shard_map/ppermute | solution.py:575
  4.2 1.2 %collective-permute-start.3 = (f32[3,64,256]{2,1,0:T(8,128)S(1)}, f32[3,64,256]{2,1,0:T(8,128)S(1)}, u32[]{:S(2)}, u32[]{:S(2)}) collective-permute-start(f32[3,64,256]{2,1,0:T(8,128)S(1)} %get-tuple-element.38), channel_id=1, source_target_pairs={{0,24},{8,16},{16,8},{24,0},{1,25},{9,17},{17,9},{25,1},{2,26},{10... | collective-permute-start | bytes 589832 | tf_op jit(solution)/shard_map/ppermute | solution.py:575
  5.6 1.3 %collective-permute-start = (f32[3,32,256]{2,1,0:T(8,128)S(1)}, f32[3,32,256]{2,1,0:T(8,128)S(1)}, u32[]{:S(2)}, u32[]{:S(2)}) collective-permute-start(f32[3,32,256]{2,1,0:T(8,128)S(1)} %get-tuple-element.34), channel_id=1, source_target_pairs={{0,1},{1,0},{2,3},{3,2},{4,5},{5,4},{6,7},{7,6},{8,9},{9,8},{10,11... | collective-permute-start | bytes 294920 | tf_op jit(solution)/shard_map/ppermute | solution.py:575
  6.9 1.3 %collective-permute-start.1 = (f32[3,32,256]{2,1,0:T(8,128)S(1)}, f32[3,32,256]{2,1,0:T(8,128)S(1)}, u32[]{:S(2)}, u32[]{:S(2)}) collective-permute-start(f32[3,32,256]{2,1,0:T(8,128)S(1)} %get-tuple-element.35), channel_id=1, source_target_pairs={{0,7},{1,2},{2,1},{3,4},{4,3},{5,6},{6,5},{7,0},{8,15},{9,10},{10,... | collective-permute-start | bytes 294920 | tf_op jit(solution)/shard_map/ppermute | solution.py:575
  8.1 1.6 %start.1 = (f32[32,64,256]{2,1,0:T(8,128)S(1)}, f32[32,64,256]{2,1,0:T(8,128)S(1)}, f32[32,64,256]{2,1,0:T(8,128)S(1)}, f32[26,64,256]{2,1,0:T(8,128)S(1)}) custom-call(f32[32,64,256]{2,1,0:T(8,128)S(1)} %copy-done, f32[32,64,256]{2,1,0:T(8,128)S(1)} %copy-done.1, bf16[512,256]{1,0:T(8,128)(2,1)S(1)} %copy-done.4), custom_call_target="tpu_custom_call" | custom-call | tf_op jit(solution)/shard_map/start/pallas_call | solution.py:586
  9.8 1.1 %collective-permute-done.1.rb_ref = f32[3,32,256]{2,1,0:T(8,128)S(1)} collective-permute-done((f32[3,32,256]{2,1,0:T(8,128)S(1)}, f32[3,32,256]{2,1,0:T(8,128)S(1)}, u32[]{:S(2)}, u32[]{:S(2)}) %collective-permute-start.1) | collective-permute-done | bytes 98336 | tf_op jit(solution)/shard_map/ppermute | solution.py:575
  10.9 3.2 %inner.1 = (f32[32,64,256]{2,1,0:T(8,128)S(1)}, f32[768,256]{1,0:T(8,128)S(1)}) custom-call(f32[32,64,256]{2,1,0:T(8,128)S(1)} %get-tuple-element.30.sum_ref, f32[32,64,256]{2,1,0:T(8,128)S(1)} %get-tuple-element.31.diff_ref, f32[32,64,256]{2,1,0:T(8,128)S(1)} %get-tuple-element.32.gx_ref, f32[26,64,256]{2,1,0:T(8,128)S(1)} %get-tuple-element.33.gz_ref.gi_ref, ...), custom_call_target="tpu_custom_call" | custom-call | tf_op jit(solution)/shard_map/inner/pallas_call | solution.py:586
  14.1 0.8 %edge.1 = (f32[6,64,256]{2,1,0:T(8,128)S(1)}, f32[16,768]{1,0:T(8,128)S(1)}, f32[3,4,384]{2,1,0:T(4,128)S(1)}, f32[3,4,384]{2,1,0:T(4,128)S(1)}) custom-call(f32[32,64,256]{2,1,0:T(8,128)S(1)} %get-tuple-element.30.sum_ref, f32[32,64,256]{2,1,0:T(8,128)S(1)} %get-tuple-element.31.diff_ref, f32[32,64,256]{2,1,0:T(8,128)S(1)} %get-tuple-element.32.gx_ref, ...), custom_call_target="tpu_custom_call" | custom-call | tf_op jit(solution)/shard_map/edge/pallas_call | solution.py:586
  15.0 1.4 %collective-permute-start.4 = (f32[3,4,384]{2,1,0:T(4,128)S(1)}, f32[3,4,384]{2,1,0:T(4,128)S(1)}, u32[]{:S(2)}, u32[]{:S(2)}) collective-permute-start(f32[3,4,384]{2,1,0:T(4,128)S(1)} %get-tuple-element.41), channel_id=1, source_target_pairs={{0,8},{8,0},{16,24},{24,16},{1,9},{9,1},{17,25},{25,17},{2,10},{10... | collective-permute-start | bytes 55304 | tf_op jit(solution)/shard_map/ppermute | solution.py:575
  16.6 1.1 %collective-permute-done.4.ra_ref = f32[3,4,384]{2,1,0:T(4,128)S(1)} collective-permute-done((f32[3,4,384]{2,1,0:T(4,128)S(1)}, f32[3,4,384]{2,1,0:T(4,128)S(1)}, u32[]{:S(2)}, u32[]{:S(2)}) %collective-permute-start.4) | collective-permute-done | bytes 18464 | tf_op jit(solution)/shard_map/ppermute | solution.py:575
  17.7 2.2 %collective-permute-done.5.rb_ref = f32[3,4,384]{2,1,0:T(4,128)S(1)} collective-permute-done((f32[3,4,384]{2,1,0:T(4,128)S(1)}, f32[3,4,384]{2,1,0:T(4,128)S(1)}, u32[]{:S(2)}, u32[]{:S(2)}) %collective-permute-start.5) | collective-permute-done | bytes 18464 | tf_op jit(solution)/shard_map/ppermute | solution.py:575
  19.9 3.7 %collective-permute-start.6 = (f32[4,768]{1,0:T(4,128)S(1)}, f32[4,768]{1,0:T(4,128)S(1)}, u32[]{:S(2)}, u32[]{:S(2)}) collective-permute-start(f32[4,768]{1,0:T(4,128)S(1)} %get-tuple-element.44), channel_id=1, source_target_pairs={{0,1},{1,0},{2,3},{3,2},{4,5},{5,4},{6,7},{7,6},{8,9},{9,8},{10,11... | collective-permute-start | bytes 36872 | tf_op jit(solution)/shard_map/ppermute | solution.py:575
  24.4 2.3 %collective-permute-done.7.rb_ref = f32[4,768]{1,0:T(4,128)S(1)} collective-permute-done((f32[4,768]{1,0:T(4,128)S(1)}, f32[4,768]{1,0:T(4,128)S(1)}, u32[]{:S(2)}, u32[]{:S(2)}) %collective-permute-start.7) | collective-permute-done | bytes 12320 | tf_op jit(solution)/shard_map/ppermute | solution.py:575
  26.7 2.9 %apply.1 = (f32[16,768]{1,0:T(8,128)S(1)}, f32[3,4,384]{2,1,0:T(4,128)S(1)}, f32[3,4,384]{2,1,0:T(4,128)S(1)}, f32[8,384]{1,0:T(8,128)S(1)}, f32[1,128]{1,0:T(1,128)S(1)}) custom-call(f32[16,768]{1,0:T(8,128)S(1)} %get-tuple-element.43.p_ref, f32[4,768]{1,0:T(4,128)S(1)} %collective-permute-done.6.ra_ref, f32[4,768]{1,0:T(4,128)S(1)} %collective-permute-done.7.rb_ref, ...), custom_call_target="tpu_custom_call" | custom-call | tf_op jit(solution)/shard_map/apply/pallas_call | solution.py:586
  29.9 1.2 %collective-permute-start.9 = (f32[3,4,384]{2,1,0:T(4,128)S(1)}, f32[3,4,384]{2,1,0:T(4,128)S(1)}, u32[]{:S(2)}, u32[]{:S(2)}) collective-permute-start(f32[3,4,384]{2,1,0:T(4,128)S(1)} %get-tuple-element.50), channel_id=1, source_target_pairs={{0,24},{8,16},{16,8},{24,0},{1,25},{9,17},{17,9},{25,1},{2,26},{10... | collective-permute-start | bytes 55304 | tf_op jit(solution)/shard_map/ppermute | solution.py:575
  31.1 1.2 %collective-permute-done.8.ra_ref = f32[3,4,384]{2,1,0:T(4,128)S(1)} collective-permute-done((f32[3,4,384]{2,1,0:T(4,128)S(1)}, f32[3,4,384]{2,1,0:T(4,128)S(1)}, u32[]{:S(2)}, u32[]{:S(2)}) %collective-permute-start.8) | collective-permute-done | bytes 18464 | tf_op jit(solution)/shard_map/ppermute | solution.py:575
  32.3 1.2 %collective-permute-done.9.rb_ref = f32[3,4,384]{2,1,0:T(4,128)S(1)} collective-permute-done((f32[3,4,384]{2,1,0:T(4,128)S(1)}, f32[3,4,384]{2,1,0:T(4,128)S(1)}, u32[]{:S(2)}, u32[]{:S(2)}) %collective-permute-start.9) | collective-permute-done | bytes 18464 | tf_op jit(solution)/shard_map/ppermute | solution.py:575
  33.5 3.4 %collective-permute-start.10 = (f32[4,768]{1,0:T(4,128)S(1)}, f32[4,768]{1,0:T(4,128)S(1)}, u32[]{:S(2)}, u32[]{:S(2)}) collective-permute-start(f32[4,768]{1,0:T(4,128)S(1)} %get-tuple-element.52), channel_id=1, source_target_pairs={{0,1},{1,0},{2,3},{3,2},{4,5},{5,4},{6,7},{7,6},{8,9},{9,8},{10,11... | collective-permute-start | bytes 36872 | tf_op jit(solution)/shard_map/ppermute | solution.py:575
  36.9 0.8 %collective-permute-done.10.ra_ref = f32[4,768]{1,0:T(4,128)S(1)} collective-permute-done((f32[4,768]{1,0:T(4,128)S(1)}, f32[4,768]{1,0:T(4,128)S(1)}, u32[]{:S(2)}, u32[]{:S(2)}) %collective-permute-start.10) | collective-permute-done | bytes 12320 | tf_op jit(solution)/shard_map/ppermute | solution.py:575
  37.7 2.3 %collective-permute-done.11.rb_ref = f32[4,768]{1,0:T(4,128)S(1)} collective-permute-done((f32[4,768]{1,0:T(4,128)S(1)}, f32[4,768]{1,0:T(4,128)S(1)}, u32[]{:S(2)}, u32[]{:S(2)}) %collective-permute-start.11) | collective-permute-done | bytes 12320 | tf_op jit(solution)/shard_map/ppermute | solution.py:575
  40.0 3.1 %last.1 = (f32[8,384]{1,0:T(8,128)S(1)}, f32[8,384]{1,0:T(8,128)S(1)}, f32[32,13,1,128]{3,2,1,0:T(1,128)S(1)}) custom-call(f32[16,768]{1,0:T(8,128)S(1)} %get-tuple-element.51.p_ref, f32[4,768]{1,0:T(4,128)S(1)} %collective-permute-done.10.ra_ref, f32[4,768]{1,0:T(4,128)S(1)} %collective-permute-done.11.rb_ref, ...), custom_call_target="tpu_custom_call" | custom-call | tf_op jit(solution)/shard_map/last/pallas_call | solution.py:586
  43.0 13.5 %all_to_all.5.got_ref = f32[32,13,1,128]{3,2,1,0:T(1,128)S(1)} all-to-all(f32[32,13,1,128]{3,2,1,0:T(1,128)S(1)} %get-tuple-element.57), channel_id=1, replica_groups=mesh['gz'=4,'gy'=8] {'gz','gy'}, dimensions={0} | all-to-all | bytes 425984 | tf_op jit(solution)/shard_map/all_to_all | solution.py:668
  56.5 1.1 %finish.1 = (f32[3,4,8,32]{3,2,1,0:T(8,128)}, f32[3,4,8,32]{3,2,1,0:T(8,128)}) custom-call(f32[8,384]{1,0:T(8,128)S(1)} %get-tuple-element.47.v0_ref, f32[8,384]{1,0:T(8,128)S(1)} %get-tuple-element.55.v1_ref, f32[8,384]{1,0:T(8,128)S(1)} %get-tuple-element.56.part_ref, f32[32,13,1,128]{3,2,1,0:T(1,128)S(1)} %all_to_all.5.got_ref), custom_call_target="tpu_custom_call" | custom-call | tf_op jit(solution)/shard_map/finish/pallas_call | solution.py:586
  (27 shorter events, 1.6 us)
Async XLA Ops:
  0.6 4.8 %copy-start.1 = (f32[32,64,256]{2,1,0:T(8,128)S(1)}, f32[32,64,256]{2,1,0:T(8,128)}, u32[]{:S(2)}) copy-start(f32[32,64,256]{2,1,0:T(8,128)} %m_ref.5) | copy-start | bytes 6291460
  0.6 4.8 %copy-start = (f32[32,64,256]{2,1,0:T(8,128)S(1)}, f32[32,64,256]{2,1,0:T(8,128)}, u32[]{:S(2)}) copy-start(f32[32,64,256]{2,1,0:T(8,128)} %f_ref.5) | copy-start | bytes 6291460
  2.1 12.0 %collective-permute-start.2 = (f32[3,64,256]{2,1,0:T(8,128)S(1)}, f32[3,64,256]{2,1,0:T(8,128)S(1)}, u32[]{:S(2)}, u32[]{:S(2)}) collective-permute-start(f32[3,64,256]{2,1,0:T(8,128)S(1)} %get-tuple-element.37), channel_id=1, source_target_pairs={{0,8},{8,0},{16,24},{24,16},{1,9},{9,1},{17,25},{25,17},{2,10},{10... | collective-permute-start | bytes 589832 | tf_op jit(solution)/shard_map/ppermute | solution.py:575
  4.2 4.0 %copy-start.4 = (bf16[512,256]{1,0:T(8,128)(2,1)S(1)}, bf16[512,256]{1,0:T(8,128)(2,1)}, u32[]{:S(2)}) copy-start(bf16[512,256]{1,0:T(8,128)(2,1)} %constant.12.clone.dx_ref) | copy-start | bytes 786436
  4.2 9.9 %collective-permute-start.3 = (f32[3,64,256]{2,1,0:T(8,128)S(1)}, f32[3,64,256]{2,1,0:T(8,128)S(1)}, u32[]{:S(2)}, u32[]{:S(2)}) collective-permute-start(f32[3,64,256]{2,1,0:T(8,128)S(1)} %get-tuple-element.38), channel_id=1, source_target_pairs={{0,24},{8,16},{16,8},{24,0},{1,25},{9,17},{17,9},{25,1},{2,26},{10... | collective-permute-start | bytes 589832 | tf_op jit(solution)/shard_map/ppermute | solution.py:575
  5.6 4.2 %collective-permute-start = (f32[3,32,256]{2,1,0:T(8,128)S(1)}, f32[3,32,256]{2,1,0:T(8,128)S(1)}, u32[]{:S(2)}, u32[]{:S(2)}) collective-permute-start(f32[3,32,256]{2,1,0:T(8,128)S(1)} %get-tuple-element.34), channel_id=1, source_target_pairs={{0,1},{1,0},{2,3},{3,2},{4,5},{5,4},{6,7},{7,6},{8,9},{9,8},{10,11... | collective-permute-start | bytes 294920 | tf_op jit(solution)/shard_map/ppermute | solution.py:575
  6.9 4.0 %copy-start.2 = (bf16[8,256,256]{2,1,0:T(8,128)(2,1)S(1)}, bf16[8,256,256]{2,1,0:T(8,128)(2,1)}, u32[]{:S(2)}) copy-start(bf16[8,256,256]{2,1,0:T(8,128)(2,1)} %constant.17.clone.re_ref) | copy-start | bytes 3145732
  6.9 4.0 %copy-start.7 = (bf16[64,160]{1,0:T(8,128)(2,1)S(1)}, bf16[64,160]{1,0:T(8,128)(2,1)}, u32[]{:S(2)}) copy-start(bf16[64,160]{1,0:T(8,128)(2,1)} %constant.13.clone.dy_ref) | copy-start | bytes 61444
  6.9 4.0 %collective-permute-start.1 = (f32[3,32,256]{2,1,0:T(8,128)S(1)}, f32[3,32,256]{2,1,0:T(8,128)S(1)}, u32[]{:S(2)}, u32[]{:S(2)}) collective-permute-start(f32[3,32,256]{2,1,0:T(8,128)S(1)} %get-tuple-element.35), channel_id=1, source_target_pairs={{0,7},{1,2},{2,1},{3,4},{4,3},{5,6},{6,5},{7,0},{8,15},{9,10},{10,... | collective-permute-start | bytes 294920 | tf_op jit(solution)/shard_map/ppermute | solution.py:575
  10.9 3.2 %copy-start.5 = (bf16[16,192]{1,0:T(8,128)(2,1)S(1)}, bf16[16,192]{1,0:T(8,128)(2,1)}, u32[]{:S(2)}) copy-start(bf16[16,192]{1,0:T(8,128)(2,1)} %constant.16.clone.ye_ref) | copy-start | bytes 18436
  14.1 12.6 %copy-start.3 = (bf16[8,256,256]{2,1,0:T(8,128)(2,1)S(1)}, bf16[8,256,256]{2,1,0:T(8,128)(2,1)}, u32[]{:S(2)}) copy-start(bf16[8,256,256]{2,1,0:T(8,128)(2,1)} %constant.15.clone.rd_ref) | copy-start | bytes 3145732
  14.1 12.6 %copy-start.6 = (bf16[64,48]{1,0:T(8,128)(2,1)S(1)}, bf16[64,48]{1,0:T(8,128)(2,1)}, u32[]{:S(2)}) copy-start(bf16[64,48]{1,0:T(8,128)(2,1)} %constant.14.clone.yd_ref) | copy-start | bytes 18436
  15.0 2.7 %collective-permute-start.4 = (f32[3,4,384]{2,1,0:T(4,128)S(1)}, f32[3,4,384]{2,1,0:T(4,128)S(1)}, u32[]{:S(2)}, u32[]{:S(2)}) collective-permute-start(f32[3,4,384]{2,1,0:T(4,128)S(1)} %get-tuple-element.41), channel_id=1, source_target_pairs={{0,8},{8,0},{16,24},{24,16},{1,9},{9,1},{17,25},{25,17},{2,10},{10... | collective-permute-start | bytes 55304 | tf_op jit(solution)/shard_map/ppermute | solution.py:575
  16.4 3.5 %collective-permute-start.5 = (f32[3,4,384]{2,1,0:T(4,128)S(1)}, f32[3,4,384]{2,1,0:T(4,128)S(1)}, u32[]{:S(2)}, u32[]{:S(2)}) collective-permute-start(f32[3,4,384]{2,1,0:T(4,128)S(1)} %get-tuple-element.42), channel_id=1, source_target_pairs={{0,24},{8,16},{16,8},{24,0},{1,25},{9,17},{17,9},{25,1},{2,26},{10... | collective-permute-start | bytes 55304 | tf_op jit(solution)/shard_map/ppermute | solution.py:575
  19.9 4.5 %collective-permute-start.6 = (f32[4,768]{1,0:T(4,128)S(1)}, f32[4,768]{1,0:T(4,128)S(1)}, u32[]{:S(2)}, u32[]{:S(2)}) collective-permute-start(f32[4,768]{1,0:T(4,128)S(1)} %get-tuple-element.44), channel_id=1, source_target_pairs={{0,1},{1,0},{2,3},{3,2},{4,5},{5,4},{6,7},{7,6},{8,9},{9,8},{10,11... | collective-permute-start | bytes 36872 | tf_op jit(solution)/shard_map/ppermute | solution.py:575
  23.6 3.1 %collective-permute-start.7 = (f32[4,768]{1,0:T(4,128)S(1)}, f32[4,768]{1,0:T(4,128)S(1)}, u32[]{:S(2)}, u32[]{:S(2)}) collective-permute-start(f32[4,768]{1,0:T(4,128)S(1)} %get-tuple-element.45), channel_id=1, source_target_pairs={{0,7},{1,2},{2,1},{3,4},{4,3},{5,6},{6,5},{7,0},{8,15},{9,10},{10,... | collective-permute-start | bytes 36872 | tf_op jit(solution)/shard_map/ppermute | solution.py:575
  29.6 2.7 %collective-permute-start.8 = (f32[3,4,384]{2,1,0:T(4,128)S(1)}, f32[3,4,384]{2,1,0:T(4,128)S(1)}, u32[]{:S(2)}, u32[]{:S(2)}) collective-permute-start(f32[3,4,384]{2,1,0:T(4,128)S(1)} %get-tuple-element.49), channel_id=1, source_target_pairs={{0,8},{8,0},{16,24},{24,16},{1,9},{9,1},{17,25},{25,17},{2,10},{10... | collective-permute-start | bytes 55304 | tf_op jit(solution)/shard_map/ppermute | solution.py:575
  29.9 3.5 %collective-permute-start.9 = (f32[3,4,384]{2,1,0:T(4,128)S(1)}, f32[3,4,384]{2,1,0:T(4,128)S(1)}, u32[]{:S(2)}, u32[]{:S(2)}) collective-permute-start(f32[3,4,384]{2,1,0:T(4,128)S(1)} %get-tuple-element.50), channel_id=1, source_target_pairs={{0,24},{8,16},{16,8},{24,0},{1,25},{9,17},{17,9},{25,1},{2,26},{10... | collective-permute-start | bytes 55304 | tf_op jit(solution)/shard_map/ppermute | solution.py:575
  33.5 4.2 %collective-permute-start.10 = (f32[4,768]{1,0:T(4,128)S(1)}, f32[4,768]{1,0:T(4,128)S(1)}, u32[]{:S(2)}, u32[]{:S(2)}) collective-permute-start(f32[4,768]{1,0:T(4,128)S(1)} %get-tuple-element.52), channel_id=1, source_target_pairs={{0,1},{1,0},{2,3},{3,2},{4,5},{5,4},{6,7},{7,6},{8,9},{9,8},{10,11... | collective-permute-start | bytes 36872 | tf_op jit(solution)/shard_map/ppermute | solution.py:575
  36.9 3.1 %collective-permute-start.11 = (f32[4,768]{1,0:T(4,128)S(1)}, f32[4,768]{1,0:T(4,128)S(1)}, u32[]{:S(2)}, u32[]{:S(2)}) collective-permute-start(f32[4,768]{1,0:T(4,128)S(1)} %get-tuple-element.53), channel_id=1, source_target_pairs={{0,7},{1,2},{2,1},{3,4},{4,3},{5,6},{6,5},{7,0},{8,15},{9,10},{10,... | collective-permute-start | bytes 36872 | tf_op jit(solution)/shard_map/ppermute | solution.py:575

commit v4 on v3

--- a/solution.py
+++ b/solution.py
@@ -7,6 +7,7 @@
 from jax.experimental import pallas as pl
 from jax.experimental.pallas import tpu as pltpu
 from jax.sharding import PartitionSpec as P
+
 
 SPACING = 8
 DAMPING = 8.0
@@ -572,7 +573,8 @@
     count = lax.axis_size(axis)
     even = [(i, i ^ 1) for i in range(count)]
     odd = [(i, (i + (1 if i % 2 else -1)) % count) for i in range(count)]
-    return lax.ppermute(value_a, axis, even), lax.ppermute(value_b, axis, odd)
+    value_b = lax.ppermute(value_b, axis, odd)
+    return lax.ppermute(value_a, axis, even), value_b
 
 
 def scratch_of(item):
@@ -581,7 +583,7 @@
     return pltpu.VMEM(*(item if isinstance(item[0], tuple) else (item, F32)))
 
 
-def call(kernel, name, outs, scratch, *args, far=0):
+def call(kernel, outs, scratch, *args, far=0):
     shapes = [jax.ShapeDtypeStruct(o, F32) for o in outs]
     return pl.pallas_call(
         kernel,
@@ -590,7 +592,6 @@
         out_specs=[VMEM] * len(outs),
         scratch_shapes=[scratch_of(n) for n in scratch],
         compiler_params=PARAMS,
-        name=name,
     )(*[pltpu.with_memory_space_constraint(v, pltpu.HBM) for v in args[:far]], *args[far:])
 
 
@@ -604,18 +605,16 @@
     zhalo, yhalo = (REACH, s.sy, s.nx), (REACH, s.sz, s.nx)
     za, zb = call(
         part(faces_z_kernel, s),
-        "faces_z",
         [zhalo, zhalo],
         [(2, 2, *zhalo), pltpu.SemaphoreType.DMA((2, 2))],
         fixed, moving, far=2,
     )
     za, zb = swap(za, zb, "gz")
-    ya, yb = call(part(faces_y_kernel, s), "faces_y", [yhalo, yhalo], [], fixed, moving)
+    ya, yb = call(part(faces_y_kernel, s), [yhalo, yhalo], [], fixed, moving)
     ya, yb = swap(ya, yb, "gy")
     volume = fixed.shape
     total, diff, gx, gz_inner = call(
         part(start_kernel, s),
-        "start",
         [volume, volume, volume, (s.sz - 2 * REACH, s.sy, s.nx)],
         [],
         fixed, moving, dx,
@@ -624,7 +623,6 @@
     half = ((s.cells, s.nx), BF16)
     gy, inner = call(
         part(inner_kernel, s),
-        "inner",
         [volume, acc],
         [(s.sz, 16, s.nx), half, half, half, half],
         total, diff, gx, gz_inner, ya, yb, dy, re,
@@ -633,7 +631,6 @@
     few = ((2 * REACH * 3 * s.sy, s.nx), BF16)
     gz_edge, grid0, za, zb = call(
         part(edge_kernel, s),
-        "edge",
         [(2 * REACH, s.sy, s.nx), grid, zface, zface],
         [(2 * REACH, s.sy, s.nx), few, few, acc],
         total, diff, gx, gy, za, zb, inner, ye, re,
@@ -641,9 +638,7 @@
 
     def fold_z(value, za, zb):
         za, zb = swap(za, zb, "gz")
-        value, ya, yb = call(
-            part(fold_z_kernel, s), "fold_z", [grid, yface, yface], [], value, za, zb
-        )
+        value, ya, yb = call(part(fold_z_kernel, s), [grid, yface, yface], [], value, za, zb)
         return (value, *swap(ya, yb, "gy"))
 
     own = (s.cy, 3 * s.own)
@@ -653,14 +648,12 @@
     grads = (gz_inner, gz_edge, gy, gx)
     grid1, za, zb, v0, sums = call(
         part(apply_kernel, s),
-        "apply",
         [grid, zface, zface, own, (1, LANES)],
         [grid, *work],
         *fold_z(grid0, za, zb), *grads, yd, rd, ye, re,
     )
     v1, mine, send = call(
         part(last_kernel, s),
-        "last",
         [own, own, (devices, s.block, 1, LANES)],
         [grid, grid, (2, 16 + s.bp, 2 * LANES), (s.bp, 3 * s.own), *work],
         *fold_z(grid1, za, zb), *grads, sums, yd, rd, ye, re,
@@ -669,7 +662,7 @@
     out = (3, s.cz, s.cy, s.cx)
     return tuple(
         call(
-            part(finish_kernel, s), "finish", [out, out], [own, (2, s.cy, LANES), (2, s.cy, LANES)], v0, v1, mine, got
+            part(finish_kernel, s), [out, out], [own, (2, s.cy, LANES), (2, s.cy, LANES)], v0, v1, mine, got
         )
     )
 

time: 57.8 us -> 57.8 us (level)
  no operation moved by 1% of the time
where the time goes in v4:
time: 57.8 us; the launch traced here: 57.6 us
  starting transfers between devices  16.3 us (28%)
  Pallas kernels  14.3 us (25%)
  blocking collectives  13.5 us (23%)
  waiting for transfers between devices  12.7 us (22%)
  between operations  0.75 us (1%)
    pallas_call x10, Pallas kernels, call(): pl.pallas_call(kernel, out_shape=shapes, in_specs=[HBM] * far + [VMEM] *...  14.3 us
    all_to_all x1, blocking collectives, shards(): got = lax.all_to_all(send, ('gz', 'gy'), 0, 0)  13.5 us
    ppermute x6, starting transfers between devices, swap(): return (lax.ppermute(value_a, axis, even), value_b)  12.2 us
    ppermute x6, waiting for transfers between devices, swap(): value_b = lax.ppermute(value_b, axis, odd)  9.08 us
    ppermute x6, starting transfers between devices, swap(): value_b = lax.ppermute(value_b, axis, odd)  4.14 us
    ppermute x6, waiting for transfers between devices, swap(): return (lax.ppermute(value_a, axis, even), value_b)  3.65 us
  transfers between devices with their start and end apart: 12, of which 9 were waited for; matrix products, arithmetic and copies ran while one was open for 0% of the time, Pallas kernels for 9%

profile of v4, /device:TPU:1, one launch (start us, length us, event | category | flops | bytes accessed | tf_op | source)
XLA Modules:
  0.0 57.6 jit_solution(1959518696361280389)
XLA Ops:
  0.6 1.4 %shard_map.98 = (f32[3,64,256]{2,1,0:T(8,128)S(1)}, f32[3,64,256]{2,1,0:T(8,128)S(1)}) custom-call(f32[32,64,256]{2,1,0:T(8,128)} %f_ref.5, f32[32,64,256]{2,1,0:T(8,128)} %m_ref.5), custom_call_target="tpu_custom_call" | custom-call | tf_op jit(solution)/shard_map/pallas_call | solution.py:588
  2.1 2.1 %collective-permute-start.2 = (f32[3,64,256]{2,1,0:T(8,128)S(1)}, f32[3,64,256]{2,1,0:T(8,128)S(1)}, u32[]{:S(2)}, u32[]{:S(2)}) collective-permute-start(f32[3,64,256]{2,1,0:T(8,128)S(1)} %get-tuple-element.37), channel_id=1, source_target_pairs={{0,8},{8,0},{16,24},{24,16},{1,9},{9,1},{17,25},{25,17},{2,10},{10... | collective-permute-start | bytes 589832 | tf_op jit(solution)/shard_map/ppermute | solution.py:577
  4.2 1.2 %collective-permute-start.3 = (f32[3,64,256]{2,1,0:T(8,128)S(1)}, f32[3,64,256]{2,1,0:T(8,128)S(1)}, u32[]{:S(2)}, u32[]{:S(2)}) collective-permute-start(f32[3,64,256]{2,1,0:T(8,128)S(1)} %get-tuple-element.38), channel_id=1, source_target_pairs={{0,24},{8,16},{16,8},{24,0},{1,25},{9,17},{17,9},{25,1},{2,26},{10... | collective-permute-start | bytes 589832 | tf_op jit(solution)/shard_map/ppermute | solution.py:576
  5.6 1.3 %collective-permute-start = (f32[3,32,256]{2,1,0:T(8,128)S(1)}, f32[3,32,256]{2,1,0:T(8,128)S(1)}, u32[]{:S(2)}, u32[]{:S(2)}) collective-permute-start(f32[3,32,256]{2,1,0:T(8,128)S(1)} %get-tuple-element.34), channel_id=1, source_target_pairs={{0,1},{1,0},{2,3},{3,2},{4,5},{5,4},{6,7},{7,6},{8,9},{9,8},{10,11... | collective-permute-start | bytes 294920 | tf_op jit(solution)/shard_map/ppermute | solution.py:577
  6.9 1.3 %collective-permute-start.1 = (f32[3,32,256]{2,1,0:T(8,128)S(1)}, f32[3,32,256]{2,1,0:T(8,128)S(1)}, u32[]{:S(2)}, u32[]{:S(2)}) collective-permute-start(f32[3,32,256]{2,1,0:T(8,128)S(1)} %get-tuple-element.35), channel_id=1, source_target_pairs={{0,7},{1,2},{2,1},{3,4},{4,3},{5,6},{6,5},{7,0},{8,15},{9,10},{10,... | collective-permute-start | bytes 294920 | tf_op jit(solution)/shard_map/ppermute | solution.py:576
  8.1 1.6 %shard_map.95 = (f32[32,64,256]{2,1,0:T(8,128)S(1)}, f32[32,64,256]{2,1,0:T(8,128)S(1)}, f32[32,64,256]{2,1,0:T(8,128)S(1)}, f32[26,64,256]{2,1,0:T(8,128)S(1)}) custom-call(f32[32,64,256]{2,1,0:T(8,128)S(1)} %copy-done, f32[32,64,256]{2,1,0:T(8,128)S(1)} %copy-done.1, bf16[512,256]{1,0:T(8,128)(2,1)S(1)} %copy-done.4), custom_call_target="tpu_custom_call" | custom-call | tf_op jit(solution)/shard_map/pallas_call | solution.py:588
  9.8 1.1 %collective-permute-done.1.rb_ref = f32[3,32,256]{2,1,0:T(8,128)S(1)} collective-permute-done((f32[3,32,256]{2,1,0:T(8,128)S(1)}, f32[3,32,256]{2,1,0:T(8,128)S(1)}, u32[]{:S(2)}, u32[]{:S(2)}) %collective-permute-start.1) | collective-permute-done | bytes 98336 | tf_op jit(solution)/shard_map/ppermute | solution.py:576
  10.9 3.2 %shard_map.97 = (f32[32,64,256]{2,1,0:T(8,128)S(1)}, f32[768,256]{1,0:T(8,128)S(1)}) custom-call(f32[32,64,256]{2,1,0:T(8,128)S(1)} %get-tuple-element.30.sum_ref, f32[32,64,256]{2,1,0:T(8,128)S(1)} %get-tuple-element.31.diff_ref, f32[32,64,256]{2,1,0:T(8,128)S(1)} %get-tuple-element.32.gx_ref, f32[26,64,256]{2,1,0:T(8,128)S(1)} %get-tuple-element.33.gz_ref.gi_ref, ...), custom_call_target="tpu_custom_call" | custom-call | tf_op jit(solution)/shard_map/pallas_call | solution.py:588
  14.1 0.8 %shard_map.99 = (f32[6,64,256]{2,1,0:T(8,128)S(1)}, f32[16,768]{1,0:T(8,128)S(1)}, f32[3,4,384]{2,1,0:T(4,128)S(1)}, f32[3,4,384]{2,1,0:T(4,128)S(1)}) custom-call(f32[32,64,256]{2,1,0:T(8,128)S(1)} %get-tuple-element.30.sum_ref, f32[32,64,256]{2,1,0:T(8,128)S(1)} %get-tuple-element.31.diff_ref, f32[32,64,256]{2,1,0:T(8,128)S(1)} %get-tuple-element.32.gx_ref, ...), custom_call_target="tpu_custom_call" | custom-call | tf_op jit(solution)/shard_map/pallas_call | solution.py:588
  15.0 1.4 %collective-permute-start.4 = (f32[3,4,384]{2,1,0:T(4,128)S(1)}, f32[3,4,384]{2,1,0:T(4,128)S(1)}, u32[]{:S(2)}, u32[]{:S(2)}) collective-permute-start(f32[3,4,384]{2,1,0:T(4,128)S(1)} %get-tuple-element.41), channel_id=1, source_target_pairs={{0,8},{8,0},{16,24},{24,16},{1,9},{9,1},{17,25},{25,17},{2,10},{10... | collective-permute-start | bytes 55304 | tf_op jit(solution)/shard_map/ppermute | solution.py:577
  16.6 1.1 %collective-permute-done.4.ra_ref = f32[3,4,384]{2,1,0:T(4,128)S(1)} collective-permute-done((f32[3,4,384]{2,1,0:T(4,128)S(1)}, f32[3,4,384]{2,1,0:T(4,128)S(1)}, u32[]{:S(2)}, u32[]{:S(2)}) %collective-permute-start.4) | collective-permute-done | bytes 18464 | tf_op jit(solution)/shard_map/ppermute | solution.py:577
  17.7 2.2 %collective-permute-done.5.rb_ref = f32[3,4,384]{2,1,0:T(4,128)S(1)} collective-permute-done((f32[3,4,384]{2,1,0:T(4,128)S(1)}, f32[3,4,384]{2,1,0:T(4,128)S(1)}, u32[]{:S(2)}, u32[]{:S(2)}) %collective-permute-start.5) | collective-permute-done | bytes 18464 | tf_op jit(solution)/shard_map/ppermute | solution.py:576
  19.9 3.7 %collective-permute-start.6 = (f32[4,768]{1,0:T(4,128)S(1)}, f32[4,768]{1,0:T(4,128)S(1)}, u32[]{:S(2)}, u32[]{:S(2)}) collective-permute-start(f32[4,768]{1,0:T(4,128)S(1)} %get-tuple-element.44), channel_id=1, source_target_pairs={{0,1},{1,0},{2,3},{3,2},{4,5},{5,4},{6,7},{7,6},{8,9},{9,8},{10,11... | collective-permute-start | bytes 36872 | tf_op jit(solution)/shard_map/ppermute | solution.py:577
  24.4 2.3 %collective-permute-done.7.rb_ref = f32[4,768]{1,0:T(4,128)S(1)} collective-permute-done((f32[4,768]{1,0:T(4,128)S(1)}, f32[4,768]{1,0:T(4,128)S(1)}, u32[]{:S(2)}, u32[]{:S(2)}) %collective-permute-start.7) | collective-permute-done | bytes 12320 | tf_op jit(solution)/shard_map/ppermute | solution.py:576
  26.7 2.9 %shard_map.101 = (f32[16,768]{1,0:T(8,128)S(1)}, f32[3,4,384]{2,1,0:T(4,128)S(1)}, f32[3,4,384]{2,1,0:T(4,128)S(1)}, f32[8,384]{1,0:T(8,128)S(1)}, f32[1,128]{1,0:T(1,128)S(1)}) custom-call(f32[16,768]{1,0:T(8,128)S(1)} %get-tuple-element.43.p_ref, f32[4,768]{1,0:T(4,128)S(1)} %collective-permute-done.6.ra_ref, f32[4,768]{1,0:T(4,128)S(1)} %collective-permute-done.7.rb_ref, ...), custom_call_target="tpu_custom_call" | custom-call | tf_op jit(solution)/shard_map/pallas_call | solution.py:588
  29.9 1.2 %collective-permute-start.9 = (f32[3,4,384]{2,1,0:T(4,128)S(1)}, f32[3,4,384]{2,1,0:T(4,128)S(1)}, u32[]{:S(2)}, u32[]{:S(2)}) collective-permute-start(f32[3,4,384]{2,1,0:T(4,128)S(1)} %get-tuple-element.50), channel_id=1, source_target_pairs={{0,24},{8,16},{16,8},{24,0},{1,25},{9,17},{17,9},{25,1},{2,26},{10... | collective-permute-start | bytes 55304 | tf_op jit(solution)/shard_map/ppermute | solution.py:576
  31.1 1.2 %collective-permute-done.8.ra_ref = f32[3,4,384]{2,1,0:T(4,128)S(1)} collective-permute-done((f32[3,4,384]{2,1,0:T(4,128)S(1)}, f32[3,4,384]{2,1,0:T(4,128)S(1)}, u32[]{:S(2)}, u32[]{:S(2)}) %collective-permute-start.8) | collective-permute-done | bytes 18464 | tf_op jit(solution)/shard_map/ppermute | solution.py:577
  32.3 1.2 %collective-permute-done.9.rb_ref = f32[3,4,384]{2,1,0:T(4,128)S(1)} collective-permute-done((f32[3,4,384]{2,1,0:T(4,128)S(1)}, f32[3,4,384]{2,1,0:T(4,128)S(1)}, u32[]{:S(2)}, u32[]{:S(2)}) %collective-permute-start.9) | collective-permute-done | bytes 18464 | tf_op jit(solution)/shard_map/ppermute | solution.py:576
  33.5 3.4 %collective-permute-start.10 = (f32[4,768]{1,0:T(4,128)S(1)}, f32[4,768]{1,0:T(4,128)S(1)}, u32[]{:S(2)}, u32[]{:S(2)}) collective-permute-start(f32[4,768]{1,0:T(4,128)S(1)} %get-tuple-element.52), channel_id=1, source_target_pairs={{0,1},{1,0},{2,3},{3,2},{4,5},{5,4},{6,7},{7,6},{8,9},{9,8},{10,11... | collective-permute-start | bytes 36872 | tf_op jit(solution)/shard_map/ppermute | solution.py:577
  36.9 0.8 %collective-permute-done.10.ra_ref = f32[4,768]{1,0:T(4,128)S(1)} collective-permute-done((f32[4,768]{1,0:T(4,128)S(1)}, f32[4,768]{1,0:T(4,128)S(1)}, u32[]{:S(2)}, u32[]{:S(2)}) %collective-permute-start.10) | collective-permute-done | bytes 12320 | tf_op jit(solution)/shard_map/ppermute | solution.py:577
  37.7 2.3 %collective-permute-done.11.rb_ref = f32[4,768]{1,0:T(4,128)S(1)} collective-permute-done((f32[4,768]{1,0:T(4,128)S(1)}, f32[4,768]{1,0:T(4,128)S(1)}, u32[]{:S(2)}, u32[]{:S(2)}) %collective-permute-start.11) | collective-permute-done | bytes 12320 | tf_op jit(solution)/shard_map/ppermute | solution.py:576
  40.0 3.1 %shard_map.103 = (f32[8,384]{1,0:T(8,128)S(1)}, f32[8,384]{1,0:T(8,128)S(1)}, f32[32,13,1,128]{3,2,1,0:T(1,128)S(1)}) custom-call(f32[16,768]{1,0:T(8,128)S(1)} %get-tuple-element.51.p_ref, f32[4,768]{1,0:T(4,128)S(1)} %collective-permute-done.10.ra_ref, f32[4,768]{1,0:T(4,128)S(1)} %collective-permute-done.11.rb_ref, ...), custom_call_target="tpu_custom_call" | custom-call | tf_op jit(solution)/shard_map/pallas_call | solution.py:588
  43.0 13.5 %all_to_all.5.got_ref = f32[32,13,1,128]{3,2,1,0:T(1,128)S(1)} all-to-all(f32[32,13,1,128]{3,2,1,0:T(1,128)S(1)} %get-tuple-element.57), channel_id=1, replica_groups=mesh['gz'=4,'gy'=8] {'gz','gy'}, dimensions={0} | all-to-all | bytes 425984 | tf_op jit(solution)/shard_map/all_to_all | solution.py:661
  56.5 1.1 %shard_map.104 = (f32[3,4,8,32]{3,2,1,0:T(8,128)}, f32[3,4,8,32]{3,2,1,0:T(8,128)}) custom-call(f32[8,384]{1,0:T(8,128)S(1)} %get-tuple-element.47.v0_ref, f32[8,384]{1,0:T(8,128)S(1)} %get-tuple-element.55.v1_ref, f32[8,384]{1,0:T(8,128)S(1)} %get-tuple-element.56.part_ref, f32[32,13,1,128]{3,2,1,0:T(1,128)S(1)} %all_to_all.5.got_ref), custom_call_target="tpu_custom_call" | custom-call | tf_op jit(solution)/shard_map/pallas_call | solution.py:588
  (27 shorter events, 1.6 us)
Async XLA Ops:
  0.6 4.8 %copy-start.1 = (f32[32,64,256]{2,1,0:T(8,128)S(1)}, f32[32,64,256]{2,1,0:T(8,128)}, u32[]{:S(2)}) copy-start(f32[32,64,256]{2,1,0:T(8,128)} %m_ref.5) | copy-start | bytes 6291460
  0.6 4.8 %copy-start = (f32[32,64,256]{2,1,0:T(8,128)S(1)}, f32[32,64,256]{2,1,0:T(8,128)}, u32[]{:S(2)}) copy-start(f32[32,64,256]{2,1,0:T(8,128)} %f_ref.5) | copy-start | bytes 6291460
  2.1 12.0 %collective-permute-start.2 = (f32[3,64,256]{2,1,0:T(8,128)S(1)}, f32[3,64,256]{2,1,0:T(8,128)S(1)}, u32[]{:S(2)}, u32[]{:S(2)}) collective-permute-start(f32[3,64,256]{2,1,0:T(8,128)S(1)} %get-tuple-element.37), channel_id=1, source_target_pairs={{0,8},{8,0},{16,24},{24,16},{1,9},{9,1},{17,25},{25,17},{2,10},{10... | collective-permute-start | bytes 589832 | tf_op jit(solution)/shard_map/ppermute | solution.py:577
  4.2 4.0 %copy-start.4 = (bf16[512,256]{1,0:T(8,128)(2,1)S(1)}, bf16[512,256]{1,0:T(8,128)(2,1)}, u32[]{:S(2)}) copy-start(bf16[512,256]{1,0:T(8,128)(2,1)} %constant.12.clone.dx_ref) | copy-start | bytes 786436
  4.2 9.9 %collective-permute-start.3 = (f32[3,64,256]{2,1,0:T(8,128)S(1)}, f32[3,64,256]{2,1,0:T(8,128)S(1)}, u32[]{:S(2)}, u32[]{:S(2)}) collective-permute-start(f32[3,64,256]{2,1,0:T(8,128)S(1)} %get-tuple-element.38), channel_id=1, source_target_pairs={{0,24},{8,16},{16,8},{24,0},{1,25},{9,17},{17,9},{25,1},{2,26},{10... | collective-permute-start | bytes 589832 | tf_op jit(solution)/shard_map/ppermute | solution.py:576
  5.6 4.2 %collective-permute-start = (f32[3,32,256]{2,1,0:T(8,128)S(1)}, f32[3,32,256]{2,1,0:T(8,128)S(1)}, u32[]{:S(2)}, u32[]{:S(2)}) collective-permute-start(f32[3,32,256]{2,1,0:T(8,128)S(1)} %get-tuple-element.34), channel_id=1, source_target_pairs={{0,1},{1,0},{2,3},{3,2},{4,5},{5,4},{6,7},{7,6},{8,9},{9,8},{10,11... | collective-permute-start | bytes 294920 | tf_op jit(solution)/shard_map/ppermute | solution.py:577
  6.9 4.0 %copy-start.2 = (bf16[8,256,256]{2,1,0:T(8,128)(2,1)S(1)}, bf16[8,256,256]{2,1,0:T(8,128)(2,1)}, u32[]{:S(2)}) copy-start(bf16[8,256,256]{2,1,0:T(8,128)(2,1)} %constant.17.clone.re_ref) | copy-start | bytes 3145732
  6.9 4.0 %copy-start.7 = (bf16[64,160]{1,0:T(8,128)(2,1)S(1)}, bf16[64,160]{1,0:T(8,128)(2,1)}, u32[]{:S(2)}) copy-start(bf16[64,160]{1,0:T(8,128)(2,1)} %constant.13.clone.dy_ref) | copy-start | bytes 61444
  6.9 4.0 %collective-permute-start.1 = (f32[3,32,256]{2,1,0:T(8,128)S(1)}, f32[3,32,256]{2,1,0:T(8,128)S(1)}, u32[]{:S(2)}, u32[]{:S(2)}) collective-permute-start(f32[3,32,256]{2,1,0:T(8,128)S(1)} %get-tuple-element.35), channel_id=1, source_target_pairs={{0,7},{1,2},{2,1},{3,4},{4,3},{5,6},{6,5},{7,0},{8,15},{9,10},{10,... | collective-permute-start | bytes 294920 | tf_op jit(solution)/shard_map/ppermute | solution.py:576
  10.9 3.2 %copy-start.5 = (bf16[16,192]{1,0:T(8,128)(2,1)S(1)}, bf16[16,192]{1,0:T(8,128)(2,1)}, u32[]{:S(2)}) copy-start(bf16[16,192]{1,0:T(8,128)(2,1)} %constant.16.clone.ye_ref) | copy-start | bytes 18436
  14.1 12.6 %copy-start.3 = (bf16[8,256,256]{2,1,0:T(8,128)(2,1)S(1)}, bf16[8,256,256]{2,1,0:T(8,128)(2,1)}, u32[]{:S(2)}) copy-start(bf16[8,256,256]{2,1,0:T(8,128)(2,1)} %constant.15.clone.rd_ref) | copy-start | bytes 3145732
  14.1 12.6 %copy-start.6 = (bf16[64,48]{1,0:T(8,128)(2,1)S(1)}, bf16[64,48]{1,0:T(8,128)(2,1)}, u32[]{:S(2)}) copy-start(bf16[64,48]{1,0:T(8,128)(2,1)} %constant.14.clone.yd_ref) | copy-start | bytes 18436
  15.0 2.7 %collective-permute-start.4 = (f32[3,4,384]{2,1,0:T(4,128)S(1)}, f32[3,4,384]{2,1,0:T(4,128)S(1)}, u32[]{:S(2)}, u32[]{:S(2)}) collective-permute-start(f32[3,4,384]{2,1,0:T(4,128)S(1)} %get-tuple-element.41), channel_id=1, source_target_pairs={{0,8},{8,0},{16,24},{24,16},{1,9},{9,1},{17,25},{25,17},{2,10},{10... | collective-permute-start | bytes 55304 | tf_op jit(solution)/shard_map/ppermute | solution.py:577
  16.4 3.5 %collective-permute-start.5 = (f32[3,4,384]{2,1,0:T(4,128)S(1)}, f32[3,4,384]{2,1,0:T(4,128)S(1)}, u32[]{:S(2)}, u32[]{:S(2)}) collective-permute-start(f32[3,4,384]{2,1,0:T(4,128)S(1)} %get-tuple-element.42), channel_id=1, source_target_pairs={{0,24},{8,16},{16,8},{24,0},{1,25},{9,17},{17,9},{25,1},{2,26},{10... | collective-permute-start | bytes 55304 | tf_op jit(solution)/shard_map/ppermute | solution.py:576
  19.9 4.5 %collective-permute-start.6 = (f32[4,768]{1,0:T(4,128)S(1)}, f32[4,768]{1,0:T(4,128)S(1)}, u32[]{:S(2)}, u32[]{:S(2)}) collective-permute-start(f32[4,768]{1,0:T(4,128)S(1)} %get-tuple-element.44), channel_id=1, source_target_pairs={{0,1},{1,0},{2,3},{3,2},{4,5},{5,4},{6,7},{7,6},{8,9},{9,8},{10,11... | collective-permute-start | bytes 36872 | tf_op jit(solution)/shard_map/ppermute | solution.py:577
  23.6 3.1 %collective-permute-start.7 = (f32[4,768]{1,0:T(4,128)S(1)}, f32[4,768]{1,0:T(4,128)S(1)}, u32[]{:S(2)}, u32[]{:S(2)}) collective-permute-start(f32[4,768]{1,0:T(4,128)S(1)} %get-tuple-element.45), channel_id=1, source_target_pairs={{0,7},{1,2},{2,1},{3,4},{4,3},{5,6},{6,5},{7,0},{8,15},{9,10},{10,... | collective-permute-start | bytes 36872 | tf_op jit(solution)/shard_map/ppermute | solution.py:576
  29.6 2.7 %collective-permute-start.8 = (f32[3,4,384]{2,1,0:T(4,128)S(1)}, f32[3,4,384]{2,1,0:T(4,128)S(1)}, u32[]{:S(2)}, u32[]{:S(2)}) collective-permute-start(f32[3,4,384]{2,1,0:T(4,128)S(1)} %get-tuple-element.49), channel_id=1, source_target_pairs={{0,8},{8,0},{16,24},{24,16},{1,9},{9,1},{17,25},{25,17},{2,10},{10... | collective-permute-start | bytes 55304 | tf_op jit(solution)/shard_map/ppermute | solution.py:577
  29.9 3.5 %collective-permute-start.9 = (f32[3,4,384]{2,1,0:T(4,128)S(1)}, f32[3,4,384]{2,1,0:T(4,128)S(1)}, u32[]{:S(2)}, u32[]{:S(2)}) collective-permute-start(f32[3,4,384]{2,1,0:T(4,128)S(1)} %get-tuple-element.50), channel_id=1, source_target_pairs={{0,24},{8,16},{16,8},{24,0},{1,25},{9,17},{17,9},{25,1},{2,26},{10... | collective-permute-start | bytes 55304 | tf_op jit(solution)/shard_map/ppermute | solution.py:576
  33.5 4.2 %collective-permute-start.10 = (f32[4,768]{1,0:T(4,128)S(1)}, f32[4,768]{1,0:T(4,128)S(1)}, u32[]{:S(2)}, u32[]{:S(2)}) collective-permute-start(f32[4,768]{1,0:T(4,128)S(1)} %get-tuple-element.52), channel_id=1, source_target_pairs={{0,1},{1,0},{2,3},{3,2},{4,5},{5,4},{6,7},{7,6},{8,9},{9,8},{10,11... | collective-permute-start | bytes 36872 | tf_op jit(solution)/shard_map/ppermute | solution.py:577
  36.9 3.1 %collective-permute-start.11 = (f32[4,768]{1,0:T(4,128)S(1)}, f32[4,768]{1,0:T(4,128)S(1)}, u32[]{:S(2)}, u32[]{:S(2)}) collective-permute-start(f32[4,768]{1,0:T(4,128)S(1)} %get-tuple-element.53), channel_id=1, source_target_pairs={{0,7},{1,2},{2,1},{3,4},{4,3},{5,6},{6,5},{7,0},{8,15},{9,10},{10,... | collective-permute-start | bytes 36872 | tf_op jit(solution)/shard_map/ppermute | solution.py:576

commit v5 on v4

--- a/solution.py
+++ b/solution.py
@@ -42,6 +42,7 @@
         self.block = self.cy + self.cy // 2 + 1
         assert self.tap % LANES == 0 and self.own % LANES == 0
         assert self.cy % 8 == 0 and self.bp == self.cy + 8 and self.cz > 1
+        assert self.sy % 16 == 0 and self.sy > 32
 
 
 def taps():
@@ -111,8 +112,10 @@
                 dy[y, s.sy + REACH + at - s.sy] = value
             else:
                 dy[y, at] = value
-    dx, dy = (v.astype(jnp.bfloat16) for v in (dx, dy))
-    return jnp.asarray(np.concatenate([dx, dx], 0)), jnp.asarray(np.concatenate([dy, dy], 1))
+    own, halo = dy[:, : s.sy], dy[:, s.sy :]
+    halo = np.concatenate([halo[:8], halo[-8:]], 0)
+    pairs = (np.concatenate([dx, dx], 0), *(np.concatenate([v, v], 1) for v in (own, halo)))
+    return tuple(jnp.asarray(v.astype(jnp.bfloat16)) for v in pairs)
 
 
 def split(value):
@@ -211,18 +214,69 @@
     return [z < REACH or z >= s.sz - REACH for z in range(s.sz)]
 
 
-def put_volume(s, row, z, rows, diff_ref, grads, high_ref, low_ref):
+def put_volume(row_of, z, rows, diff_ref, grads, high_ref, low_ref):
     mm = diff_ref[z, rows]
     for c in range(3):
         high, low = split(mm * grads[c])
-        at = slice(row + c * s.sy + rows.start, row + c * s.sy + rows.stop)
+        at = slice(row_of(c), row_of(c) + rows.stop - rows.start)
         high_ref[at, :] = high
         low_ref[at, :] = low
 
 
+def gy_rows(s, gy_ref, side_ref, z, rows):
+    if rows.start == 0:
+        return jnp.concatenate([side_ref[z, :8], gy_ref[z, 8:16]], 0)
+    if rows.stop == s.sy:
+        return jnp.concatenate([gy_ref[z, s.sy - 16 : s.sy - 8], side_ref[z, 8:]], 0)
+    return gy_ref[z, rows]
+
+
+def encode_planes(s, starts, diff_ref, gx_ref, gz_ref, gy_of, re_ref, acc_ref, scratch):
+    waits = edge_planes(s)
+    count = 16 * len(starts)
+    part = 3 * count
+    acc_ref[...] = jnp.zeros_like(acc_ref)
+    for k in range(SPACING):
+        vh, vl = scratch[2 * (k % 2) : 2 * (k % 2) + 2]
+        ready = [zc for zc in range(s.cz) if not waits[zc * SPACING + k]]
+        for zc in ready:
+            z = zc * SPACING + k
+            for i, y in enumerate(starts):
+                rows = slice(y, y + 16)
+                grads = [gz_ref[z - REACH, rows], gy_of(z, rows), gx_ref[z, rows]]
+                base = zc * part + 16 * i
+                put_volume(lambda c: base + c * count, z, rows, diff_ref, grads, vh, vl)
+        at = slice(ready[0] * part, (ready[-1] + 1) * part)
+        weights = re_ref[k]
+        acc_ref[at, :] += dot(
+            jnp.concatenate([vh[at, :], vl[at, :]], 1), jnp.concatenate([weights, weights], 0)
+        )
+
+
 def inner_kernel(
-    s, sum_ref, diff_ref, gx_ref, gz_ref, ra_ref, rb_ref, dy_ref, re_ref,
-    gy_ref, acc_ref, h_ref, vh0, vh1, vl0, vl1,
+    s, sum_ref, diff_ref, gx_ref, gz_ref, dy_ref, re_ref, gy_ref, raw_ref, acc_ref, *scratch
+):
+    dy = dy_ref[...]
+
+    def step(i, carry):
+        for j in range(GROUP):
+            z = i * GROUP + j
+            sh, sl = split(sum_ref[z])
+            value = dot(dy, jnp.concatenate([sh, sl], 0))
+            raw_ref[z] = jnp.concatenate([value[:8], value[s.sy - 8 :]], 0)
+            gy_ref[z] = rounded(value)
+        return carry
+
+    lax.fori_loop(0, s.sz // GROUP, step, 0)
+    starts = range(16, s.sy - 16, 16)
+    encode_planes(
+        s, starts, diff_ref, gx_ref, gz_ref, lambda z, rows: gy_ref[z, rows], re_ref, acc_ref, scratch
+    )
+
+
+def side_kernel(
+    s, diff_ref, gx_ref, gz_ref, gy_ref, raw_ref, ra_ref, rb_ref, dy_ref, re_ref,
+    side_ref, acc_ref, h_ref, *scratch,
 ):
     below, above, even = place("gy")
     h_ref[...] = jnp.zeros_like(h_ref)
@@ -235,33 +289,19 @@
     def step(i, carry):
         for j in range(GROUP):
             z = i * GROUP + j
-            sh, sl = split(sum_ref[z])
-            hh, hl = split(h_ref[z])
-            gy_ref[z] = rounded(dot(dy, jnp.concatenate([sh, hh, sl, hl], 0)))
+            add = dot(dy, jnp.concatenate(split(h_ref[z]), 0))
+            side_ref[z] = rounded(raw_ref[z] + add)
         return carry
 
     lax.fori_loop(0, s.sz // GROUP, step, 0)
-    waits = edge_planes(s)
-    part = 3 * s.sy
-    acc_ref[...] = jnp.zeros_like(acc_ref)
-    for k in range(SPACING):
-        vh, vl = ((vh0, vl0), (vh1, vl1))[k % 2]
-        ready = [zc for zc in range(s.cz) if not waits[zc * SPACING + k]]
-        for zc in ready:
-            z = zc * SPACING + k
-            for y in range(0, s.sy, 16):
-                rows = slice(y, y + 16)
-                grads = [r[i, rows] for r, i in ((gz_ref, z - REACH), (gy_ref, z), (gx_ref, z))]
-                put_volume(s, zc * part, z, rows, diff_ref, grads, vh, vl)
-        at = slice(ready[0] * part, (ready[-1] + 1) * part)
-        weights = re_ref[k]
-        acc_ref[at, :] += dot(
-            jnp.concatenate([vh[at, :], vl[at, :]], 1), jnp.concatenate([weights, weights], 0)
-        )
+    encode_planes(
+        s, (0, s.sy - 16), diff_ref, gx_ref, gz_ref,
+        lambda z, rows: gy_rows(s, gy_ref, side_ref, z, rows), re_ref, acc_ref, scratch,
+    )
 
 
 def edge_kernel(
-    s, sum_ref, diff_ref, gx_ref, gy_ref, ra_ref, rb_ref, acc_in, ye_ref, re_ref,
+    s, sum_ref, diff_ref, gx_ref, gy_ref, gs_ref, ra_ref, rb_ref, mid_ref, side_ref, ye_ref, re_ref,
     gz_ref, p_ref, za_ref, zb_ref, h_ref, vh_ref, vl_ref, acc_ref,
 ):
     below, above, even = place("gz")
@@ -270,7 +310,7 @@
         h_ref[k] = jnp.where(below, down, 0.0)
         h_ref[REACH + k] = jnp.where(above, up, 0.0)
     part = 3 * s.sy
-    for side, zc in ((0, 0), (1, s.cz - 1)):
+    for side in (0, 1):
         first = 0 if side == 0 else s.sz - REACH
         for j in range(REACH):
             z = first + j
@@ -286,9 +326,9 @@
 
                 gz = rounded(difference(near))
                 gz_ref[side * REACH + j, rows] = gz
-                row = (side * REACH + j) * part
-                grads = [gz, gy_ref[z, rows], gx_ref[z, rows]]
-                put_volume(s, row, z, rows, diff_ref, grads, vh_ref, vl_ref)
+                row = (side * REACH + j) * part + y
+                grads = [gz, gy_rows(s, gy_ref, gs_ref, z, rows), gx_ref[z, rows]]
+                put_volume(lambda c: row + c * s.sy, z, rows, diff_ref, grads, vh_ref, vl_ref)
         lhs, rhs = [], []
         for j in range(REACH):
             row = (side * REACH + j) * part
@@ -296,16 +336,33 @@
             for ref in (vh_ref, vl_ref):
                 lhs.append(ref[row : row + part, :])
                 rhs.append(weights)
-        at = slice(zc * part, (zc + 1) * part)
-        acc_ref[at, :] = acc_in[at, :] + dot(jnp.concatenate(lhs, 1), jnp.concatenate(rhs, 0))
-    encode_y(s, [acc_ref] + [acc_in] * (s.cz - 2) + [acc_ref], ye_ref, p_ref)
+        at = slice(side * part, (side + 1) * part)
+        acc_ref[at, :] = dot(jnp.concatenate(lhs, 1), jnp.concatenate(rhs, 0))
+
+    def rows_of(i):
+        inner = s.sy - 32
+        both = jnp.concatenate(
+            [
+                side_ref[32 * i : 32 * i + 16, :],
+                mid_ref[inner * i : inner * (i + 1), :],
+                side_ref[32 * i + 16 : 32 * i + 32, :],
+            ],
+            0,
+        )
+        zc, c = divmod(i, 3)
+        if zc in (0, s.cz - 1):
+            row = (3 * (zc > 0) + c) * s.sy
+            both = both + acc_ref[row : row + s.sy, :]
+        return both
+
+    encode_y(s, rows_of, ye_ref, p_ref)
     send_faces(s, p_ref, za_ref, zb_ref)
 
 
-def encode_y(s, acc_refs, ye_ref, p_ref):
+def encode_y(s, rows_of, ye_ref, p_ref):
     columns = []
     for i in range(3 * s.cz):
-        both = acc_refs[i // 3][i * s.sy : (i + 1) * s.sy, :]
+        both = rows_of(i)
         columns.append(both[:, : s.tap] + both[:, s.tap :])
     high, low = split(jnp.concatenate(columns, 1))
     out = dot(ye_ref[...], jnp.concatenate([high, low, high], 0))
@@ -390,7 +447,7 @@
         for j, ref in enumerate((even_ref, odd_ref)):
             low = (2 * i + j) * s.tap
             ref[at, :] = jnp.concatenate(split(inner[:, low : low + s.tap]), 1)
-    gz_inner, gz_edge, gy_ref, gx_ref = grads
+    gz_inner, gz_edge, gy_ref, gs_ref, gx_ref = grads
     square = jnp.zeros((16, s.nx), F32)
     half = SPACING // 2
     for k in range(half):
@@ -413,7 +470,7 @@
                         gz_ref, iz = gz_edge, REACH + z - (s.sz - REACH)
                     else:
                         gz_ref, iz = gz_inner, z - REACH
-                    g = [r[i, rows] for r, i in ((gz_ref, iz), (gy_ref, z), (gx_ref, z))]
+                    g = [gz_ref[iz, rows], gy_rows(s, gy_ref, gs_ref, z, rows), gx_ref[z, rows]]
                     f = [e + o if sign > 0 else e - o for e, o in zip(even, odd)]
                     dotted = g[0] * f[0] + g[1] * f[1] + g[2] * f[2]
                     square = square + dotted * dotted
@@ -427,31 +484,41 @@
     return square
 
 
+def square_tile(square):
+    total = square[:8] + square[8:]
+    return sum(total[:, i : i + LANES] for i in range(0, total.shape[1], LANES))
+
+
+def tile_of(own):
+    square = own * own
+    return sum(square[:, i : i + LANES] for i in range(0, own.shape[1], LANES))
+
+
 def total_of(value):
     return jnp.sum(value, keepdims=True)
 
 
-def moments(sums, start):
+def moments(sums):
     lane = iota((1, LANES), 1)
     out = jnp.zeros((1, LANES), F32)
     for k, value in enumerate(sums):
-        out = jnp.where(lane == start + k, value, out)
+        out = jnp.where(lane == k, value, out)
     return out
 
 
 def apply_kernel(
-    s, p_ref, ra_ref, rb_ref, gi_ref, ge_ref, gy_ref, gx_ref, yd_ref, rd_ref, ye_ref, re_ref,
+    s, p_ref, ra_ref, rb_ref, gi_ref, ge_ref, gy_ref, gs_ref, gx_ref, yd_ref, rd_ref, ye_ref, re_ref,
     o_ref, za_ref, zb_ref, own_ref, sum_ref, v_ref, *scratch,
 ):
     fold_y(s, p_ref, ra_ref, rb_ref, v_ref)
     own_part(s, v_ref, own_ref)
     square = operate(
-        s, v_ref, yd_ref, rd_ref, re_ref, (gi_ref, ge_ref, gy_ref, gx_ref), scratch
-    )
-    encode_y(s, [scratch[-1]] * s.cz, ye_ref, o_ref)
+        s, v_ref, yd_ref, rd_ref, re_ref, (gi_ref, ge_ref, gy_ref, gs_ref, gx_ref), scratch
+    )
+    encode_y(s, lambda i: scratch[-1][i * s.sy : (i + 1) * s.sy, :], ye_ref, o_ref)
     send_faces(s, o_ref, za_ref, zb_ref)
-    own = own_ref[...]
-    sum_ref[...] = moments([total_of(own * own), total_of(square)], 0)
+    sum_ref[0] = tile_of(own_ref[...])
+    sum_ref[1] = square_tile(square)
 
 
 NEIGHBOURS = [(dz, dy) for dz in (-1, 0, 1) for dy in (-1, 0, 1) if dz or dy]
@@ -466,18 +533,19 @@
 
 
 def last_kernel(
-    s, p_ref, ra_ref, rb_ref, gi_ref, ge_ref, gy_ref, gx_ref, m_ref,
+    s, p_ref, ra_ref, rb_ref, gi_ref, ge_ref, gy_ref, gs_ref, gx_ref, m_ref,
     yd_ref, rd_ref, ye_ref, re_ref,
     own_ref, part_ref, send_ref, v_ref, o_ref, t_ref, y_ref, *scratch,
 ):
     fold_y(s, p_ref, ra_ref, rb_ref, v_ref)
     own_part(s, v_ref, own_ref)
     square = operate(
-        s, v_ref, yd_ref, rd_ref, re_ref, (gi_ref, ge_ref, gy_ref, gx_ref), scratch
+        s, v_ref, yd_ref, rd_ref, re_ref, (gi_ref, ge_ref, gy_ref, gs_ref, gx_ref), scratch
     )
     own = own_ref[...]
-    sums = m_ref[...] + moments([total_of(own * own), total_of(square)], 2)
-    encode_y(s, [scratch[-1]] * s.cz, ye_ref, o_ref)
+    parts = [m_ref[0], m_ref[1], tile_of(own), square_tile(square)]
+    sums = moments([total_of(v) for v in parts])
+    encode_y(s, lambda i: scratch[-1][i * s.sy : (i + 1) * s.sy, :], ye_ref, o_ref)
     own_part(s, o_ref, part_ref)
     for d in range(send_ref.shape[0]):
         send_ref[d, s.block - 1, :, :] = sums
@@ -598,7 +666,7 @@
 def shards(fixed, moving):
     s = Sizes(fixed.shape)
     devices = lax.axis_size("gz") * lax.axis_size("gy")
-    dx, dy = gradient_consts(s)
+    dx, dy, dy_halo = gradient_consts(s)
     yd, rd, ye, re = consts(s)
     part = functools.partial
 
@@ -621,19 +689,29 @@
     )
     acc = (s.cells, 2 * s.tap)
     half = ((s.cells, s.nx), BF16)
-    gy, inner = call(
-        part(inner_kernel, s),
-        [volume, acc],
-        [(s.sz, 16, s.nx), half, half, half, half],
-        total, diff, gx, gz_inner, ya, yb, dy, re,
+
+    def rows_of(count):
+        rows = 3 * s.cz * count
+        return (rows, 2 * s.tap), [((rows, s.nx), BF16)] * 4
+
+    sides = (s.sz, 16, s.nx)
+    mid_acc, mid_work = rows_of(s.sy - 32)
+    gy, raw, inner = call(
+        part(inner_kernel, s), [volume, sides, mid_acc], mid_work,
+        total, diff, gx, gz_inner, dy, re,
+    )
+    side_acc, side_work = rows_of(32)
+    gy_side, side = call(
+        part(side_kernel, s), [sides, side_acc], [sides, *side_work],
+        diff, gx, gz_inner, gy, raw, ya, yb, dy_halo, re,
     )
     grid, zface, yface = (s.bp, s.wide), (round_up(s.nb, 4) // 4, 4, 3 * s.face), (4, s.wide)
     few = ((2 * REACH * 3 * s.sy, s.nx), BF16)
     gz_edge, grid0, za, zb = call(
         part(edge_kernel, s),
         [(2 * REACH, s.sy, s.nx), grid, zface, zface],
-        [(2 * REACH, s.sy, s.nx), few, few, acc],
-        total, diff, gx, gy, za, zb, inner, ye, re,
+        [(2 * REACH, s.sy, s.nx), few, few, (2 * 3 * s.sy, 2 * s.tap)],
+        total, diff, gx, gy, gy_side, za, zb, inner, side, ye, re,
     )
 
     def fold_z(value, za, zb):
@@ -645,10 +723,10 @@
     field = (s.cells, s.nx)
     left = ((s.cells, 2 * s.tap), BF16)
     work = [left, left, *[field, field, half, half] * 2, acc]
-    grads = (gz_inner, gz_edge, gy, gx)
+    grads = (gz_inner, gz_edge, gy, gy_side, gx)
     grid1, za, zb, v0, sums = call(
         part(apply_kernel, s),
-        [grid, zface, zface, own, (1, LANES)],
+        [grid, zface, zface, own, (2, s.cy, LANES)],
         [grid, *work],
         *fold_z(grid0, za, zb), *grads, yd, rd, ye, re,
     )

time: 57.8 us -> 57.8 us (level)
  Pallas kernels: 14.3 us -> 15.5 us
  waiting for transfers between devices: 12.7 us -> 11.8 us
    ppermute x6, waiting for transfers between devices: 9.08 us -> 7.85 us  [swap(): value_b = lax.ppermute(value_b, axis, odd)]
    pallas_call x10 -> x11, Pallas kernels: 14.3 us -> 15.5 us  [call(): pl.pallas_call(kernel, out_shape=shapes, in_specs=[HBM] * far + [VMEM] *...]
  transfers between devices with their start and end apart: 12 -> 12, of which waited for: 9 -> 8; matrix products, arithmetic and copies ran while one was open for 0% -> 0% of each run, Pallas kernels for 9% -> 11%
where the time goes in v5:
time: 57.8 us; the launch traced here: 57.6 us
  starting transfers between devices  16.2 us (28%)
  Pallas kernels  15.5 us (27%)
  blocking collectives  13.3 us (23%)
  waiting for transfers between devices  11.8 us (20%)
  between operations  0.81 us (1%)
    pallas_call x11, Pallas kernels, call(): pl.pallas_call(kernel, out_shape=shapes, in_specs=[HBM] * far + [VMEM] *...  15.5 us
    all_to_all x1, blocking collectives, shards(): got = lax.all_to_all(send, ('gz', 'gy'), 0, 0)  13.3 us
    ppermute x6, starting transfers between devices, swap(): return (lax.ppermute(value_a, axis, even), value_b)  12.3 us
    ppermute x6, waiting for transfers between devices, swap(): value_b = lax.ppermute(value_b, axis, odd)  7.85 us
    ppermute x6, waiting for transfers between devices, swap(): return (lax.ppermute(value_a, axis, even), value_b)  3.99 us
    ppermute x6, starting transfers between devices, swap(): value_b = lax.ppermute(value_b, axis, odd)  3.92 us
  transfers between devices with their start and end apart: 12, of which 8 were waited for; matrix products, arithmetic and copies ran while one was open for 0% of the time, Pallas kernels for 11%

profile of v5, /device:TPU:1, one launch (start us, length us, event | category | flops | bytes accessed | tf_op | source)
XLA Modules:
  0.0 57.6 jit_solution(14808493139895910276)
XLA Ops:
  0.6 1.4 %shard_map.108 = (f32[3,64,256]{2,1,0:T(8,128)S(1)}, f32[3,64,256]{2,1,0:T(8,128)S(1)}) custom-call(f32[32,64,256]{2,1,0:T(8,128)} %f_ref.5, f32[32,64,256]{2,1,0:T(8,128)} %m_ref.5), custom_call_target="tpu_custom_call" | custom-call | tf_op jit(solution)/shard_map/pallas_call | solution.py:656
  2.1 2.1 %collective-permute-start.2 = (f32[3,64,256]{2,1,0:T(8,128)S(1)}, f32[3,64,256]{2,1,0:T(8,128)S(1)}, u32[]{:S(2)}, u32[]{:S(2)}) collective-permute-start(f32[3,64,256]{2,1,0:T(8,128)S(1)} %get-tuple-element.42), channel_id=1, source_target_pairs={{0,8},{8,0},{16,24},{24,16},{1,9},{9,1},{17,25},{25,17},{2,10},{10... | collective-permute-start | bytes 589832 | tf_op jit(solution)/shard_map/ppermute | solution.py:645
  4.2 1.2 %collective-permute-start.3 = (f32[3,64,256]{2,1,0:T(8,128)S(1)}, f32[3,64,256]{2,1,0:T(8,128)S(1)}, u32[]{:S(2)}, u32[]{:S(2)}) collective-permute-start(f32[3,64,256]{2,1,0:T(8,128)S(1)} %get-tuple-element.43), channel_id=1, source_target_pairs={{0,24},{8,16},{16,8},{24,0},{1,25},{9,17},{17,9},{25,1},{2,26},{10... | collective-permute-start | bytes 589832 | tf_op jit(solution)/shard_map/ppermute | solution.py:644
  5.6 1.3 %collective-permute-start = (f32[3,32,256]{2,1,0:T(8,128)S(1)}, f32[3,32,256]{2,1,0:T(8,128)S(1)}, u32[]{:S(2)}, u32[]{:S(2)}) collective-permute-start(f32[3,32,256]{2,1,0:T(8,128)S(1)} %get-tuple-element.39), channel_id=1, source_target_pairs={{0,1},{1,0},{2,3},{3,2},{4,5},{5,4},{6,7},{7,6},{8,9},{9,8},{10,11... | collective-permute-start | bytes 294920 | tf_op jit(solution)/shard_map/ppermute | solution.py:645
  6.9 1.3 %collective-permute-start.1 = (f32[3,32,256]{2,1,0:T(8,128)S(1)}, f32[3,32,256]{2,1,0:T(8,128)S(1)}, u32[]{:S(2)}, u32[]{:S(2)}) collective-permute-start(f32[3,32,256]{2,1,0:T(8,128)S(1)} %get-tuple-element.40), channel_id=1, source_target_pairs={{0,7},{1,2},{2,1},{3,4},{4,3},{5,6},{6,5},{7,0},{8,15},{9,10},{10,... | collective-permute-start | bytes 294920 | tf_op jit(solution)/shard_map/ppermute | solution.py:644
  8.1 1.6 %shard_map.104 = (f32[32,64,256]{2,1,0:T(8,128)S(1)}, f32[32,64,256]{2,1,0:T(8,128)S(1)}, f32[32,64,256]{2,1,0:T(8,128)S(1)}, f32[26,64,256]{2,1,0:T(8,128)S(1)}) custom-call(f32[32,64,256]{2,1,0:T(8,128)S(1)} %copy-done.1, f32[32,64,256]{2,1,0:T(8,128)S(1)} %copy-done.2, bf16[512,256]{1,0:T(8,128)(2,1)S(1)} %copy-done.4), custom_call_target="tpu_custom_call" | custom-call | tf_op jit(solution)/shard_map/pallas_call | solution.py:656
  9.8 2.3 %shard_map.105 = (f32[32,64,256]{2,1,0:T(8,128)S(1)}, f32[32,16,256]{2,1,0:T(8,128)S(1)}, f32[384,256]{1,0:T(8,128)S(1)}) custom-call(f32[32,64,256]{2,1,0:T(8,128)S(1)} %get-tuple-element.33.sum_ref, f32[32,64,256]{2,1,0:T(8,128)S(1)} %get-tuple-element.34.diff_ref, f32[32,64,256]{2,1,0:T(8,128)S(1)} %get-tuple-element.35.gx_ref, ...), custom_call_target="tpu_custom_call" | custom-call | tf_op jit(solution)/shard_map/pallas_call | solution.py:656
  12.1 2.0 %shard_map.107 = (f32[32,16,256]{2,1,0:T(8,128)S(1)}, f32[384,256]{1,0:T(8,128)S(1)}) custom-call(f32[32,64,256]{2,1,0:T(8,128)S(1)} %get-tuple-element.34.diff_ref, f32[32,64,256]{2,1,0:T(8,128)S(1)} %get-tuple-element.35.gx_ref, f32[26,64,256]{2,1,0:T(8,128)S(1)} %get-tuple-element.36.gz_ref.gi_ref, f32[32,64,256]{2,1,0:T(8,128)S(1)} %get-tuple-element.37.gy_ref, ...), custom_call_target="tpu_custom_call" | custom-call | tf_op jit(solution)/shard_map/pallas_call | solution.py:656
  14.2 0.8 %shard_map.109 = (f32[6,64,256]{2,1,0:T(8,128)S(1)}, f32[16,768]{1,0:T(8,128)S(1)}, f32[3,4,384]{2,1,0:T(4,128)S(1)}, f32[3,4,384]{2,1,0:T(4,128)S(1)}) custom-call(f32[32,64,256]{2,1,0:T(8,128)S(1)} %get-tuple-element.33.sum_ref, f32[32,64,256]{2,1,0:T(8,128)S(1)} %get-tuple-element.34.diff_ref, f32[32,64,256]{2,1,0:T(8,128)S(1)} %get-tuple-element.35.gx_ref, ...), custom_call_target="tpu_custom_call" | custom-call | tf_op jit(solution)/shard_map/pallas_call | solution.py:656
  15.1 1.3 %collective-permute-start.4 = (f32[3,4,384]{2,1,0:T(4,128)S(1)}, f32[3,4,384]{2,1,0:T(4,128)S(1)}, u32[]{:S(2)}, u32[]{:S(2)}) collective-permute-start(f32[3,4,384]{2,1,0:T(4,128)S(1)} %get-tuple-element.47), channel_id=1, source_target_pairs={{0,8},{8,0},{16,24},{24,16},{1,9},{9,1},{17,25},{25,17},{2,10},{10... | collective-permute-start | bytes 55304 | tf_op jit(solution)/shard_map/ppermute | solution.py:645
  16.6 1.2 %collective-permute-done.4.ra_ref = f32[3,4,384]{2,1,0:T(4,128)S(1)} collective-permute-done((f32[3,4,384]{2,1,0:T(4,128)S(1)}, f32[3,4,384]{2,1,0:T(4,128)S(1)}, u32[]{:S(2)}, u32[]{:S(2)}) %collective-permute-start.4) | collective-permute-done | bytes 18464 | tf_op jit(solution)/shard_map/ppermute | solution.py:645
  17.8 2.1 %collective-permute-done.5.rb_ref = f32[3,4,384]{2,1,0:T(4,128)S(1)} collective-permute-done((f32[3,4,384]{2,1,0:T(4,128)S(1)}, f32[3,4,384]{2,1,0:T(4,128)S(1)}, u32[]{:S(2)}, u32[]{:S(2)}) %collective-permute-start.5) | collective-permute-done | bytes 18464 | tf_op jit(solution)/shard_map/ppermute | solution.py:644
  19.9 3.9 %collective-permute-start.6 = (f32[4,768]{1,0:T(4,128)S(1)}, f32[4,768]{1,0:T(4,128)S(1)}, u32[]{:S(2)}, u32[]{:S(2)}) collective-permute-start(f32[4,768]{1,0:T(4,128)S(1)} %get-tuple-element.50), channel_id=1, source_target_pairs={{0,1},{1,0},{2,3},{3,2},{4,5},{5,4},{6,7},{7,6},{8,9},{9,8},{10,11... | collective-permute-start | bytes 36872 | tf_op jit(solution)/shard_map/ppermute | solution.py:645
  24.7 2.3 %collective-permute-done.7.rb_ref = f32[4,768]{1,0:T(4,128)S(1)} collective-permute-done((f32[4,768]{1,0:T(4,128)S(1)}, f32[4,768]{1,0:T(4,128)S(1)}, u32[]{:S(2)}, u32[]{:S(2)}) %collective-permute-start.7) | collective-permute-done | bytes 12320 | tf_op jit(solution)/shard_map/ppermute | solution.py:644
  27.0 2.9 %shard_map.111 = (f32[16,768]{1,0:T(8,128)S(1)}, f32[3,4,384]{2,1,0:T(4,128)S(1)}, f32[3,4,384]{2,1,0:T(4,128)S(1)}, f32[8,384]{1,0:T(8,128)S(1)}, f32[2,8,128]{2,1,0:T(8,128)S(1)}) custom-call(f32[16,768]{1,0:T(8,128)S(1)} %get-tuple-element.49.p_ref, f32[4,768]{1,0:T(4,128)S(1)} %collective-permute-done.6.ra_ref, ...), custom_call_target="tpu_custom_call" | custom-call | tf_op jit(solution)/shard_map/pallas_call | solution.py:656
  30.2 1.2 %collective-permute-start.9 = (f32[3,4,384]{2,1,0:T(4,128)S(1)}, f32[3,4,384]{2,1,0:T(4,128)S(1)}, u32[]{:S(2)}, u32[]{:S(2)}) collective-permute-start(f32[3,4,384]{2,1,0:T(4,128)S(1)} %get-tuple-element.56), channel_id=1, source_target_pairs={{0,24},{8,16},{16,8},{24,0},{1,25},{9,17},{17,9},{25,1},{2,26},{10... | collective-permute-start | bytes 55304 | tf_op jit(solution)/shard_map/ppermute | solution.py:644
  31.3 1.2 %collective-permute-done.8.ra_ref = f32[3,4,384]{2,1,0:T(4,128)S(1)} collective-permute-done((f32[3,4,384]{2,1,0:T(4,128)S(1)}, f32[3,4,384]{2,1,0:T(4,128)S(1)}, u32[]{:S(2)}, u32[]{:S(2)}) %collective-permute-start.8) | collective-permute-done | bytes 18464 | tf_op jit(solution)/shard_map/ppermute | solution.py:645
  32.5 1.2 %collective-permute-done.9.rb_ref = f32[3,4,384]{2,1,0:T(4,128)S(1)} collective-permute-done((f32[3,4,384]{2,1,0:T(4,128)S(1)}, f32[3,4,384]{2,1,0:T(4,128)S(1)}, u32[]{:S(2)}, u32[]{:S(2)}) %collective-permute-start.9) | collective-permute-done | bytes 18464 | tf_op jit(solution)/shard_map/ppermute | solution.py:644
  33.7 3.4 %collective-permute-start.10 = (f32[4,768]{1,0:T(4,128)S(1)}, f32[4,768]{1,0:T(4,128)S(1)}, u32[]{:S(2)}, u32[]{:S(2)}) collective-permute-start(f32[4,768]{1,0:T(4,128)S(1)} %get-tuple-element.58), channel_id=1, source_target_pairs={{0,1},{1,0},{2,3},{3,2},{4,5},{5,4},{6,7},{7,6},{8,9},{9,8},{10,11... | collective-permute-start | bytes 36872 | tf_op jit(solution)/shard_map/ppermute | solution.py:645
  37.1 0.8 %collective-permute-done.10.ra_ref = f32[4,768]{1,0:T(4,128)S(1)} collective-permute-done((f32[4,768]{1,0:T(4,128)S(1)}, f32[4,768]{1,0:T(4,128)S(1)}, u32[]{:S(2)}, u32[]{:S(2)}) %collective-permute-start.10) | collective-permute-done | bytes 12320 | tf_op jit(solution)/shard_map/ppermute | solution.py:645
  37.9 2.3 %collective-permute-done.11.rb_ref = f32[4,768]{1,0:T(4,128)S(1)} collective-permute-done((f32[4,768]{1,0:T(4,128)S(1)}, f32[4,768]{1,0:T(4,128)S(1)}, u32[]{:S(2)}, u32[]{:S(2)}) %collective-permute-start.11) | collective-permute-done | bytes 12320 | tf_op jit(solution)/shard_map/ppermute | solution.py:644
  40.2 3.1 %shard_map.113 = (f32[8,384]{1,0:T(8,128)S(1)}, f32[8,384]{1,0:T(8,128)S(1)}, f32[32,13,1,128]{3,2,1,0:T(1,128)S(1)}) custom-call(f32[16,768]{1,0:T(8,128)S(1)} %get-tuple-element.57.p_ref, f32[4,768]{1,0:T(4,128)S(1)} %collective-permute-done.10.ra_ref, f32[4,768]{1,0:T(4,128)S(1)} %collective-permute-done.11.rb_ref, ...), custom_call_target="tpu_custom_call" | custom-call | tf_op jit(solution)/shard_map/pallas_call | solution.py:656
  43.3 13.3 %all_to_all.5.got_ref = f32[32,13,1,128]{3,2,1,0:T(1,128)S(1)} all-to-all(f32[32,13,1,128]{3,2,1,0:T(1,128)S(1)} %get-tuple-element.63), channel_id=1, replica_groups=mesh['gz'=4,'gy'=8] {'gz','gy'}, dimensions={0} | all-to-all | bytes 425984 | tf_op jit(solution)/shard_map/all_to_all | solution.py:739
  56.6 1.1 %shard_map.114 = (f32[3,4,8,32]{3,2,1,0:T(8,128)}, f32[3,4,8,32]{3,2,1,0:T(8,128)}) custom-call(f32[8,384]{1,0:T(8,128)S(1)} %get-tuple-element.53.v0_ref, f32[8,384]{1,0:T(8,128)S(1)} %get-tuple-element.61.v1_ref, f32[8,384]{1,0:T(8,128)S(1)} %get-tuple-element.62.part_ref, f32[32,13,1,128]{3,2,1,0:T(1,128)S(1)} %all_to_all.5.got_ref), custom_call_target="tpu_custom_call" | custom-call | tf_op jit(solution)/shard_map/pallas_call | solution.py:656
  (30 shorter events, 1.6 us)
Async XLA Ops:
  0.6 4.8 %copy-start.2 = (f32[32,64,256]{2,1,0:T(8,128)S(1)}, f32[32,64,256]{2,1,0:T(8,128)}, u32[]{:S(2)}) copy-start(f32[32,64,256]{2,1,0:T(8,128)} %m_ref.5) | copy-start | bytes 6291460
  0.6 4.8 %copy-start.1 = (f32[32,64,256]{2,1,0:T(8,128)S(1)}, f32[32,64,256]{2,1,0:T(8,128)}, u32[]{:S(2)}) copy-start(f32[32,64,256]{2,1,0:T(8,128)} %f_ref.5) | copy-start | bytes 6291460
  2.1 12.1 %collective-permute-start.2 = (f32[3,64,256]{2,1,0:T(8,128)S(1)}, f32[3,64,256]{2,1,0:T(8,128)S(1)}, u32[]{:S(2)}, u32[]{:S(2)}) collective-permute-start(f32[3,64,256]{2,1,0:T(8,128)S(1)} %get-tuple-element.42), channel_id=1, source_target_pairs={{0,8},{8,0},{16,24},{24,16},{1,9},{9,1},{17,25},{25,17},{2,10},{10... | collective-permute-start | bytes 589832 | tf_op jit(solution)/shard_map/ppermute | solution.py:645
  4.2 4.0 %copy-start.4 = (bf16[512,256]{1,0:T(8,128)(2,1)S(1)}, bf16[512,256]{1,0:T(8,128)(2,1)}, u32[]{:S(2)}) copy-start(bf16[512,256]{1,0:T(8,128)(2,1)} %constant.14.clone.dx_ref) | copy-start | bytes 786436
  4.2 10.0 %collective-permute-start.3 = (f32[3,64,256]{2,1,0:T(8,128)S(1)}, f32[3,64,256]{2,1,0:T(8,128)S(1)}, u32[]{:S(2)}, u32[]{:S(2)}) collective-permute-start(f32[3,64,256]{2,1,0:T(8,128)S(1)} %get-tuple-element.43), channel_id=1, source_target_pairs={{0,24},{8,16},{16,8},{24,0},{1,25},{9,17},{17,9},{25,1},{2,26},{10... | collective-permute-start | bytes 589832 | tf_op jit(solution)/shard_map/ppermute | solution.py:644
  5.6 6.5 %collective-permute-start = (f32[3,32,256]{2,1,0:T(8,128)S(1)}, f32[3,32,256]{2,1,0:T(8,128)S(1)}, u32[]{:S(2)}, u32[]{:S(2)}) collective-permute-start(f32[3,32,256]{2,1,0:T(8,128)S(1)} %get-tuple-element.39), channel_id=1, source_target_pairs={{0,1},{1,0},{2,3},{3,2},{4,5},{5,4},{6,7},{7,6},{8,9},{9,8},{10,11... | collective-permute-start | bytes 294920 | tf_op jit(solution)/shard_map/ppermute | solution.py:645
  6.9 2.9 %copy-start = (bf16[8,256,256]{2,1,0:T(8,128)(2,1)S(1)}, bf16[8,256,256]{2,1,0:T(8,128)(2,1)}, u32[]{:S(2)}) copy-start(bf16[8,256,256]{2,1,0:T(8,128)(2,1)} %constant.20.clone.re_ref) | copy-start | bytes 3145732
  6.9 2.9 %copy-start.7 = (bf16[64,128]{1,0:T(8,128)(2,1)S(1)}, bf16[64,128]{1,0:T(8,128)(2,1)}, u32[]{:S(2)}) copy-start(bf16[64,128]{1,0:T(8,128)(2,1)} %constant.15.clone.dy_ref) | copy-start | bytes 49156
  6.9 5.2 %collective-permute-start.1 = (f32[3,32,256]{2,1,0:T(8,128)S(1)}, f32[3,32,256]{2,1,0:T(8,128)S(1)}, u32[]{:S(2)}, u32[]{:S(2)}) collective-permute-start(f32[3,32,256]{2,1,0:T(8,128)S(1)} %get-tuple-element.40), channel_id=1, source_target_pairs={{0,7},{1,2},{2,1},{3,4},{4,3},{5,6},{6,5},{7,0},{8,15},{9,10},{10,... | collective-permute-start | bytes 294920 | tf_op jit(solution)/shard_map/ppermute | solution.py:644
  9.8 2.3 %copy-start.8 = (bf16[16,32]{1,0:T(8,128)(2,1)S(1)}, bf16[16,32]{1,0:T(8,128)(2,1)}, u32[]{:S(2)}) copy-start(bf16[16,32]{1,0:T(8,128)(2,1)} %constant.16.clone.dy_ref) | copy-start | bytes 3076
  12.1 2.1 %copy-start.5 = (bf16[16,192]{1,0:T(8,128)(2,1)S(1)}, bf16[16,192]{1,0:T(8,128)(2,1)}, u32[]{:S(2)}) copy-start(bf16[16,192]{1,0:T(8,128)(2,1)} %constant.19.clone.ye_ref) | copy-start | bytes 18436
  14.2 12.8 %copy-start.3 = (bf16[8,256,256]{2,1,0:T(8,128)(2,1)S(1)}, bf16[8,256,256]{2,1,0:T(8,128)(2,1)}, u32[]{:S(2)}) copy-start(bf16[8,256,256]{2,1,0:T(8,128)(2,1)} %constant.18.clone.rd_ref) | copy-start | bytes 3145732
  14.2 12.7 %copy-start.6 = (bf16[64,48]{1,0:T(8,128)(2,1)S(1)}, bf16[64,48]{1,0:T(8,128)(2,1)}, u32[]{:S(2)}) copy-start(bf16[64,48]{1,0:T(8,128)(2,1)} %constant.17.clone.yd_ref) | copy-start | bytes 18436
  15.1 2.7 %collective-permute-start.4 = (f32[3,4,384]{2,1,0:T(4,128)S(1)}, f32[3,4,384]{2,1,0:T(4,128)S(1)}, u32[]{:S(2)}, u32[]{:S(2)}) collective-permute-start(f32[3,4,384]{2,1,0:T(4,128)S(1)} %get-tuple-element.47), channel_id=1, source_target_pairs={{0,8},{8,0},{16,24},{24,16},{1,9},{9,1},{17,25},{25,17},{2,10},{10... | collective-permute-start | bytes 55304 | tf_op jit(solution)/shard_map/ppermute | solution.py:645
  16.4 3.5 %collective-permute-start.5 = (f32[3,4,384]{2,1,0:T(4,128)S(1)}, f32[3,4,384]{2,1,0:T(4,128)S(1)}, u32[]{:S(2)}, u32[]{:S(2)}) collective-permute-start(f32[3,4,384]{2,1,0:T(4,128)S(1)} %get-tuple-element.48), channel_id=1, source_target_pairs={{0,24},{8,16},{16,8},{24,0},{1,25},{9,17},{17,9},{25,1},{2,26},{10... | collective-permute-start | bytes 55304 | tf_op jit(solution)/shard_map/ppermute | solution.py:644
  19.9 4.8 %collective-permute-start.6 = (f32[4,768]{1,0:T(4,128)S(1)}, f32[4,768]{1,0:T(4,128)S(1)}, u32[]{:S(2)}, u32[]{:S(2)}) collective-permute-start(f32[4,768]{1,0:T(4,128)S(1)} %get-tuple-element.50), channel_id=1, source_target_pairs={{0,1},{1,0},{2,3},{3,2},{4,5},{5,4},{6,7},{7,6},{8,9},{9,8},{10,11... | collective-permute-start | bytes 36872 | tf_op jit(solution)/shard_map/ppermute | solution.py:645
  23.8 3.1 %collective-permute-start.7 = (f32[4,768]{1,0:T(4,128)S(1)}, f32[4,768]{1,0:T(4,128)S(1)}, u32[]{:S(2)}, u32[]{:S(2)}) collective-permute-start(f32[4,768]{1,0:T(4,128)S(1)} %get-tuple-element.51), channel_id=1, source_target_pairs={{0,7},{1,2},{2,1},{3,4},{4,3},{5,6},{6,5},{7,0},{8,15},{9,10},{10,... | collective-permute-start | bytes 36872 | tf_op jit(solution)/shard_map/ppermute | solution.py:644
  29.8 2.7 %collective-permute-start.8 = (f32[3,4,384]{2,1,0:T(4,128)S(1)}, f32[3,4,384]{2,1,0:T(4,128)S(1)}, u32[]{:S(2)}, u32[]{:S(2)}) collective-permute-start(f32[3,4,384]{2,1,0:T(4,128)S(1)} %get-tuple-element.55), channel_id=1, source_target_pairs={{0,8},{8,0},{16,24},{24,16},{1,9},{9,1},{17,25},{25,17},{2,10},{10... | collective-permute-start | bytes 55304 | tf_op jit(solution)/shard_map/ppermute | solution.py:645
  30.2 3.5 %collective-permute-start.9 = (f32[3,4,384]{2,1,0:T(4,128)S(1)}, f32[3,4,384]{2,1,0:T(4,128)S(1)}, u32[]{:S(2)}, u32[]{:S(2)}) collective-permute-start(f32[3,4,384]{2,1,0:T(4,128)S(1)} %get-tuple-element.56), channel_id=1, source_target_pairs={{0,24},{8,16},{16,8},{24,0},{1,25},{9,17},{17,9},{25,1},{2,26},{10... | collective-permute-start | bytes 55304 | tf_op jit(solution)/shard_map/ppermute | solution.py:644
  33.7 4.2 %collective-permute-start.10 = (f32[4,768]{1,0:T(4,128)S(1)}, f32[4,768]{1,0:T(4,128)S(1)}, u32[]{:S(2)}, u32[]{:S(2)}) collective-permute-start(f32[4,768]{1,0:T(4,128)S(1)} %get-tuple-element.58), channel_id=1, source_target_pairs={{0,1},{1,0},{2,3},{3,2},{4,5},{5,4},{6,7},{7,6},{8,9},{9,8},{10,11... | collective-permute-start | bytes 36872 | tf_op jit(solution)/shard_map/ppermute | solution.py:645
  37.1 3.1 %collective-permute-start.11 = (f32[4,768]{1,0:T(4,128)S(1)}, f32[4,768]{1,0:T(4,128)S(1)}, u32[]{:S(2)}, u32[]{:S(2)}) collective-permute-start(f32[4,768]{1,0:T(4,128)S(1)} %get-tuple-element.59), channel_id=1, source_target_pairs={{0,7},{1,2},{2,1},{3,4},{4,3},{5,6},{6,5},{7,0},{8,15},{9,10},{10,... | collective-permute-start | bytes 36872 | tf_op jit(solution)/shard_map/ppermute | solution.py:644

commit v6 on v5

--- a/solution.py
+++ b/solution.py
@@ -17,7 +17,9 @@
 BF16 = jnp.bfloat16
 VMEM = pl.BlockSpec(memory_space=pltpu.VMEM)
 HBM = pl.BlockSpec(memory_space=pltpu.MemorySpace.HBM)
-PARAMS = pltpu.CompilerParams(vmem_limit_bytes=20 * 1024 * 1024)
+VMEM_LIMIT = 20 * 1024 * 1024
+PARAMS = pltpu.CompilerParams(vmem_limit_bytes=VMEM_LIMIT)
+SPREAD = pltpu.CompilerParams(vmem_limit_bytes=VMEM_LIMIT)
 
 
 def round_up(value, step):
@@ -651,7 +653,7 @@
     return pltpu.VMEM(*(item if isinstance(item[0], tuple) else (item, F32)))
 
 
-def call(kernel, outs, scratch, *args, far=0):
+def call(kernel, name, outs, scratch, *args, far=0):
     shapes = [jax.ShapeDtypeStruct(o, F32) for o in outs]
     return pl.pallas_call(
         kernel,
@@ -659,7 +661,7 @@
         in_specs=[HBM] * far + [VMEM] * (len(args) - far),
         out_specs=[VMEM] * len(outs),
         scratch_shapes=[scratch_of(n) for n in scratch],
-        compiler_params=PARAMS,
+        compiler_params=SPREAD if name in ("apply", "last") else PARAMS,
     )(*[pltpu.with_memory_space_constraint(v, pltpu.HBM) for v in args[:far]], *args[far:])
 
 
@@ -673,16 +675,18 @@
     zhalo, yhalo = (REACH, s.sy, s.nx), (REACH, s.sz, s.nx)
     za, zb = call(
         part(faces_z_kernel, s),
+        "faces_z",
         [zhalo, zhalo],
         [(2, 2, *zhalo), pltpu.SemaphoreType.DMA((2, 2))],
         fixed, moving, far=2,
     )
     za, zb = swap(za, zb, "gz")
-    ya, yb = call(part(faces_y_kernel, s), [yhalo, yhalo], [], fixed, moving)
+    ya, yb = call(part(faces_y_kernel, s), "faces_y", [yhalo, yhalo], [], fixed, moving)
     ya, yb = swap(ya, yb, "gy")
     volume = fixed.shape
     total, diff, gx, gz_inner = call(
         part(start_kernel, s),
+        "start",
         [volume, volume, volume, (s.sz - 2 * REACH, s.sy, s.nx)],
         [],
         fixed, moving, dx,
@@ -697,18 +701,19 @@
     sides = (s.sz, 16, s.nx)
     mid_acc, mid_work = rows_of(s.sy - 32)
     gy, raw, inner = call(
-        part(inner_kernel, s), [volume, sides, mid_acc], mid_work,
+        part(inner_kernel, s), "inner", [volume, sides, mid_acc], mid_work,
         total, diff, gx, gz_inner, dy, re,
     )
     side_acc, side_work = rows_of(32)
     gy_side, side = call(
-        part(side_kernel, s), [sides, side_acc], [sides, *side_work],
+        part(side_kernel, s), "side", [sides, side_acc], [sides, *side_work],
         diff, gx, gz_inner, gy, raw, ya, yb, dy_halo, re,
     )
     grid, zface, yface = (s.bp, s.wide), (round_up(s.nb, 4) // 4, 4, 3 * s.face), (4, s.wide)
     few = ((2 * REACH * 3 * s.sy, s.nx), BF16)
     gz_edge, grid0, za, zb = call(
         part(edge_kernel, s),
+        "edge",
         [(2 * REACH, s.sy, s.nx), grid, zface, zface],
         [(2 * REACH, s.sy, s.nx), few, few, (2 * 3 * s.sy, 2 * s.tap)],
         total, diff, gx, gy, gy_side, za, zb, inner, side, ye, re,
@@ -716,7 +721,9 @@
 
     def fold_z(value, za, zb):
         za, zb = swap(za, zb, "gz")
-        value, ya, yb = call(part(fold_z_kernel, s), [grid, yface, yface], [], value, za, zb)
+        value, ya, yb = call(
+            part(fold_z_kernel, s), "fold_z", [grid, yface, yface], [], value, za, zb
+        )
         return (value, *swap(ya, yb, "gy"))
 
     own = (s.cy, 3 * s.own)
@@ -726,12 +733,14 @@
     grads = (gz_inner, gz_edge, gy, gy_side, gx)
     grid1, za, zb, v0, sums = call(
         part(apply_kernel, s),
+        "apply",
         [grid, zface, zface, own, (2, s.cy, LANES)],
         [grid, *work],
         *fold_z(grid0, za, zb), *grads, yd, rd, ye, re,
     )
     v1, mine, send = call(
         part(last_kernel, s),
+        "last",
         [own, own, (devices, s.block, 1, LANES)],
         [grid, grid, (2, 16 + s.bp, 2 * LANES), (s.bp, 3 * s.own), *work],
         *fold_z(grid1, za, zb), *grads, sums, yd, rd, ye, re,
@@ -740,7 +749,7 @@
     out = (3, s.cz, s.cy, s.cx)
     return tuple(
         call(
-            part(finish_kernel, s), [out, out], [own, (2, s.cy, LANES), (2, s.cy, LANES)], v0, v1, mine, got
+            part(finish_kernel, s), "finish", [out, out], [own, (2, s.cy, LANES), (2, s.cy, LANES)], v0, v1, mine, got
         )
     )
 

time: 57.8 us -> 57.8 us (level)
  no operation moved by 1% of the time
where the time goes in v6:
time: 57.8 us; the launch traced here: 57.6 us
  starting transfers between devices  16.2 us (28%)
  Pallas kernels  15.5 us (27%)
  blocking collectives  13.3 us (23%)
  waiting for transfers between devices  11.8 us (20%)
  between operations  0.81 us (1%)
    pallas_call x11, Pallas kernels, call(): pl.pallas_call(kernel, out_shape=shapes, in_specs=[HBM] * far + [VMEM] *...  15.5 us
    all_to_all x1, blocking collectives, shards(): got = lax.all_to_all(send, ('gz', 'gy'), 0, 0)  13.3 us
    ppermute x6, starting transfers between devices, swap(): return (lax.ppermute(value_a, axis, even), value_b)  12.3 us
    ppermute x6, waiting for transfers between devices, swap(): value_b = lax.ppermute(value_b, axis, odd)  7.85 us
    ppermute x6, waiting for transfers between devices, swap(): return (lax.ppermute(value_a, axis, even), value_b)  3.99 us
    ppermute x6, starting transfers between devices, swap(): value_b = lax.ppermute(value_b, axis, odd)  3.92 us
  transfers between devices with their start and end apart: 12, of which 8 were waited for; matrix products, arithmetic and copies ran while one was open for 0% of the time, Pallas kernels for 11%

profile of v6, /device:TPU:1, one launch (start us, length us, event | category | flops | bytes accessed | tf_op | source)
XLA Modules:
  0.0 57.6 jit_solution(14808493139895910276)
XLA Ops:
  0.6 1.4 %shard_map.108 = (f32[3,64,256]{2,1,0:T(8,128)S(1)}, f32[3,64,256]{2,1,0:T(8,128)S(1)}) custom-call(f32[32,64,256]{2,1,0:T(8,128)} %f_ref.5, f32[32,64,256]{2,1,0:T(8,128)} %m_ref.5), custom_call_target="tpu_custom_call" | custom-call | tf_op jit(solution)/shard_map/pallas_call | solution.py:658
  2.1 2.1 %collective-permute-start.2 = (f32[3,64,256]{2,1,0:T(8,128)S(1)}, f32[3,64,256]{2,1,0:T(8,128)S(1)}, u32[]{:S(2)}, u32[]{:S(2)}) collective-permute-start(f32[3,64,256]{2,1,0:T(8,128)S(1)} %get-tuple-element.42), channel_id=1, source_target_pairs={{0,8},{8,0},{16,24},{24,16},{1,9},{9,1},{17,25},{25,17},{2,10},{10... | collective-permute-start | bytes 589832 | tf_op jit(solution)/shard_map/ppermute | solution.py:647
  4.2 1.2 %collective-permute-start.3 = (f32[3,64,256]{2,1,0:T(8,128)S(1)}, f32[3,64,256]{2,1,0:T(8,128)S(1)}, u32[]{:S(2)}, u32[]{:S(2)}) collective-permute-start(f32[3,64,256]{2,1,0:T(8,128)S(1)} %get-tuple-element.43), channel_id=1, source_target_pairs={{0,24},{8,16},{16,8},{24,0},{1,25},{9,17},{17,9},{25,1},{2,26},{10... | collective-permute-start | bytes 589832 | tf_op jit(solution)/shard_map/ppermute | solution.py:646
  5.6 1.3 %collective-permute-start = (f32[3,32,256]{2,1,0:T(8,128)S(1)}, f32[3,32,256]{2,1,0:T(8,128)S(1)}, u32[]{:S(2)}, u32[]{:S(2)}) collective-permute-start(f32[3,32,256]{2,1,0:T(8,128)S(1)} %get-tuple-element.39), channel_id=1, source_target_pairs={{0,1},{1,0},{2,3},{3,2},{4,5},{5,4},{6,7},{7,6},{8,9},{9,8},{10,11... | collective-permute-start | bytes 294920 | tf_op jit(solution)/shard_map/ppermute | solution.py:647
  6.9 1.3 %collective-permute-start.1 = (f32[3,32,256]{2,1,0:T(8,128)S(1)}, f32[3,32,256]{2,1,0:T(8,128)S(1)}, u32[]{:S(2)}, u32[]{:S(2)}) collective-permute-start(f32[3,32,256]{2,1,0:T(8,128)S(1)} %get-tuple-element.40), channel_id=1, source_target_pairs={{0,7},{1,2},{2,1},{3,4},{4,3},{5,6},{6,5},{7,0},{8,15},{9,10},{10,... | collective-permute-start | bytes 294920 | tf_op jit(solution)/shard_map/ppermute | solution.py:646
  8.1 1.6 %shard_map.104 = (f32[32,64,256]{2,1,0:T(8,128)S(1)}, f32[32,64,256]{2,1,0:T(8,128)S(1)}, f32[32,64,256]{2,1,0:T(8,128)S(1)}, f32[26,64,256]{2,1,0:T(8,128)S(1)}) custom-call(f32[32,64,256]{2,1,0:T(8,128)S(1)} %copy-done.1, f32[32,64,256]{2,1,0:T(8,128)S(1)} %copy-done.2, bf16[512,256]{1,0:T(8,128)(2,1)S(1)} %copy-done.4), custom_call_target="tpu_custom_call" | custom-call | tf_op jit(solution)/shard_map/pallas_call | solution.py:658
  9.8 2.3 %shard_map.105 = (f32[32,64,256]{2,1,0:T(8,128)S(1)}, f32[32,16,256]{2,1,0:T(8,128)S(1)}, f32[384,256]{1,0:T(8,128)S(1)}) custom-call(f32[32,64,256]{2,1,0:T(8,128)S(1)} %get-tuple-element.33.sum_ref, f32[32,64,256]{2,1,0:T(8,128)S(1)} %get-tuple-element.34.diff_ref, f32[32,64,256]{2,1,0:T(8,128)S(1)} %get-tuple-element.35.gx_ref, ...), custom_call_target="tpu_custom_call" | custom-call | tf_op jit(solution)/shard_map/pallas_call | solution.py:658
  12.1 2.0 %shard_map.107 = (f32[32,16,256]{2,1,0:T(8,128)S(1)}, f32[384,256]{1,0:T(8,128)S(1)}) custom-call(f32[32,64,256]{2,1,0:T(8,128)S(1)} %get-tuple-element.34.diff_ref, f32[32,64,256]{2,1,0:T(8,128)S(1)} %get-tuple-element.35.gx_ref, f32[26,64,256]{2,1,0:T(8,128)S(1)} %get-tuple-element.36.gz_ref.gi_ref, f32[32,64,256]{2,1,0:T(8,128)S(1)} %get-tuple-element.37.gy_ref, ...), custom_call_target="tpu_custom_call" | custom-call | tf_op jit(solution)/shard_map/pallas_call | solution.py:658
  14.2 0.8 %shard_map.109 = (f32[6,64,256]{2,1,0:T(8,128)S(1)}, f32[16,768]{1,0:T(8,128)S(1)}, f32[3,4,384]{2,1,0:T(4,128)S(1)}, f32[3,4,384]{2,1,0:T(4,128)S(1)}) custom-call(f32[32,64,256]{2,1,0:T(8,128)S(1)} %get-tuple-element.33.sum_ref, f32[32,64,256]{2,1,0:T(8,128)S(1)} %get-tuple-element.34.diff_ref, f32[32,64,256]{2,1,0:T(8,128)S(1)} %get-tuple-element.35.gx_ref, ...), custom_call_target="tpu_custom_call" | custom-call | tf_op jit(solution)/shard_map/pallas_call | solution.py:658
  15.1 1.3 %collective-permute-start.4 = (f32[3,4,384]{2,1,0:T(4,128)S(1)}, f32[3,4,384]{2,1,0:T(4,128)S(1)}, u32[]{:S(2)}, u32[]{:S(2)}) collective-permute-start(f32[3,4,384]{2,1,0:T(4,128)S(1)} %get-tuple-element.47), channel_id=1, source_target_pairs={{0,8},{8,0},{16,24},{24,16},{1,9},{9,1},{17,25},{25,17},{2,10},{10... | collective-permute-start | bytes 55304 | tf_op jit(solution)/shard_map/ppermute | solution.py:647
  16.6 1.2 %collective-permute-done.4.ra_ref = f32[3,4,384]{2,1,0:T(4,128)S(1)} collective-permute-done((f32[3,4,384]{2,1,0:T(4,128)S(1)}, f32[3,4,384]{2,1,0:T(4,128)S(1)}, u32[]{:S(2)}, u32[]{:S(2)}) %collective-permute-start.4) | collective-permute-done | bytes 18464 | tf_op jit(solution)/shard_map/ppermute | solution.py:647
  17.8 2.1 %collective-permute-done.5.rb_ref = f32[3,4,384]{2,1,0:T(4,128)S(1)} collective-permute-done((f32[3,4,384]{2,1,0:T(4,128)S(1)}, f32[3,4,384]{2,1,0:T(4,128)S(1)}, u32[]{:S(2)}, u32[]{:S(2)}) %collective-permute-start.5) | collective-permute-done | bytes 18464 | tf_op jit(solution)/shard_map/ppermute | solution.py:646
  19.9 3.9 %collective-permute-start.6 = (f32[4,768]{1,0:T(4,128)S(1)}, f32[4,768]{1,0:T(4,128)S(1)}, u32[]{:S(2)}, u32[]{:S(2)}) collective-permute-start(f32[4,768]{1,0:T(4,128)S(1)} %get-tuple-element.50), channel_id=1, source_target_pairs={{0,1},{1,0},{2,3},{3,2},{4,5},{5,4},{6,7},{7,6},{8,9},{9,8},{10,11... | collective-permute-start | bytes 36872 | tf_op jit(solution)/shard_map/ppermute | solution.py:647
  24.7 2.3 %collective-permute-done.7.rb_ref = f32[4,768]{1,0:T(4,128)S(1)} collective-permute-done((f32[4,768]{1,0:T(4,128)S(1)}, f32[4,768]{1,0:T(4,128)S(1)}, u32[]{:S(2)}, u32[]{:S(2)}) %collective-permute-start.7) | collective-permute-done | bytes 12320 | tf_op jit(solution)/shard_map/ppermute | solution.py:646
  27.0 2.9 %shard_map.111 = (f32[16,768]{1,0:T(8,128)S(1)}, f32[3,4,384]{2,1,0:T(4,128)S(1)}, f32[3,4,384]{2,1,0:T(4,128)S(1)}, f32[8,384]{1,0:T(8,128)S(1)}, f32[2,8,128]{2,1,0:T(8,128)S(1)}) custom-call(f32[16,768]{1,0:T(8,128)S(1)} %get-tuple-element.49.p_ref, f32[4,768]{1,0:T(4,128)S(1)} %collective-permute-done.6.ra_ref, ...), custom_call_target="tpu_custom_call" | custom-call | tf_op jit(solution)/shard_map/pallas_call | solution.py:658
  30.2 1.2 %collective-permute-start.9 = (f32[3,4,384]{2,1,0:T(4,128)S(1)}, f32[3,4,384]{2,1,0:T(4,128)S(1)}, u32[]{:S(2)}, u32[]{:S(2)}) collective-permute-start(f32[3,4,384]{2,1,0:T(4,128)S(1)} %get-tuple-element.56), channel_id=1, source_target_pairs={{0,24},{8,16},{16,8},{24,0},{1,25},{9,17},{17,9},{25,1},{2,26},{10... | collective-permute-start | bytes 55304 | tf_op jit(solution)/shard_map/ppermute | solution.py:646
  31.3 1.2 %collective-permute-done.8.ra_ref = f32[3,4,384]{2,1,0:T(4,128)S(1)} collective-permute-done((f32[3,4,384]{2,1,0:T(4,128)S(1)}, f32[3,4,384]{2,1,0:T(4,128)S(1)}, u32[]{:S(2)}, u32[]{:S(2)}) %collective-permute-start.8) | collective-permute-done | bytes 18464 | tf_op jit(solution)/shard_map/ppermute | solution.py:647
  32.5 1.2 %collective-permute-done.9.rb_ref = f32[3,4,384]{2,1,0:T(4,128)S(1)} collective-permute-done((f32[3,4,384]{2,1,0:T(4,128)S(1)}, f32[3,4,384]{2,1,0:T(4,128)S(1)}, u32[]{:S(2)}, u32[]{:S(2)}) %collective-permute-start.9) | collective-permute-done | bytes 18464 | tf_op jit(solution)/shard_map/ppermute | solution.py:646
  33.7 3.4 %collective-permute-start.10 = (f32[4,768]{1,0:T(4,128)S(1)}, f32[4,768]{1,0:T(4,128)S(1)}, u32[]{:S(2)}, u32[]{:S(2)}) collective-permute-start(f32[4,768]{1,0:T(4,128)S(1)} %get-tuple-element.58), channel_id=1, source_target_pairs={{0,1},{1,0},{2,3},{3,2},{4,5},{5,4},{6,7},{7,6},{8,9},{9,8},{10,11... | collective-permute-start | bytes 36872 | tf_op jit(solution)/shard_map/ppermute | solution.py:647
  37.1 0.8 %collective-permute-done.10.ra_ref = f32[4,768]{1,0:T(4,128)S(1)} collective-permute-done((f32[4,768]{1,0:T(4,128)S(1)}, f32[4,768]{1,0:T(4,128)S(1)}, u32[]{:S(2)}, u32[]{:S(2)}) %collective-permute-start.10) | collective-permute-done | bytes 12320 | tf_op jit(solution)/shard_map/ppermute | solution.py:647
  37.9 2.3 %collective-permute-done.11.rb_ref = f32[4,768]{1,0:T(4,128)S(1)} collective-permute-done((f32[4,768]{1,0:T(4,128)S(1)}, f32[4,768]{1,0:T(4,128)S(1)}, u32[]{:S(2)}, u32[]{:S(2)}) %collective-permute-start.11) | collective-permute-done | bytes 12320 | tf_op jit(solution)/shard_map/ppermute | solution.py:646
  40.2 3.1 %shard_map.113 = (f32[8,384]{1,0:T(8,128)S(1)}, f32[8,384]{1,0:T(8,128)S(1)}, f32[32,13,1,128]{3,2,1,0:T(1,128)S(1)}) custom-call(f32[16,768]{1,0:T(8,128)S(1)} %get-tuple-element.57.p_ref, f32[4,768]{1,0:T(4,128)S(1)} %collective-permute-done.10.ra_ref, f32[4,768]{1,0:T(4,128)S(1)} %collective-permute-done.11.rb_ref, ...), custom_call_target="tpu_custom_call" | custom-call | tf_op jit(solution)/shard_map/pallas_call | solution.py:658
  43.3 13.3 %all_to_all.5.got_ref = f32[32,13,1,128]{3,2,1,0:T(1,128)S(1)} all-to-all(f32[32,13,1,128]{3,2,1,0:T(1,128)S(1)} %get-tuple-element.63), channel_id=1, replica_groups=mesh['gz'=4,'gy'=8] {'gz','gy'}, dimensions={0} | all-to-all | bytes 425984 | tf_op jit(solution)/shard_map/all_to_all | solution.py:748
  56.6 1.1 %shard_map.114 = (f32[3,4,8,32]{3,2,1,0:T(8,128)}, f32[3,4,8,32]{3,2,1,0:T(8,128)}) custom-call(f32[8,384]{1,0:T(8,128)S(1)} %get-tuple-element.53.v0_ref, f32[8,384]{1,0:T(8,128)S(1)} %get-tuple-element.61.v1_ref, f32[8,384]{1,0:T(8,128)S(1)} %get-tuple-element.62.part_ref, f32[32,13,1,128]{3,2,1,0:T(1,128)S(1)} %all_to_all.5.got_ref), custom_call_target="tpu_custom_call" | custom-call | tf_op jit(solution)/shard_map/pallas_call | solution.py:658
  (30 shorter events, 1.6 us)
Async XLA Ops:
  0.6 4.8 %copy-start.2 = (f32[32,64,256]{2,1,0:T(8,128)S(1)}, f32[32,64,256]{2,1,0:T(8,128)}, u32[]{:S(2)}) copy-start(f32[32,64,256]{2,1,0:T(8,128)} %m_ref.5) | copy-start | bytes 6291460
  0.6 4.8 %copy-start.1 = (f32[32,64,256]{2,1,0:T(8,128)S(1)}, f32[32,64,256]{2,1,0:T(8,128)}, u32[]{:S(2)}) copy-start(f32[32,64,256]{2,1,0:T(8,128)} %f_ref.5) | copy-start | bytes 6291460
  2.1 12.1 %collective-permute-start.2 = (f32[3,64,256]{2,1,0:T(8,128)S(1)}, f32[3,64,256]{2,1,0:T(8,128)S(1)}, u32[]{:S(2)}, u32[]{:S(2)}) collective-permute-start(f32[3,64,256]{2,1,0:T(8,128)S(1)} %get-tuple-element.42), channel_id=1, source_target_pairs={{0,8},{8,0},{16,24},{24,16},{1,9},{9,1},{17,25},{25,17},{2,10},{10... | collective-permute-start | bytes 589832 | tf_op jit(solution)/shard_map/ppermute | solution.py:647
  4.2 4.0 %copy-start.4 = (bf16[512,256]{1,0:T(8,128)(2,1)S(1)}, bf16[512,256]{1,0:T(8,128)(2,1)}, u32[]{:S(2)}) copy-start(bf16[512,256]{1,0:T(8,128)(2,1)} %constant.14.clone.dx_ref) | copy-start | bytes 786436
  4.2 10.0 %collective-permute-start.3 = (f32[3,64,256]{2,1,0:T(8,128)S(1)}, f32[3,64,256]{2,1,0:T(8,128)S(1)}, u32[]{:S(2)}, u32[]{:S(2)}) collective-permute-start(f32[3,64,256]{2,1,0:T(8,128)S(1)} %get-tuple-element.43), channel_id=1, source_target_pairs={{0,24},{8,16},{16,8},{24,0},{1,25},{9,17},{17,9},{25,1},{2,26},{10... | collective-permute-start | bytes 589832 | tf_op jit(solution)/shard_map/ppermute | solution.py:646
  5.6 6.5 %collective-permute-start = (f32[3,32,256]{2,1,0:T(8,128)S(1)}, f32[3,32,256]{2,1,0:T(8,128)S(1)}, u32[]{:S(2)}, u32[]{:S(2)}) collective-permute-start(f32[3,32,256]{2,1,0:T(8,128)S(1)} %get-tuple-element.39), channel_id=1, source_target_pairs={{0,1},{1,0},{2,3},{3,2},{4,5},{5,4},{6,7},{7,6},{8,9},{9,8},{10,11... | collective-permute-start | bytes 294920 | tf_op jit(solution)/shard_map/ppermute | solution.py:647
  6.9 2.9 %copy-start = (bf16[8,256,256]{2,1,0:T(8,128)(2,1)S(1)}, bf16[8,256,256]{2,1,0:T(8,128)(2,1)}, u32[]{:S(2)}) copy-start(bf16[8,256,256]{2,1,0:T(8,128)(2,1)} %constant.20.clone.re_ref) | copy-start | bytes 3145732
  6.9 2.9 %copy-start.7 = (bf16[64,128]{1,0:T(8,128)(2,1)S(1)}, bf16[64,128]{1,0:T(8,128)(2,1)}, u32[]{:S(2)}) copy-start(bf16[64,128]{1,0:T(8,128)(2,1)} %constant.15.clone.dy_ref) | copy-start | bytes 49156
  6.9 5.2 %collective-permute-start.1 = (f32[3,32,256]{2,1,0:T(8,128)S(1)}, f32[3,32,256]{2,1,0:T(8,128)S(1)}, u32[]{:S(2)}, u32[]{:S(2)}) collective-permute-start(f32[3,32,256]{2,1,0:T(8,128)S(1)} %get-tuple-element.40), channel_id=1, source_target_pairs={{0,7},{1,2},{2,1},{3,4},{4,3},{5,6},{6,5},{7,0},{8,15},{9,10},{10,... | collective-permute-start | bytes 294920 | tf_op jit(solution)/shard_map/ppermute | solution.py:646
  9.8 2.3 %copy-start.8 = (bf16[16,32]{1,0:T(8,128)(2,1)S(1)}, bf16[16,32]{1,0:T(8,128)(2,1)}, u32[]{:S(2)}) copy-start(bf16[16,32]{1,0:T(8,128)(2,1)} %constant.16.clone.dy_ref) | copy-start | bytes 3076
  12.1 2.1 %copy-start.5 = (bf16[16,192]{1,0:T(8,128)(2,1)S(1)}, bf16[16,192]{1,0:T(8,128)(2,1)}, u32[]{:S(2)}) copy-start(bf16[16,192]{1,0:T(8,128)(2,1)} %constant.19.clone.ye_ref) | copy-start | bytes 18436
  14.2 12.8 %copy-start.3 = (bf16[8,256,256]{2,1,0:T(8,128)(2,1)S(1)}, bf16[8,256,256]{2,1,0:T(8,128)(2,1)}, u32[]{:S(2)}) copy-start(bf16[8,256,256]{2,1,0:T(8,128)(2,1)} %constant.18.clone.rd_ref) | copy-start | bytes 3145732
  14.2 12.7 %copy-start.6 = (bf16[64,48]{1,0:T(8,128)(2,1)S(1)}, bf16[64,48]{1,0:T(8,128)(2,1)}, u32[]{:S(2)}) copy-start(bf16[64,48]{1,0:T(8,128)(2,1)} %constant.17.clone.yd_ref) | copy-start | bytes 18436
  15.1 2.7 %collective-permute-start.4 = (f32[3,4,384]{2,1,0:T(4,128)S(1)}, f32[3,4,384]{2,1,0:T(4,128)S(1)}, u32[]{:S(2)}, u32[]{:S(2)}) collective-permute-start(f32[3,4,384]{2,1,0:T(4,128)S(1)} %get-tuple-element.47), channel_id=1, source_target_pairs={{0,8},{8,0},{16,24},{24,16},{1,9},{9,1},{17,25},{25,17},{2,10},{10... | collective-permute-start | bytes 55304 | tf_op jit(solution)/shard_map/ppermute | solution.py:647
  16.4 3.5 %collective-permute-start.5 = (f32[3,4,384]{2,1,0:T(4,128)S(1)}, f32[3,4,384]{2,1,0:T(4,128)S(1)}, u32[]{:S(2)}, u32[]{:S(2)}) collective-permute-start(f32[3,4,384]{2,1,0:T(4,128)S(1)} %get-tuple-element.48), channel_id=1, source_target_pairs={{0,24},{8,16},{16,8},{24,0},{1,25},{9,17},{17,9},{25,1},{2,26},{10... | collective-permute-start | bytes 55304 | tf_op jit(solution)/shard_map/ppermute | solution.py:646
  19.9 4.8 %collective-permute-start.6 = (f32[4,768]{1,0:T(4,128)S(1)}, f32[4,768]{1,0:T(4,128)S(1)}, u32[]{:S(2)}, u32[]{:S(2)}) collective-permute-start(f32[4,768]{1,0:T(4,128)S(1)} %get-tuple-element.50), channel_id=1, source_target_pairs={{0,1},{1,0},{2,3},{3,2},{4,5},{5,4},{6,7},{7,6},{8,9},{9,8},{10,11... | collective-permute-start | bytes 36872 | tf_op jit(solution)/shard_map/ppermute | solution.py:647
  23.8 3.1 %collective-permute-start.7 = (f32[4,768]{1,0:T(4,128)S(1)}, f32[4,768]{1,0:T(4,128)S(1)}, u32[]{:S(2)}, u32[]{:S(2)}) collective-permute-start(f32[4,768]{1,0:T(4,128)S(1)} %get-tuple-element.51), channel_id=1, source_target_pairs={{0,7},{1,2},{2,1},{3,4},{4,3},{5,6},{6,5},{7,0},{8,15},{9,10},{10,... | collective-permute-start | bytes 36872 | tf_op jit(solution)/shard_map/ppermute | solution.py:646
  29.8 2.7 %collective-permute-start.8 = (f32[3,4,384]{2,1,0:T(4,128)S(1)}, f32[3,4,384]{2,1,0:T(4,128)S(1)}, u32[]{:S(2)}, u32[]{:S(2)}) collective-permute-start(f32[3,4,384]{2,1,0:T(4,128)S(1)} %get-tuple-element.55), channel_id=1, source_target_pairs={{0,8},{8,0},{16,24},{24,16},{1,9},{9,1},{17,25},{25,17},{2,10},{10... | collective-permute-start | bytes 55304 | tf_op jit(solution)/shard_map/ppermute | solution.py:647
  30.2 3.5 %collective-permute-start.9 = (f32[3,4,384]{2,1,0:T(4,128)S(1)}, f32[3,4,384]{2,1,0:T(4,128)S(1)}, u32[]{:S(2)}, u32[]{:S(2)}) collective-permute-start(f32[3,4,384]{2,1,0:T(4,128)S(1)} %get-tuple-element.56), channel_id=1, source_target_pairs={{0,24},{8,16},{16,8},{24,0},{1,25},{9,17},{17,9},{25,1},{2,26},{10... | collective-permute-start | bytes 55304 | tf_op jit(solution)/shard_map/ppermute | solution.py:646
  33.7 4.2 %collective-permute-start.10 = (f32[4,768]{1,0:T(4,128)S(1)}, f32[4,768]{1,0:T(4,128)S(1)}, u32[]{:S(2)}, u32[]{:S(2)}) collective-permute-start(f32[4,768]{1,0:T(4,128)S(1)} %get-tuple-element.58), channel_id=1, source_target_pairs={{0,1},{1,0},{2,3},{3,2},{4,5},{5,4},{6,7},{7,6},{8,9},{9,8},{10,11... | collective-permute-start | bytes 36872 | tf_op jit(solution)/shard_map/ppermute | solution.py:647
  37.1 3.1 %collective-permute-start.11 = (f32[4,768]{1,0:T(4,128)S(1)}, f32[4,768]{1,0:T(4,128)S(1)}, u32[]{:S(2)}, u32[]{:S(2)}) collective-permute-start(f32[4,768]{1,0:T(4,128)S(1)} %get-tuple-element.59), channel_id=1, source_target_pairs={{0,7},{1,2},{2,1},{3,4},{4,3},{5,6},{6,5},{7,0},{8,15},{9,10},{10,... | collective-permute-start | bytes 36872 | tf_op jit(solution)/shard_map/ppermute | solution.py:646
